TPU v7x, 256 devices: a whole 4x4x8 slice. The times are simulated.
256 devices in a mesh: ctx: 128 (over x, y, z_lo, core), tp: 2 (over z_hi).
Axes of the slice: x: 4, y: 4, z: 8 (z_hi: 2, z_lo: 4; z = z_hi * 4 + z_lo), core: 2. Of those that a mesh axis runs over, the one named last changes fastest.
Arguments:
- queries: bfloat16 [65536, 2048], P('ctx', 'tp'), may hold values from -7 to 7
- key_rows: bfloat16 [65536, 2048], P('ctx', 'tp'), may hold values from -7 to 7
- value_rows: bfloat16 [65536, 2048], P('ctx', 'tp'), may hold values from -6 to 6
Outputs:
- attended: bfloat16 [65536, 2048], P(('ctx', 'tp'))
All inputs are finite; a program needn't handle non-finite values.
Results may differ from a plain program's by a relative error of at most 0.0029.
Values may be sent and summed in bfloat16 or wider, within the bound.
No kernel may reach another device: no remote copies, remote signals or barrier semaphores. Data moves between devices by JAX's collectives and lax.ppermute only.
A program may use at most 64 MiB of HBM per device.

v0:
```python
from functools import reduce
import math

import jax
import jax.numpy as jnp
from jax import lax
from jax.sharding import PartitionSpec as P

HEAD_DIM = 128
DILATION_SECOND = 4
DILATION_THIRD = 16
DILATION_FOURTH = 64


masked_score = -1e30


def swapped(value, axis, distance):
    mask = 2**distance
    pairs = [(source, source ^ mask) for source in range(lax.axis_size(axis))]
    return lax.ppermute(value, axis, pairs)


def split_heads(matrix, heads_here):
    return matrix.reshape(matrix.shape[0], heads_here, HEAD_DIM).transpose(1, 0, 2)


def gather_rows(tensor, stride, offsets):
    leading = tensor.shape[:-3]
    heads_here, row_total, head_dim = tensor.shape[-3:]
    shaped = tensor.reshape(leading + (heads_here, row_total // stride, stride, head_dim))
    picked_axis = len(leading) + 1
    chosen = [
        lax.dynamic_index_in_dim(
            shaped[..., head_pos, :, :, :], offsets[head_pos], axis=picked_axis, keepdims=False
        )
        for head_pos in range(heads_here)
    ]
    return jnp.stack(chosen, axis=len(leading))


def join_rows(own_rows, partner, is_upper):
    return jnp.where(
        is_upper,
        jnp.concatenate([partner, own_rows], axis=2),
        jnp.concatenate([own_rows, partner], axis=2),
    )


def attend(query_part, key_part, value_part, first_row):
    scores = jnp.einsum(
        "hqd,hkd->hqk", query_part, key_part, preferred_element_type=jnp.float32
    ) * (1.0 / math.sqrt(HEAD_DIM))
    query_pos = first_row + jnp.arange(query_part.shape[1], dtype=jnp.int32)
    allowed = jnp.arange(key_part.shape[1], dtype=jnp.int32)[None, :] <= query_pos[:, None]
    scores = jnp.where(allowed[None, :, :], scores, masked_score)
    row_max = jnp.max(scores, axis=2)
    exponent = jnp.exp(scores - row_max[:, :, None])
    row_sum = jnp.sum(exponent, axis=2)
    weighted = jnp.einsum(
        "hqk,hkd->hqd",
        exponent.astype(jnp.bfloat16),
        value_part,
        preferred_element_type=jnp.float32,
    )
    return (row_max, row_sum, weighted)


def spread(outcome, stride, offsets):
    row_max, row_sum, weighted = outcome
    heads_here, selected = row_max.shape
    chosen = jnp.arange(stride, dtype=jnp.int32)[None, :] == offsets[:, None]
    max_full = jnp.where(chosen[:, None, :], row_max[:, :, None], masked_score).reshape(
        heads_here, selected * stride
    )
    sum_full = jnp.where(chosen[:, None, :], row_sum[:, :, None], 0.0).reshape(
        heads_here, selected * stride
    )
    weighted_full = jnp.where(chosen[:, None, :, None], weighted[:, :, None, :], 0.0).reshape(
        heads_here, selected * stride, weighted.shape[2]
    )
    return (max_full, sum_full, weighted_full)


def local(queries, key_rows, value_rows):
    nearby_local_rows, feature_width = queries.shape
    heads_here = feature_width // HEAD_DIM
    context_index = lax.axis_index("ctx")
    tp_index = lax.axis_index("tp")
    head_numbers = tp_index * heads_here + jnp.arange(heads_here, dtype=jnp.int32)
    query_heads = split_heads(queries, heads_here)
    key_value_couple = jnp.stack(
        [split_heads(key_rows, heads_here), split_heads(value_rows, heads_here)]
    )
    block_rows = min(512, nearby_local_rows)
    block_outs = [
        attend(
            query_heads, key_value_couple[0, :, :block_rows], key_value_couple[1, :, :block_rows], 0
        )
    ]
    level_zero = tuple(
        (
            jnp.concatenate([block_out[member] for block_out in block_outs], axis=1)
            for member in range(3)
        )
    )
    shift_level_one = head_numbers % DILATION_SECOND
    shift_level_two = head_numbers % DILATION_THIRD
    shift_level_three = head_numbers % DILATION_FOURTH
    closest_rows = gather_rows(key_value_couple, DILATION_SECOND, shift_level_one)
    for index_bit_value in range(DILATION_SECOND.bit_length() - 1):
        partner = swapped(closest_rows, "ctx", index_bit_value)
        closest_rows = join_rows(
            closest_rows, partner, context_index // (1 << index_bit_value) % 2 == 1
        )
    middle_rows = gather_rows(key_value_couple, DILATION_THIRD, shift_level_two)
    for index_bit_value in range(DILATION_THIRD.bit_length() - 1):
        partner = swapped(middle_rows, "ctx", index_bit_value)
        middle_rows = join_rows(
            middle_rows, partner, context_index // (1 << index_bit_value) % 2 == 1
        )
    distant_rows = lax.all_gather(
        gather_rows(key_value_couple, DILATION_FOURTH, shift_level_three), "ctx", axis=2, tiled=True
    )
    level_one = spread(
        attend(
            gather_rows(query_heads, DILATION_SECOND, shift_level_one),
            closest_rows[0],
            closest_rows[1],
            context_index % DILATION_SECOND * (nearby_local_rows // DILATION_SECOND),
        ),
        DILATION_SECOND,
        shift_level_one,
    )
    level_two = spread(
        attend(
            gather_rows(query_heads, DILATION_THIRD, shift_level_two),
            middle_rows[0],
            middle_rows[1],
            context_index % DILATION_THIRD * (nearby_local_rows // DILATION_THIRD),
        ),
        DILATION_THIRD,
        shift_level_two,
    )
    level_three = spread(
        attend(
            gather_rows(query_heads, DILATION_FOURTH, shift_level_three),
            distant_rows[0],
            distant_rows[1],
            context_index * (nearby_local_rows // DILATION_FOURTH),
        ),
        DILATION_FOURTH,
        shift_level_three,
    )
    outcomes = [level_zero, level_one, level_two, level_three]
    peak_max = reduce(jnp.maximum, [outcome[0] for outcome in outcomes])
    numerator = jnp.zeros(level_zero[2].shape, jnp.float32)
    denominator = jnp.zeros(level_zero[1].shape, jnp.float32)
    for outcome in outcomes:
        factor = jnp.exp(outcome[0] - peak_max)
        numerator = numerator + factor[:, :, None] * outcome[2]
        denominator = denominator + factor * outcome[1]
    combined = (numerator / denominator[:, :, None]).astype(jnp.bfloat16)
    combined = combined.transpose(1, 0, 2).reshape(nearby_local_rows, feature_width)
    return lax.all_to_all(combined, "tp", split_axis=0, concat_axis=1, tiled=True)


def solution(mesh):
    return jax.shard_map(
        local,
        mesh=mesh,
        in_specs=(P("ctx", "tp"), P("ctx", "tp"), P("ctx", "tp")),
        out_specs=P(("ctx", "tp"), None),
        check_vma=False,
    )
```

profile of v0, /device:TPU:6, one launch (start us, length us, event | category | flops | bytes accessed | tf_op | source)
XLA Modules:
  0.0 306.4 jit_solution(7927321641937379747)
XLA Ops:
  6.6 0.7 fusion.60
  17.2 1.5 copy_bitcast_fusion.1
  18.9 0.7 copy_dynamic-update-slice_fusion.1
  19.6 0.9 copy_dynamic-update-slice_fusion
  20.5 1.2 fusion.56
  26.7 0.7 constant_dynamic-update-slice_fusion.47
  27.4 0.7 constant_dynamic-update-slice_fusion.46
  28.1 0.7 constant_dynamic-update-slice_fusion.45
  28.8 0.7 constant_dynamic-update-slice_fusion.44
  29.4 0.7 constant_dynamic-update-slice_fusion.43
  30.1 0.7 constant_dynamic-update-slice_fusion.42
  30.8 0.7 constant_dynamic-update-slice_fusion.41
  31.5 0.6 copy-done.13
  32.2 0.7 fusion.61
  43.5 1.3 fusion.57
  49.8 1.5 constant_dynamic-update-slice_fusion.15
  51.3 1.5 constant_dynamic-update-slice_fusion.14
  52.8 1.5 constant_dynamic-update-slice_fusion.13
  54.3 1.5 constant_dynamic-update-slice_fusion.12
  55.8 1.5 constant_dynamic-update-slice_fusion.11
  57.3 1.5 constant_dynamic-update-slice_fusion.10
  58.7 1.5 constant_dynamic-update-slice_fusion.9
  60.2 0.6 constant_dynamic-update-slice_fusion.8
  60.9 0.7 fusion.59
  77.2 0.6 constant_dynamic-update-slice_fusion.31
  80.8 0.6 constant_dynamic-update-slice_fusion.25
  81.4 0.6 constant_dynamic-update-slice_fusion.24
  82.7 0.7 iota_compare_fusion.3
  85.1 0.6 copy-done.8
  85.7 0.7 iota_compare_fusion.2
  86.6 1.7 fusion
  88.3 3.9 %fusion.3 = f32[8,512,128]{2,1,0:T(8,128)} fusion(f32[8,512,512]{1,2,0:T(8,128)S(1)} %get-tuple-element.69, f32[8,512]{1,0:T(8,128)S(1)} %get-tuple-element.68, pred[512,512]{0,1:T(8,128)(4,1)S(1)} %iota_compare_fusion, bf16[512,1024]{1,0:T(8,128)(2,1)S(1)} %copy-done.6), kind=kOutput, calls=%fused_computation.5 | convolution fusion | flops 545259520 | bytes 11812864 | tf_op jit(solution)/shard_map/hqk,hkd->hqd/dot_general | solution.py:60
  92.3 0.7 broadcast_in_dim.274
  93.0 0.7 broadcast_in_dim.268
  93.8 0.7 copy.152
  94.5 1.1 maximum_select_fusion.5
  95.6 2.0 collective-permute-start.3
  97.6 1.8 maximum_select_fusion.2
  99.6 5.2 %collective-permute-done.3 = bf16[2,8,64,128]{3,2,1,0:T(8,128)(2,1)S(1)} collective-permute-done((bf16[2,8,64,128]{3,2,1,0:T(8,128)(2,1)S(1)}, bf16[2,8,64,128]{3,2,1,0:T(8,128)(2,1)S(1)}, u32[]{:S(2)}, u32[]{:S(2)}) %collective-permute-start.3) | collective-permute-done | bytes 262176 | tf_op jit(solution)/shard_map/ppermute | solution.py:21
  105.0 3.3 %collective-permute-start.4 = (bf16[2,8,128,128]{3,2,1,0:T(8,128)(2,1)S(1)}, bf16[2,8,128,128]{3,2,1,0:T(8,128)(2,1)S(1)}, u32[]{:S(2)}, u32[]{:S(2)}) collective-permute-start(bf16[2,8,128,128]{3,2,1,0:T(8,128)(2,1)S(1)} %maximum_select_fusion.4), channel_id=1, source_target_pairs={{0,8},{2,10},{4,12},{6,14},{8,0},{10,2},{12,4},{14,6},{16,24},{18,... | collective-permute-start | bytes 1572872 | tf_op jit(solution)/shard_map/ppermute | solution.py:21
  108.3 5.7 %fusion.1 = f32[8,512]{1,0:T(8,128)} fusion(f32[8,512,512]{1,2,0:T(8,128)} %copy-done.1, f32[8,512]{1,0:T(8,128)S(1)} %get-tuple-element.68, pred[512,512]{0,1:T(8,128)(4,1)S(1)} %iota_compare_fusion), kind=kLoop, calls=%fused_computation.3 | loop fusion | flops 8384512 | bytes 8683520 | tf_op jit(solution)/shard_map/reduce_sum | solution.py:59
  114.1 22.9 %collective-permute-done.4 = bf16[2,8,128,128]{3,2,1,0:T(8,128)(2,1)S(1)} collective-permute-done((bf16[2,8,128,128]{3,2,1,0:T(8,128)(2,1)S(1)}, bf16[2,8,128,128]{3,2,1,0:T(8,128)(2,1)S(1)}, u32[]{:S(2)}, u32[]{:S(2)}) %collective-permute-start.4) | collective-permute-done | bytes 524320 | tf_op jit(solution)/shard_map/ppermute | solution.py:21
  137.0 1.3 maximum_select_fusion.3
  138.3 1.6 collective-permute-start.5
  140.5 1.3 copy-done.2
  141.8 1.1 fusion.17
  142.9 0.8 copy.151
  143.7 1.3 fusion.18
  145.0 0.7 copy.176
  145.7 0.9 broadcast_in_dim.289
  146.6 0.7 copy.178
  147.5 2.7 fusion.23
  150.1 14.7 %collective-permute-done.5 = bf16[2,8,256,128]{3,2,1,0:T(8,128)(2,1)} collective-permute-done((bf16[2,8,256,128]{3,2,1,0:T(8,128)(2,1)}, bf16[2,8,256,128]{3,2,1,0:T(8,128)(2,1)}, u32[]{:S(2)}, u32[]{:S(2)}) %collective-permute-start.5) | collective-permute-done | bytes 1048608 | tf_op jit(solution)/shard_map/ppermute | solution.py:21
  164.9 2.8 maximum_select_fusion.1
  167.7 1.3 fusion.63
  169.2 1.3 fusion.34
  170.7 1.4 fusion.25
  172.1 82.3 %all-gather.2.cloned.1.call-done = bf16[2,8,1024,128]{3,2,1,0:T(8,128)(2,1)} async-done(((bf16[2,8,8,128]{3,2,1,0:T(8,128)(2,1)}), bf16[2,8,1024,128]{3,2,1,0:T(8,128)(2,1)}) %all-gather.2.cloned.1.call-update) | async-done | bytes 4194320 | tf_op jit(solution)/shard_map/all_gather | solution.py:122
  254.4 2.3 fusion.62
  257.3 2.2 fusion.9
  259.8 5.1 %fusion.16 = bf16[8,512,128]{2,1,0:T(8,128)(2,1)S(1)} fusion(f32[8,512,128]{2,1,0:T(8,128)S(1)} %bitcast.332, f32[8,512,128]{2,1,0:T(8,128)S(1)} %copy-done.3, f32[8,512]{1,0:T(8,128)S(1)} %get-tuple-element.5, f32[8,8,128]{2,1,0:T(8,128)S(1)} %fusion.9, f32[8,512]{1,0:T(8,128)S(1)} %get-tuple-element.9, f32[8,32,128]{2,1,0:T(8,128)S(1)} %fusion.25, ...), kind=kLoop, calls=%fused_computation.25 | loop fusion | flops 6291456 | bytes 5500928 | tf_op jit(solution)/shard_map/convert_element_type | solution.py:163
  264.9 0.7 copy.179
  266.1 31.4 %all_to_all.19 = bf16[2,256,1024]{2,1,0:T(8,128)(2,1)S(1)} all-to-all(bf16[2,256,1024]{2,1,0:T(8,128)(2,1)S(1)} %all_to_all.14), channel_id=1, replica_groups=mesh['ctx'=128,'tp'=2] {'tp'}, dimensions={0} | all-to-all | bytes 2097152 | tf_op jit(solution)/shard_map/all_to_all | solution.py:165
  298.1 1.4 copy.181
  (137 shorter events, 10.8 us)
Async XLA Ops:
  6.5 76.9 %copy-start = (bf16[512,1024]{1,0:T(8,128)(2,1)S(1)}, bf16[512,1024]{1,0:T(8,128)(2,1)}, u32[]{:S(2)}) copy-start(bf16[512,1024]{1,0:T(8,128)(2,1)} %param.3) | copy-start | bytes 3145732
  6.5 247.8 %all-gather.2.cloned.1.call-start = ((), (), s32[]{:S(2)}) async-start(), calls=%async_computation.1 | async-start | bytes 4227072 | tf_op jit(solution)/shard_map/all_gather | solution.py:122
  17.2 1.5 copy-start.5
  31.5 0.6 copy-start.13
  60.9 36.7 %collective-permute-start = (bf16[2,8,128,128]{3,2,1,0:T(8,128)(2,1)}, bf16[2,8,128,128]{3,2,1,0:T(8,128)(2,1)}, u32[]{:S(2)}, u32[]{:S(2)}) collective-permute-start(bf16[2,8,128,128]{3,2,1,0:T(8,128)(2,1)} %constant_dynamic-update-slice_fusion.8), channel_id=1, source_target_pairs={{0,2},{2,0},{4,6},{6,4},{8,10},{10,8},{12,14},{14,12},{16,18},{18,... | collective-permute-start | bytes 1572872 | tf_op jit(solution)/shard_map/ppermute | solution.py:21
  82.0 12.5 %collective-permute-start.2 = (bf16[2,8,32,128]{3,2,1,0:T(8,128)(2,1)}, bf16[2,8,32,128]{3,2,1,0:T(8,128)(2,1)S(1)}, u32[]{:S(2)}, u32[]{:S(2)}) collective-permute-start(bf16[2,8,32,128]{3,2,1,0:T(8,128)(2,1)} %constant_dynamic-update-slice_fusion.24), channel_id=1, source_target_pairs={{0,2},{2,0},{4,6},{6,4},{8,10},{10,8},{12,14},{14,12},{16,18},{18,... | collective-permute-start | bytes 393224 | tf_op jit(solution)/shard_map/ppermute | solution.py:21
  83.6 3.0 copy-start.4
  85.0 0.6 copy-start.8
  86.6 1.7 copy-start.6
  88.3 3.9 %copy-start.1 = (f32[8,512,512]{1,2,0:T(8,128)}, f32[8,512,512]{1,2,0:T(8,128)S(1)}, u32[]{:S(2)}) copy-start(f32[8,512,512]{1,2,0:T(8,128)S(1)} %get-tuple-element.69) | copy-start | bytes 25165828
  95.6 9.3 %collective-permute-start.3 = (bf16[2,8,64,128]{3,2,1,0:T(8,128)(2,1)S(1)}, bf16[2,8,64,128]{3,2,1,0:T(8,128)(2,1)S(1)}, u32[]{:S(2)}, u32[]{:S(2)}) collective-permute-start(bf16[2,8,64,128]{3,2,1,0:T(8,128)(2,1)S(1)} %maximum_select_fusion.5), channel_id=1, source_target_pairs={{0,4},{2,6},{4,0},{6,2},{8,12},{10,14},{12,8},{14,10},{16,20},{18,... | collective-permute-start | bytes 786440 | tf_op jit(solution)/shard_map/ppermute | solution.py:21
  99.4 40.4 %collective-permute-start.1 = (bf16[2,8,256,128]{3,2,1,0:T(8,128)(2,1)S(1)}, bf16[2,8,256,128]{3,2,1,0:T(8,128)(2,1)S(1)}, u32[]{:S(2)}, u32[]{:S(2)}) collective-permute-start(bf16[2,8,256,128]{3,2,1,0:T(8,128)(2,1)S(1)} %maximum_select_fusion.2), channel_id=1, source_target_pairs={{0,4},{2,6},{4,0},{6,2},{8,12},{10,14},{12,8},{14,10},{16,20},{18,... | collective-permute-start | bytes 3145736 | tf_op jit(solution)/shard_map/ppermute | solution.py:21
  99.6 14.4 %copy-start.18 = (bf16[8,8,128]{2,1,0:T(8,128)(2,1)}, bf16[8,8,128]{2,1,0:T(8,128)(2,1)S(1)}, u32[]{:S(2)}) copy-start(bf16[8,8,128]{2,1,0:T(8,128)(2,1)S(1)} %constant_dynamic-update-slice_fusion.32) | copy-start | bytes 49156
  105.0 32.0 %collective-permute-start.4 = (bf16[2,8,128,128]{3,2,1,0:T(8,128)(2,1)S(1)}, bf16[2,8,128,128]{3,2,1,0:T(8,128)(2,1)S(1)}, u32[]{:S(2)}, u32[]{:S(2)}) collective-permute-start(bf16[2,8,128,128]{3,2,1,0:T(8,128)(2,1)S(1)} %maximum_select_fusion.4), channel_id=1, source_target_pairs={{0,8},{2,10},{4,12},{6,14},{8,0},{10,2},{12,4},{14,6},{16,24},{18,... | collective-permute-start | bytes 1572872 | tf_op jit(solution)/shard_map/ppermute | solution.py:21
  138.3 26.6 %collective-permute-start.5 = (bf16[2,8,256,128]{3,2,1,0:T(8,128)(2,1)}, bf16[2,8,256,128]{3,2,1,0:T(8,128)(2,1)}, u32[]{:S(2)}, u32[]{:S(2)}) collective-permute-start(bf16[2,8,256,128]{3,2,1,0:T(8,128)(2,1)} %maximum_select_fusion.3), channel_id=1, source_target_pairs={{0,16},{2,18},{4,20},{6,22},{8,24},{10,26},{12,28},{14,30},{16,0},... | collective-permute-start | bytes 3145736 | tf_op jit(solution)/shard_map/ppermute | solution.py:21
  140.4 1.3 copy-start.2
  150.1 17.5 %copy-start.9 = (bf16[8,32,128]{2,1,0:T(8,128)(2,1)S(1)}, bf16[8,32,128]{2,1,0:T(8,128)(2,1)}, u32[]{:S(2)}) copy-start(bf16[8,32,128]{2,1,0:T(8,128)(2,1)} %copy-done.8) | copy-start | bytes 196612
  150.1 17.5 %copy-start.11 = (pred[32,512]{1,0:T(8,128)(4,1)S(1)}, pred[32,512]{1,0:T(8,128)(4,1)}, u32[]{:S(2)}) copy-start(pred[32,512]{1,0:T(8,128)(4,1)} %iota_compare_fusion.2) | copy-start | bytes 49156
  167.7 86.7 %copy-start.17 = (pred[8,1024]{1,0:T(8,128)(4,1)S(1)}, pred[8,1024]{1,0:T(8,128)(4,1)}, u32[]{:S(2)}) copy-start(pred[8,1024]{1,0:T(8,128)(4,1)} %iota_compare_fusion.3) | copy-start | bytes 24580
  167.7 86.7 %copy-start.19 = (bf16[8,8,128]{2,1,0:T(8,128)(2,1)S(1)}, bf16[8,8,128]{2,1,0:T(8,128)(2,1)}, u32[]{:S(2)}) copy-start(bf16[8,8,128]{2,1,0:T(8,128)(2,1)} %copy-done.18) | copy-start | bytes 49156
  170.7 86.5 %copy-start.10 = (f32[8,512]{1,0:T(8,128)S(1)}, f32[8,512]{1,0:T(8,128)}, u32[]{:S(2)}) copy-start(f32[8,512]{1,0:T(8,128)} %fusion.1) | copy-start | bytes 49156
  170.7 86.5 %copy-start.12 = (f32[8,512]{1,0:T(8,128)S(1)}, f32[8,512]{1,0:T(8,128)}, u32[]{:S(2)}) copy-start(f32[8,512]{1,0:T(8,128)} %copy.178) | copy-start | bytes 49156
  170.7 86.5 %copy-start.14 = (pred[8,512]{1,0:T(8,128)(4,1)S(1)}, pred[8,512]{1,0:T(8,128)(4,1)}, u32[]{:S(2)}) copy-start(pred[8,512]{1,0:T(8,128)(4,1)} %broadcast_in_dim.274) | copy-start | bytes 12292
  170.7 86.5 %copy-start.15 = (pred[8,512]{1,0:T(8,128)(4,1)S(1)}, pred[8,512]{1,0:T(8,128)(4,1)}, u32[]{:S(2)}) copy-start(pred[8,512]{1,0:T(8,128)(4,1)} %broadcast_in_dim.268) | copy-start | bytes 12292
  170.7 86.5 %copy-start.16 = (pred[8,512]{1,0:T(8,128)(4,1)S(1)}, pred[8,512]{1,0:T(8,128)(4,1)}, u32[]{:S(2)}) copy-start(pred[8,512]{1,0:T(8,128)(4,1)} %copy.152) | copy-start | bytes 12292
  256.7 2.8 copy-start.7
  257.3 2.6 copy-start.3
Sparse Core Ops, SparseCore 0:
  32.3 222.0 all-gather.1
where the time goes:
time: 310 us; the launch traced here: 306 us
  waiting for transfers between devices  125 us (40%)
  between operations  58.8 us (19%)
  local copies, waits for them, and re-layouts  43.8 us (14%)
  blocking collectives  31.4 us (10%)
  other arithmetic  23 us (7%)
  matrix products  16.5 us (5%)
  starting transfers between devices  7.63 us (2%)
    all_gather x1, waiting for transfers between devices, local(): lax.all_gather(gather_rows(key_value_couple, DILATION_FOURTH, shift_level...  82.3 us
    ppermute x6, waiting for transfers between devices, swapped(): return lax.ppermute(value, axis, pairs)  42.9 us
    all_to_all x1, blocking collectives, local(): lax.all_to_all(combined, 'tp', split_axis=0, concat_axis=1, tiled=True)  31.4 us
    unnamed x85, local copies, waits for them, and re-layouts  23.5 us
    dot_general x4, matrix products, attend(): jnp.einsum('hqk,hkd->hqd', exponent.astype(jnp.bfloat16), value_part, pre...  10.1 us
    reduce_sum x4, other arithmetic, attend(): row_sum = jnp.sum(exponent, axis=2)  8.45 us
    select_n x6, other arithmetic, join_rows(): jnp.where(is_upper, jnp.concatenate([partner, own_rows], axis=2), jnp.con...  7.67 us
    ppermute x6, starting transfers between devices, swapped(): return lax.ppermute(value, axis, pairs)  7.62 us
  transfers between devices with their start and end apart: 7, of which 4 were waited for; matrix products, arithmetic and copies ran while one was open for 19% of the time, Pallas kernels for 0%

commit v1 on v0

v1 whole, which is shorter than its diff:
```python
import math

import jax
import jax.numpy as jnp
from jax import lax
from jax.experimental import pallas as pl
from jax.experimental.pallas import tpu as pltpu
from jax.sharding import PartitionSpec as P

F32 = jnp.float32
BF16 = jnp.bfloat16
HD = 128
NEG = -1e30
SCALE = 1.0 / math.sqrt(HD)
VMEM = pltpu.VMEM


def dot_t(a, b):
    return lax.dot_general(a, b, (((1,), (1,)), ((), ())), preferred_element_type=F32)


def dot(a, b):
    return lax.dot_general(a, b, (((1,), (0,)), ((), ())), preferred_element_type=F32)


def softmax_terms(s, v):
    m = jnp.max(s, axis=1, keepdims=True)
    e = jnp.exp(s - m)
    l = jnp.sum(e, axis=1, keepdims=True)
    return m, l, dot(e.astype(BF16), v)


def iota(shape, axis):
    return lax.broadcasted_iota(jnp.int32, shape, axis)


def pack_stats(m, l):
    lane = iota((m.shape[0], HD), 1)
    return jnp.where(lane < 64, m, l)


def select_kernel(sc, q, k, v, q1, kv1, x2, wide, mid):
    h = pl.program_id(0)
    off = 2 * sc[0] + h // 4
    far = []
    for n, ref in enumerate((q, k, v)):
        wide[...] = ref[...].astype(F32)
        rows = wide[pl.ds(h % 4, 128, stride=4), :]
        mid[...] = rows
        if n == 0:
            q1[0] = rows.astype(BF16)
        else:
            kv1[n - 1, 0] = rows.astype(BF16)
            far.append(mid[pl.ds(off, 8, stride=16), :])
        x2[0, 32 * n : 32 * n + 32] = mid[pl.ds(off, 32, stride=4), :].astype(BF16)
    x2[0, 96:112] = jnp.concatenate(far, axis=0).astype(BF16)


def local_kernel(sc, q, k, v, keep, send, part, outs, sums, stats):
    h = pl.program_id(0)
    tp = sc[0]
    for b in range(2):
        rows = pl.ds(256 * b, 256)
        width = 256 * (b + 1)
        s = dot_t(q[rows, :], k[:width, :]) * SCALE
        ok = iota(s.shape, 1) <= iota(s.shape, 0) + 256 * b
        m, l, a = softmax_terms(jnp.where(ok, s, NEG), v[:width, :])
        outs[rows, :] = a / l
        sums[rows, :] = a
        stats[rows, :] = pack_stats(m, l)
    for n in range(3):
        r = (h + n + 1) % 4
        keep[0, n] = outs[pl.ds(r + 256 * tp, 64, stride=4), :].astype(BF16)
        send[0, n] = outs[pl.ds(r + 256 * (1 - tp), 64, stride=4), :].astype(BF16)
    part[0, :, :HD] = sums[pl.ds(h % 4, 128, stride=4), :]
    part[0, :, HD:] = stats[pl.ds(h % 4, 128, stride=4), :]


def near_kernel(sc, q1, own, mate, far_a, far_b, part, keep, send, keep2, send2, outs, sums):
    h = pl.program_id(0)
    tp, c4 = sc[0], sc[1]
    keys = jnp.concatenate([far_a[0, 0], far_b[0, 0], mate[0, 0], own[0, 0]], axis=0)
    vals = jnp.concatenate([far_a[1, 0], far_b[1, 0], mate[1, 0], own[1, 0]], axis=0)
    s = dot_t(q1[0], keys) * SCALE
    row, col = iota(s.shape, 0), iota(s.shape, 1)
    start = jnp.where(c4 >= 2, 0, 256)
    stop = jnp.where(c4 % 2 == 1, 384, 256)
    ok = ((col >= start) & (col < stop)) | ((col >= 384) & (col - 384 <= row))
    m1, l1, a1 = softmax_terms(jnp.where(ok, s, NEG), vals)
    a0 = part[0, :, :HD]
    m0 = part[0, :, HD : HD + 1]
    l0 = part[0, :, HD + 64 : HD + 65]
    top = jnp.maximum(m0, m1)
    e0, e1 = jnp.exp(m0 - top), jnp.exp(m1 - top)
    num = e0 * a0 + e1 * a1
    den = e0 * l0 + e1 * l1
    outs[...] = num / den
    keep[0] = outs[pl.ds(pl.multiple_of(64 * tp, 64), 64), :].astype(BF16)
    send[0] = outs[pl.ds(pl.multiple_of(64 * (1 - tp), 64), 64), :].astype(BF16)
    sums[0] = num
    sums[1] = pack_stats(top, den)
    off = 2 * tp + h // 4
    for n in range(2):
        cols = pl.ds(HD * n, HD)
        keep2[0, :, cols] = sums[n, pl.ds(off + 64 * tp, 16, stride=4), :]
        send2[0, :, cols] = sums[n, pl.ds(off + 64 * (1 - tp), 16, stride=4), :]


def far_kernel(sc, own, mate, line, g1, g2, g3, out, rows, sums, stats):
    x, y = sc[0], sc[1]
    blk = own[...].astype(F32)
    part = [blk[:, 32 * n : 32 * n + 32].reshape(256, HD) for n in range(3)]
    q2, k2, v2 = [p.astype(BF16) for p in part]
    rows[...] = part[0]
    oth = mate[...].astype(F32)
    k2o = oth[:, 0:32].reshape(256, HD).astype(BF16)
    v2o = oth[:, 32:64].reshape(256, HD).astype(BF16)
    s = dot_t(q2, jnp.concatenate([k2o, k2], axis=0)) * SCALE
    row, col = iota(s.shape, 0), iota(s.shape, 1)
    ok = ((col < 256) & (y % 2 == 1)) | ((col >= 256) & (col - 256 <= row))
    m2, l2, a2 = softmax_terms(jnp.where(ok, s, NEG), jnp.concatenate([v2o, v2], axis=0))
    sums[...] = a2
    stats[...] = pack_stats(m2, l2)

    q3 = rows[pl.ds(0, 64, stride=4), :].astype(BF16)
    keys, vals = [], []
    for ref in (g1, g2, g3, line):
        for j in range(4):
            b = ref[j].astype(F32)
            keys.append(b[:, 0:8].reshape(64, HD))
            vals.append(b[:, 8:16].reshape(64, HD))
    keys = jnp.concatenate(keys, axis=0).astype(BF16)
    vals = jnp.concatenate(vals, axis=0).astype(BF16)
    s = dot_t(q3, keys) * SCALE
    row, col = iota(s.shape, 0), iota(s.shape, 1)
    slot = col // 64
    earlier_x = (slot < 12) & (slot // 4 + 1 <= x)
    theirs = jnp.bitwise_xor(slot - 12, y)
    earlier_y = (slot > 12) & (theirs < y)
    mine = (slot == 12) & (col - 768 <= row)
    m3, l3, a3 = softmax_terms(jnp.where(earlier_x | earlier_y | mine, s, NEG), vals)
    a2 = sums[pl.ds(0, 64, stride=4), :]
    st = stats[pl.ds(0, 64, stride=4), :]
    m2, l2 = st[:, 0:1], st[:, 64:65]
    top = jnp.maximum(m2, m3)
    e2, e3 = jnp.exp(m2 - top), jnp.exp(m3 - top)
    sums[pl.ds(0, 64, stride=4), :] = e2 * a2 + e3 * a3
    stats[pl.ds(0, 64, stride=4), :] = pack_stats(top, e2 * l2 + e3 * l3)
    for j in range(16):
        out[j, :, :HD] = sums[16 * j : 16 * j + 16, :]
        out[j, :, HD:] = stats[16 * j : 16 * j + 16, :]


def join_kernel(sc, ka, kb, k2, ra, rb, r2, back, out, wide):
    tp = sc[0]
    for side, (first, second, third) in enumerate(((ka, kb, k2), (ra, rb, r2))):
        src = tp if side == 0 else 1 - tp
        for h in range(8):
            for n in range(3):
                wide[pl.ds((h + n + 1) % 4, 64, stride=4), :] = first[h, n].astype(F32)
            wide[pl.ds(h % 4, 64, stride=4), :] = second[h].astype(F32)
            mine = third[h]
            a0, m0, l0 = mine[:, :HD], mine[:, HD : HD + 1], mine[:, HD + 64 : HD + 65]
            more = back[2 * h + src]
            a1, m1, l1 = more[:, :HD], more[:, HD : HD + 1], more[:, HD + 64 : HD + 65]
            top = jnp.maximum(m0, m1)
            e0, e1 = jnp.exp(m0 - top), jnp.exp(m1 - top)
            wide[pl.ds(8 * src + h, 16, stride=16), :] = (e0 * a0 + e1 * a1) / (e0 * l0 + e1 * l1)
            cols = pl.ds(pl.multiple_of(src * 1024 + h * HD, HD), HD)
            out[:, cols] = wide[...].astype(BF16)


def spec(shape, index):
    return pl.BlockSpec(shape, index)


def head_call(kernel, name, ins, in_specs, outs, out_specs, scratch, scalars):
    return pl.pallas_call(
        kernel,
        out_shape=outs,
        grid_spec=pltpu.PrefetchScalarGridSpec(
            num_scalar_prefetch=1,
            grid=(8,),
            in_specs=in_specs,
            out_specs=out_specs,
            scratch_shapes=scratch,
        ),
        name=name,
    )(scalars, *ins)


def shape(dims, dtype):
    return jax.ShapeDtypeStruct(dims, dtype)


def local(queries, key_rows, value_rows):
    c = lax.axis_index("ctx")
    tp = lax.axis_index("tp")
    tps = jnp.stack([tp, c % 4]).astype(jnp.int32)
    xys = jnp.stack([c // 32, (c // 8) % 4]).astype(jnp.int32)

    cols = spec((512, HD), lambda h, s: (0, h))
    q1, kv1, x2 = head_call(
        select_kernel, "select", (queries, key_rows, value_rows), [cols] * 3,
        (shape((8, 128, HD), BF16), shape((2, 8, 128, HD), BF16), shape((8, 112, HD), BF16)),
        (spec((1, 128, HD), lambda h, s: (h, 0, 0)),
         spec((2, 1, 128, HD), lambda h, s: (0, h, 0, 0)),
         spec((1, 112, HD), lambda h, s: (h, 0, 0))),
        [VMEM((512, HD), F32), VMEM((128, HD), F32)], tps)

    n = 128
    mate = lax.ppermute(kv1, "ctx", [(i, i + 1) for i in range(0, n, 2)])
    far_a = lax.ppermute(kv1, "ctx", [(i, i + 2) for i in range(n) if i % 4 < 2])

    groups = [[8 * b + i for i in range(8)] for b in range(16)]
    y2 = lax.all_to_all(
        x2, "ctx", split_axis=0, concat_axis=0, tiled=True, axis_index_groups=groups)

    kv2 = y2[:, 32:112]
    kv3 = y2[:, 96:112]

    def flip_y(value, k):
        return lax.ppermute(value, "ctx", [(i, i ^ (8 * k)) for i in range(n)])

    from_1 = flip_y(kv2, 1)
    from_2 = flip_y(kv3, 2)
    from_3 = flip_y(kv3, 3)
    line = jnp.stack([kv3, from_1[:, 64:80], from_2, from_3])
    ahead = [
        lax.ppermute(line, "ctx", [(i, i + 32 * d) for i in range(n - 32 * d)]) for d in (1, 2, 3)
    ]
    far_b = lax.ppermute(far_a, "ctx", [(i, i ^ 1) for i in range(n) if i % 4 >= 2])

    rows3 = spec((1, 3, 64, HD), lambda h, s: (h, 0, 0, 0))
    keep, send, part = head_call(
        local_kernel, "local", (queries, key_rows, value_rows), [cols] * 3,
        (shape((8, 3, 64, HD), BF16), shape((8, 3, 64, HD), BF16), shape((8, 128, 256), F32)),
        (rows3, rows3, spec((1, 128, 256), lambda h, s: (h, 0, 0))),
        [VMEM((512, HD), F32)] * 3, tps)
    swap = [(0, 1), (1, 0)]
    got = lax.ppermute(send, "tp", swap)

    pair = spec((2, 1, 128, HD), lambda h, s: (0, h, 0, 0))
    half = spec((1, 64, HD), lambda h, s: (h, 0, 0))
    few = spec((1, 16, 256), lambda h, s: (h, 0, 0))
    keep1, send1, keep2, send2 = head_call(
        near_kernel, "near", (q1, kv1, mate, far_a, far_b, part),
        [spec((1, 128, HD), lambda h, s: (h, 0, 0)), pair, pair, pair, pair,
         spec((1, 128, 256), lambda h, s: (h, 0, 0))],
        (shape((8, 64, HD), BF16), shape((8, 64, HD), BF16),
         shape((8, 16, 256), F32), shape((8, 16, 256), F32)),
        (half, half, few, few),
        [VMEM((128, HD), F32), VMEM((2, 128, HD), F32)], tps)
    got1 = lax.ppermute(send1, "tp", swap)
    got2 = lax.ppermute(send2, "tp", swap)

    smem = pl.BlockSpec(memory_space=pltpu.SMEM)
    vm = pl.BlockSpec(memory_space=pltpu.VMEM)
    back = pl.pallas_call(
        far_kernel,
        out_shape=shape((16, 16, 256), F32),
        in_specs=[smem] + [vm] * 6,
        out_specs=vm,
        scratch_shapes=[VMEM((256, HD), F32)] * 3,
        name="far",
    )(xys, y2, from_1, line, *ahead)
    groups2 = [[16 * b + i for i in range(16)] for b in range(16)]
    back = lax.all_to_all(
        back, ("ctx", "tp"), split_axis=0, concat_axis=0, tiled=True, axis_index_groups=groups2)

    return pl.pallas_call(
        join_kernel,
        out_shape=shape((256, 2048), BF16),
        in_specs=[smem] + [vm] * 7,
        out_specs=vm,
        scratch_shapes=[VMEM((256, HD), F32)],
        name="join",
    )(tps, keep, keep1, keep2, got, got1, got2, back)


def solution(mesh):
    return jax.shard_map(
        local,
        mesh=mesh,
        in_specs=(P("ctx", "tp"), P("ctx", "tp"), P("ctx", "tp")),
        out_specs=P(("ctx", "tp"), None),
        check_vma=False,
    )
```

time: 310 us -> 106 us (0.34)
  waiting for transfers between devices: 125 us -> 28.3 us
  between operations: 58.8 us -> 0.21 us
  local copies, waits for them, and re-layouts: 43.8 us -> 2.4 us
  starting transfers between devices: 7.63 us -> 41.2 us
  Pallas kernels: 0 us -> 31.7 us
  blocking collectives: 31.4 us -> 0 us
  other arithmetic: 23 us -> 1.3 us
  matrix products: 16.5 us -> 0 us
    all_gather x1 -> x0, waiting for transfers between devices: 82.3 us -> none  [local(): lax.all_gather(gather_rows(key_value_couple, DILATION_FOURTH, shift_level...]
    pallas_call x0 -> x5, Pallas kernels: none -> 31.7 us  [the longest x3 25.7 us: head_call(): pl.pallas_call(kernel, out_shape=outs, grid_spec=pltpu.PrefetchScalarGrid...]
    all_to_all x1 -> x0, blocking collectives: 31.4 us -> none  [local(): lax.all_to_all(combined, 'tp', split_axis=0, concat_axis=1, tiled=True)]
    unnamed x85 -> x26, local copies, waits for them, and re-layouts: 23.5 us -> 2.38 us
    ppermute x6 -> x12, starting transfers between devices: 7.62 us -> 27 us  [the longest x1 5.91 us: local(): got = lax.ppermute(send, 'tp', swap)]
    ppermute x6 -> x12, waiting for transfers between devices: 42.9 us -> 25 us  [the longest x3 8.2 us: local(): lax.ppermute(line, 'ctx', [(i, i + 32 * d) for i in range(n - 32 * d)])]
    dot_general x8 -> x0, matrix products: 16.5 us -> none  [the longest x4 10.1 us: attend(): jnp.einsum('hqk,hkd->hqd', exponent.astype(jnp.bfloat16), value_part, pre...]
    all_to_all x0 -> x2, starting transfers between devices: none -> 14.2 us  [the longest x1 8.32 us: local(): lax.all_to_all(back, ('ctx', 'tp'), split_axis=0, concat_axis=0, tiled=Tr...]
  transfers between devices with their start and end apart: 7 -> 14, of which waited for: 4 -> 9; matrix products, arithmetic and copies ran while one was open for 19% -> 1% of each run, Pallas kernels for 0% -> 21%
where the time goes in v1:
time: 106 us; the launch traced here: 105 us
  starting transfers between devices  41.2 us (39%)
  Pallas kernels  31.7 us (30%)
  waiting for transfers between devices  28.3 us (27%)
  local copies, waits for them, and re-layouts  2.4 us (2%)
  other arithmetic  1.3 us (1%)
    pallas_call x3, Pallas kernels, head_call(): pl.pallas_call(kernel, out_shape=outs, grid_spec=pltpu.PrefetchScalarGrid...  25.7 us
    all_to_all x1, starting transfers between devices, local(): lax.all_to_all(back, ('ctx', 'tp'), split_axis=0, concat_axis=0, tiled=Tr...  8.32 us
    ppermute x3, waiting for transfers between devices, local(): lax.ppermute(line, 'ctx', [(i, i + 32 * d) for i in range(n - 32 * d)])  8.2 us
    ppermute x1, waiting for transfers between devices, local(): got1 = lax.ppermute(send1, 'tp', swap)  7.21 us
    ppermute x1, starting transfers between devices, local(): got = lax.ppermute(send, 'tp', swap)  5.91 us
    all_to_all x1, starting transfers between devices, local(): lax.all_to_all(x2, 'ctx', split_axis=0, concat_axis=0, tiled=True, axis_i...  5.9 us
    ppermute x1, starting transfers between devices, local(): got2 = lax.ppermute(send2, 'tp', swap)  5.83 us
    ppermute x1, waiting for transfers between devices, local(): got2 = lax.ppermute(send2, 'tp', swap)  4.98 us
  transfers between devices with their start and end apart: 14, of which 9 were waited for; matrix products, arithmetic and copies ran while one was open for 1% of the time, Pallas kernels for 21%

profile of v1, /device:TPU:6, one launch (start us, length us, event | category | flops | bytes accessed | tf_op | source)
XLA Modules:
  0.0 105.1 jit_solution(6657051122998762629)
XLA Ops:
  0.0 0.7 pad_add_fusion.sc
  0.7 6.7 %select.13 = (bf16[8,128,128]{2,1,0:T(8,128)(2,1)}, bf16[2,8,128,128]{3,2,1,0:T(8,128)(2,1)}, bf16[8,112,128]{2,1,0:T(8,128)(2,1)}) custom-call(s32[2]{0:T(128)} %pad_add_fusion.sc, bf16[512,1024]{1,0:T(8,128)(2,1)} %q.3, bf16[512,1024]{1,0:T(8,128)(2,1)} %k.3, bf16[512,1024]{1,0:T(8,128)(2,1)} %v.3), custom_call_target="tpu_custom_call" | custom-call | tf_op jit(solution)/shard_map/select/pallas_call | solution.py:178
  7.3 5.9 %all-to-all-start = ((bf16[8,112,128]{2,1,0:T(8,128)(2,1)}), bf16[8,112,128]{2,1,0:T(8,128)(2,1)S(1)}, u32[]{:S(2)}, u32[]{:S(2)}) async-start(bf16[8,112,128]{2,1,0:T(8,128)(2,1)} %get-tuple-element.24), calls=%async_computation | async-start | bytes 458752 | tf_op jit(solution)/shard_map/all_to_all | solution.py:216
  13.2 3.9 %collective-permute-start.1 = (bf16[2,8,128,128]{3,2,1,0:T(8,128)(2,1)}, bf16[2,8,128,128]{3,2,1,0:T(8,128)(2,1)S(1)}, u32[]{:S(2)}, u32[]{:S(2)}) collective-permute-start(bf16[2,8,128,128]{3,2,1,0:T(8,128)(2,1)} %get-tuple-element.17.own), channel_id=1, source_target_pairs={{0,4},{2,6},{8,12},{10,14},{16,20},{18,22},{24,28},{26,30},{32,36}... | collective-permute-start | bytes 1572872 | tf_op jit(solution)/shard_map/ppermute | solution.py:213
  17.2 1.8 %collective-permute-start = (bf16[2,8,128,128]{3,2,1,0:T(8,128)(2,1)}, bf16[2,8,128,128]{3,2,1,0:T(8,128)(2,1)S(1)}, u32[]{:S(2)}, u32[]{:S(2)}) collective-permute-start(bf16[2,8,128,128]{3,2,1,0:T(8,128)(2,1)} %get-tuple-element.17.own), channel_id=1, source_target_pairs={{0,2},{4,6},{8,10},{12,14},{16,18},{20,22},{24,26},{28,30},{32,34}... | collective-permute-start | bytes 1572872 | tf_op jit(solution)/shard_map/ppermute | solution.py:212
  19.0 3.3 %all-to-all-done.own = bf16[8,112,128]{2,1,0:T(8,128)(2,1)S(1)} async-done(((bf16[8,112,128]{2,1,0:T(8,128)(2,1)}), bf16[8,112,128]{2,1,0:T(8,128)(2,1)S(1)}, u32[]{:S(2)}, u32[]{:S(2)}) %all-to-all-start) | async-done | bytes 229408 | tf_op jit(solution)/shard_map/all_to_all | solution.py:216
  22.2 0.0 copy-start
  22.3 1.7 %collective-permute-start.6 = (bf16[8,80,128]{2,1,0:T(8,128)(2,1)S(1)}, bf16[8,80,128]{2,1,0:T(8,128)(2,1)S(1)}, u32[]{:S(2)}, u32[]{:S(2)}) collective-permute-start(bf16[8,80,128]{2,1,0:T(8,128)(2,1)S(1)} %slice.12), channel_id=1, source_target_pairs={{0,16},{2,18},{4,20},{6,22},{8,24},{10,26},{12,28},{14,30},{16,0},... | collective-permute-start | bytes 491528 | tf_op jit(solution)/shard_map/ppermute | solution.py:223
  23.9 2.3 %collective-permute-start.8 = (bf16[8,16,128]{2,1,0:T(8,128)(2,1)S(1)}, bf16[8,16,128]{2,1,0:T(8,128)(2,1)S(1)}, u32[]{:S(2)}, u32[]{:S(2)}) collective-permute-start(bf16[8,16,128]{2,1,0:T(8,128)(2,1)S(1)} %get-tuple-element.26), channel_id=1, source_target_pairs={{0,48},{2,50},{4,52},{6,54},{8,56},{10,58},{12,60},{14,62},{16,32}... | collective-permute-start | bytes 98312 | tf_op jit(solution)/shard_map/ppermute | solution.py:223
  26.2 0.8 collective-permute-start.7
  27.0 2.3 %collective-permute-done.1.far_a = bf16[2,8,128,128]{3,2,1,0:T(8,128)(2,1)S(1)} collective-permute-done((bf16[2,8,128,128]{3,2,1,0:T(8,128)(2,1)}, bf16[2,8,128,128]{3,2,1,0:T(8,128)(2,1)S(1)}, u32[]{:S(2)}, u32[]{:S(2)}) %collective-permute-start.1) | collective-permute-done | bytes 524320 | tf_op jit(solution)/shard_map/ppermute | solution.py:213
  29.4 0.0 copy-start.3
  29.4 0.7 collective-permute-start.2
  30.1 0.0 collective-permute-done.6.mate
  30.1 0.0 copy-start.7
  30.1 0.0 copy-done
  30.1 0.0 collective-permute-done.8
  30.1 1.5 %collective-permute-done.7 = bf16[8,16,128]{2,1,0:T(8,128)(2,1)S(1)} collective-permute-done((bf16[8,16,128]{2,1,0:T(8,128)(2,1)S(1)}, bf16[8,16,128]{2,1,0:T(8,128)(2,1)S(1)}, u32[]{:S(2)}, u32[]{:S(2)}) %collective-permute-start.7) | collective-permute-done | bytes 32800 | tf_op jit(solution)/shard_map/ppermute | solution.py:223
  31.6 0.0 copy-done.7
  31.7 0.0 copy-start.2
  31.7 1.3 %collective-permute-start.9 = (bf16[4,8,16,128]{3,2,1,0:T(8,128)(2,1)S(1)}, bf16[4,8,16,128]{3,2,1,0:T(8,128)(2,1)S(1)}, u32[]{:S(2)}, u32[]{:S(2)}) collective-permute-start(bf16[4,8,16,128]{3,2,1,0:T(8,128)(2,1)S(1)} %pad_maximum_fusion.line), channel_id=1, source_target_pairs={{0,64},{2,66},{4,68},{6,70},{8,72},{10,74},{12,76},{14,78},{16,80}... | collective-permute-start | bytes 393224 | tf_op jit(solution)/shard_map/ppermute | solution.py:230
  33.0 1.3 %collective-permute-start.10 = (bf16[4,8,16,128]{3,2,1,0:T(8,128)(2,1)S(1)}, bf16[4,8,16,128]{3,2,1,0:T(8,128)(2,1)S(1)}, u32[]{:S(2)}, u32[]{:S(2)}) collective-permute-start(bf16[4,8,16,128]{3,2,1,0:T(8,128)(2,1)S(1)} %pad_maximum_fusion.line), channel_id=1, source_target_pairs={{0,128},{2,130},{4,132},{6,134},{8,136},{10,138},{12,140},{14,142}... | collective-permute-start | bytes 393224 | tf_op jit(solution)/shard_map/ppermute | solution.py:230
  34.3 1.3 %collective-permute-start.11 = (bf16[4,8,16,128]{3,2,1,0:T(8,128)(2,1)S(1)}, bf16[4,8,16,128]{3,2,1,0:T(8,128)(2,1)S(1)}, u32[]{:S(2)}, u32[]{:S(2)}) collective-permute-start(bf16[4,8,16,128]{3,2,1,0:T(8,128)(2,1)S(1)} %pad_maximum_fusion.line), channel_id=1, source_target_pairs={{0,192},{2,194},{4,196},{6,198},{8,200},{10,202},{12,204},{14,206}... | collective-permute-start | bytes 393224 | tf_op jit(solution)/shard_map/ppermute | solution.py:230
  35.6 0.6 pad_add_fusion.1.sc
  36.2 2.3 %collective-permute-done.9.g1 = bf16[4,8,16,128]{3,2,1,0:T(8,128)(2,1)S(1)} collective-permute-done((bf16[4,8,16,128]{3,2,1,0:T(8,128)(2,1)S(1)}, bf16[4,8,16,128]{3,2,1,0:T(8,128)(2,1)S(1)}, u32[]{:S(2)}, u32[]{:S(2)}) %collective-permute-start.9) | collective-permute-done | bytes 131104 | tf_op jit(solution)/shard_map/ppermute | solution.py:230
  38.5 0.0 copy-start.8
  38.5 2.9 %collective-permute-done.10.g2 = bf16[4,8,16,128]{3,2,1,0:T(8,128)(2,1)S(1)} collective-permute-done((bf16[4,8,16,128]{3,2,1,0:T(8,128)(2,1)S(1)}, bf16[4,8,16,128]{3,2,1,0:T(8,128)(2,1)S(1)}, u32[]{:S(2)}, u32[]{:S(2)}) %collective-permute-start.10) | collective-permute-done | bytes 131104 | tf_op jit(solution)/shard_map/ppermute | solution.py:230
  41.4 0.0 copy-start.9
  41.4 3.0 %collective-permute-done.11.g3 = bf16[4,8,16,128]{3,2,1,0:T(8,128)(2,1)S(1)} collective-permute-done((bf16[4,8,16,128]{3,2,1,0:T(8,128)(2,1)S(1)}, bf16[4,8,16,128]{3,2,1,0:T(8,128)(2,1)S(1)}, u32[]{:S(2)}, u32[]{:S(2)}) %collective-permute-start.11) | collective-permute-done | bytes 131104 | tf_op jit(solution)/shard_map/ppermute | solution.py:230
  44.4 0.0 copy-done.2
  44.4 0.0 copy-done.8
  44.4 0.0 copy-done.9
  44.4 0.0 copy-start.10
  44.4 0.7 copy-done.10
  45.1 2.9 %far.1 = f32[16,16,256]{2,1,0:T(8,128)} custom-call(s32[2]{0:T(128)} %pad_add_fusion.1.sc, bf16[8,112,128]{2,1,0:T(8,128)(2,1)} %copy-done, bf16[8,80,128]{2,1,0:T(8,128)(2,1)} %copy-done.7, bf16[4,8,16,128]{3,2,1,0:T(8,128)(2,1)} %copy-done.2, bf16[4,8,16,128]{3,2,1,0:T(8,128)(2,1)} %copy-done.8, bf16[4,8,16,128]{3,2,1,0:T(8,128)(2,1)} %copy-done.9, ...), custom_call_target="tpu_custom_call" | custom-call | tf_op jit(solution)/shard_map/far/pallas_call | solution.py:259
  48.0 8.3 %all-to-all-start.1 = ((f32[16,16,256]{2,1,0:T(8,128)}), f32[16,16,256]{2,1,0:T(8,128)S(1)}, u32[]{:S(2)}, u32[]{:S(2)}) async-start(f32[16,16,256]{2,1,0:T(8,128)} %far.1), calls=%async_computation.1 | async-start | bytes 524288 | tf_op jit(solution)/shard_map/all_to_all | solution.py:268
  56.3 9.9 %local.1 = (bf16[8,3,64,128]{3,2,1,0:T(8,128)(2,1)}, bf16[8,3,64,128]{3,2,1,0:T(8,128)(2,1)}, f32[8,128,256]{2,1,0:T(8,128)}) custom-call(s32[2]{0:T(128)} %pad_add_fusion.sc, bf16[512,1024]{1,0:T(8,128)(2,1)} %q.3, bf16[512,1024]{1,0:T(8,128)(2,1)} %k.3, bf16[512,1024]{1,0:T(8,128)(2,1)} %v.3), custom_call_target="tpu_custom_call" | custom-call | tf_op jit(solution)/shard_map/local/pallas_call | solution.py:178
  66.2 0.0 copy-done.3
  66.2 5.9 %collective-permute-start.3 = (bf16[8,3,64,128]{3,2,1,0:T(8,128)(2,1)}, bf16[8,3,64,128]{3,2,1,0:T(8,128)(2,1)S(1)}, u32[]{:S(2)}, u32[]{:S(2)}) collective-permute-start(bf16[8,3,64,128]{3,2,1,0:T(8,128)(2,1)} %get-tuple-element.21), channel_id=1, source_target_pairs={{0,1},{1,0},{2,3},{3,2},{4,5},{5,4},{6,7},{7,6},{8,9},{9,8},{10,11... | collective-permute-start | bytes 1179656 | tf_op jit(solution)/shard_map/ppermute | solution.py:241
  72.1 0.0 collective-permute-done.mate
  72.1 0.0 copy-start.4
  72.1 0.0 collective-permute-done.2.far_b
  72.1 0.0 copy-start.5
  72.1 0.8 copy-done.4
  72.9 0.2 copy-done.5
  73.1 9.2 %near.1 = (bf16[8,64,128]{2,1,0:T(8,128)(2,1)}, bf16[8,64,128]{2,1,0:T(8,128)(2,1)}, f32[8,16,256]{2,1,0:T(8,128)}, f32[8,16,256]{2,1,0:T(8,128)}) custom-call(s32[2]{0:T(128)} %pad_add_fusion.sc, bf16[8,128,128]{2,1,0:T(8,128)(2,1)} %get-tuple-element.16.q1, bf16[2,8,128,128]{3,2,1,0:T(8,128)(2,1)} %get-tuple-element.17.own, ...), custom_call_target="tpu_custom_call" | custom-call | tf_op jit(solution)/shard_map/near/pallas_call | solution.py:178
  82.2 0.2 collective-permute-start.4
  82.4 5.8 %collective-permute-start.5 = (f32[8,16,256]{2,1,0:T(8,128)}, f32[8,16,256]{2,1,0:T(8,128)S(1)}, u32[]{:S(2)}, u32[]{:S(2)}) collective-permute-start(f32[8,16,256]{2,1,0:T(8,128)} %get-tuple-element.23), channel_id=1, source_target_pairs={{0,1},{1,0},{2,3},{3,2},{4,5},{5,4},{6,7},{7,6},{8,9},{9,8},{10,11... | collective-permute-start | bytes 393224 | tf_op jit(solution)/shard_map/ppermute | solution.py:255
  88.2 0.8 collective-permute-done.3.ra
  89.0 0.0 copy-start.6
  89.0 7.2 %collective-permute-done.4.rb = bf16[8,64,128]{2,1,0:T(8,128)(2,1)S(1)} collective-permute-done((bf16[8,64,128]{2,1,0:T(8,128)(2,1)}, bf16[8,64,128]{2,1,0:T(8,128)(2,1)S(1)}, u32[]{:S(2)}, u32[]{:S(2)}) %collective-permute-start.4) | collective-permute-done | bytes 131104 | tf_op jit(solution)/shard_map/ppermute | solution.py:254
  96.2 0.0 copy-start.11
  96.2 5.0 %collective-permute-done.5.r2 = f32[8,16,256]{2,1,0:T(8,128)S(1)} collective-permute-done((f32[8,16,256]{2,1,0:T(8,128)}, f32[8,16,256]{2,1,0:T(8,128)S(1)}, u32[]{:S(2)}, u32[]{:S(2)}) %collective-permute-start.5) | collective-permute-done | bytes 131104 | tf_op jit(solution)/shard_map/ppermute | solution.py:255
  101.2 0.0 copy-start.12
  101.2 0.0 all-to-all-done.1.back
  101.2 0.0 copy-start.1
  101.2 0.0 copy-done.6
  101.2 0.0 copy-done.11
  101.2 0.6 copy-done.12
  101.9 0.1 copy-done.1
  102.0 3.1 %join.1 = bf16[256,2048]{1,0:T(8,128)(2,1)} custom-call(s32[2]{0:T(128)} %pad_add_fusion.sc, bf16[8,3,64,128]{3,2,1,0:T(8,128)(2,1)} %get-tuple-element.15.ka, bf16[8,64,128]{2,1,0:T(8,128)(2,1)} %get-tuple-element.19.kb, f32[8,16,256]{2,1,0:T(8,128)} %get-tuple-element.20.k2, bf16[8,3,64,128]{3,2,1,0:T(8,128)(2,1)} %copy-done.6, ...), custom_call_target="tpu_custom_call" | custom-call | tf_op jit(solution)/shard_map/join/pallas_call | solution.py:271
  (4 shorter events, 0.0 us)
Async XLA Ops:
  7.3 14.9 %all-to-all-start = ((bf16[8,112,128]{2,1,0:T(8,128)(2,1)}), bf16[8,112,128]{2,1,0:T(8,128)(2,1)S(1)}, u32[]{:S(2)}, u32[]{:S(2)}) async-start(bf16[8,112,128]{2,1,0:T(8,128)(2,1)} %get-tuple-element.24), calls=%async_computation | async-start | bytes 458752 | tf_op jit(solution)/shard_map/all_to_all | solution.py:216
  13.2 16.1 %collective-permute-start.1 = (bf16[2,8,128,128]{3,2,1,0:T(8,128)(2,1)}, bf16[2,8,128,128]{3,2,1,0:T(8,128)(2,1)S(1)}, u32[]{:S(2)}, u32[]{:S(2)}) collective-permute-start(bf16[2,8,128,128]{3,2,1,0:T(8,128)(2,1)} %get-tuple-element.17.own), channel_id=1, source_target_pairs={{0,4},{2,6},{8,12},{10,14},{16,20},{18,22},{24,28},{26,30},{32,36}... | collective-permute-start | bytes 1572872 | tf_op jit(solution)/shard_map/ppermute | solution.py:213
  17.2 54.9 %collective-permute-start = (bf16[2,8,128,128]{3,2,1,0:T(8,128)(2,1)}, bf16[2,8,128,128]{3,2,1,0:T(8,128)(2,1)S(1)}, u32[]{:S(2)}, u32[]{:S(2)}) collective-permute-start(bf16[2,8,128,128]{3,2,1,0:T(8,128)(2,1)} %get-tuple-element.17.own), channel_id=1, source_target_pairs={{0,2},{4,6},{8,10},{12,14},{16,18},{20,22},{24,26},{28,30},{32,34}... | collective-permute-start | bytes 1572872 | tf_op jit(solution)/shard_map/ppermute | solution.py:212
  22.2 7.9 %copy-start = (bf16[8,112,128]{2,1,0:T(8,128)(2,1)}, bf16[8,112,128]{2,1,0:T(8,128)(2,1)S(1)}, u32[]{:S(2)}) copy-start(bf16[8,112,128]{2,1,0:T(8,128)(2,1)S(1)} %all-to-all-done.own) | copy-start | bytes 688132
  22.3 7.8 %collective-permute-start.6 = (bf16[8,80,128]{2,1,0:T(8,128)(2,1)S(1)}, bf16[8,80,128]{2,1,0:T(8,128)(2,1)S(1)}, u32[]{:S(2)}, u32[]{:S(2)}) collective-permute-start(bf16[8,80,128]{2,1,0:T(8,128)(2,1)S(1)} %slice.12), channel_id=1, source_target_pairs={{0,16},{2,18},{4,20},{6,22},{8,24},{10,26},{12,28},{14,30},{16,0},... | collective-permute-start | bytes 491528 | tf_op jit(solution)/shard_map/ppermute | solution.py:223
  23.9 6.2 %collective-permute-start.8 = (bf16[8,16,128]{2,1,0:T(8,128)(2,1)S(1)}, bf16[8,16,128]{2,1,0:T(8,128)(2,1)S(1)}, u32[]{:S(2)}, u32[]{:S(2)}) collective-permute-start(bf16[8,16,128]{2,1,0:T(8,128)(2,1)S(1)} %get-tuple-element.26), channel_id=1, source_target_pairs={{0,48},{2,50},{4,52},{6,54},{8,56},{10,58},{12,60},{14,62},{16,32}... | collective-permute-start | bytes 98312 | tf_op jit(solution)/shard_map/ppermute | solution.py:223
  26.2 5.4 %collective-permute-start.7 = (bf16[8,16,128]{2,1,0:T(8,128)(2,1)S(1)}, bf16[8,16,128]{2,1,0:T(8,128)(2,1)S(1)}, u32[]{:S(2)}, u32[]{:S(2)}) collective-permute-start(bf16[8,16,128]{2,1,0:T(8,128)(2,1)S(1)} %get-tuple-element.26), channel_id=1, source_target_pairs={{0,32},{2,34},{4,36},{6,38},{8,40},{10,42},{12,44},{14,46},{16,48}... | collective-permute-start | bytes 98312 | tf_op jit(solution)/shard_map/ppermute | solution.py:223
  29.4 36.8 %copy-start.3 = (bf16[2,8,128,128]{3,2,1,0:T(8,128)(2,1)}, bf16[2,8,128,128]{3,2,1,0:T(8,128)(2,1)S(1)}, u32[]{:S(2)}) copy-start(bf16[2,8,128,128]{3,2,1,0:T(8,128)(2,1)S(1)} %collective-permute-done.1.far_a) | copy-start | bytes 1572868
  29.4 42.7 %collective-permute-start.2 = (bf16[2,8,128,128]{3,2,1,0:T(8,128)(2,1)S(1)}, bf16[2,8,128,128]{3,2,1,0:T(8,128)(2,1)S(1)}, u32[]{:S(2)}, u32[]{:S(2)}) collective-permute-start(bf16[2,8,128,128]{3,2,1,0:T(8,128)(2,1)S(1)} %collective-permute-done.1.far_a), channel_id=1, source_target_pairs={{4,6},{6,4},{12,14},{14,12},{20,22},{22,20},{28,30},{30,28},{36,38... | collective-permute-start | bytes 1572872 | tf_op jit(solution)/shard_map/ppermute | solution.py:232
  30.1 1.6 %copy-start.7 = (bf16[8,80,128]{2,1,0:T(8,128)(2,1)}, bf16[8,80,128]{2,1,0:T(8,128)(2,1)S(1)}, u32[]{:S(2)}) copy-start(bf16[8,80,128]{2,1,0:T(8,128)(2,1)S(1)} %collective-permute-done.6.mate) | copy-start | bytes 491524
  31.7 12.8 %copy-start.2 = (bf16[4,8,16,128]{3,2,1,0:T(8,128)(2,1)}, bf16[4,8,16,128]{3,2,1,0:T(8,128)(2,1)S(1)}, u32[]{:S(2)}) copy-start(bf16[4,8,16,128]{3,2,1,0:T(8,128)(2,1)S(1)} %pad_maximum_fusion.line) | copy-start | bytes 393220
  31.7 6.9 %collective-permute-start.9 = (bf16[4,8,16,128]{3,2,1,0:T(8,128)(2,1)S(1)}, bf16[4,8,16,128]{3,2,1,0:T(8,128)(2,1)S(1)}, u32[]{:S(2)}, u32[]{:S(2)}) collective-permute-start(bf16[4,8,16,128]{3,2,1,0:T(8,128)(2,1)S(1)} %pad_maximum_fusion.line), channel_id=1, source_target_pairs={{0,64},{2,66},{4,68},{6,70},{8,72},{10,74},{12,76},{14,78},{16,80}... | collective-permute-start | bytes 393224 | tf_op jit(solution)/shard_map/ppermute | solution.py:230
  33.0 8.4 %collective-permute-start.10 = (bf16[4,8,16,128]{3,2,1,0:T(8,128)(2,1)S(1)}, bf16[4,8,16,128]{3,2,1,0:T(8,128)(2,1)S(1)}, u32[]{:S(2)}, u32[]{:S(2)}) collective-permute-start(bf16[4,8,16,128]{3,2,1,0:T(8,128)(2,1)S(1)} %pad_maximum_fusion.line), channel_id=1, source_target_pairs={{0,128},{2,130},{4,132},{6,134},{8,136},{10,138},{12,140},{14,142}... | collective-permute-start | bytes 393224 | tf_op jit(solution)/shard_map/ppermute | solution.py:230
  34.3 10.2 %collective-permute-start.11 = (bf16[4,8,16,128]{3,2,1,0:T(8,128)(2,1)S(1)}, bf16[4,8,16,128]{3,2,1,0:T(8,128)(2,1)S(1)}, u32[]{:S(2)}, u32[]{:S(2)}) collective-permute-start(bf16[4,8,16,128]{3,2,1,0:T(8,128)(2,1)S(1)} %pad_maximum_fusion.line), channel_id=1, source_target_pairs={{0,192},{2,194},{4,196},{6,198},{8,200},{10,202},{12,204},{14,206}... | collective-permute-start | bytes 393224 | tf_op jit(solution)/shard_map/ppermute | solution.py:230
  38.5 5.9 %copy-start.8 = (bf16[4,8,16,128]{3,2,1,0:T(8,128)(2,1)}, bf16[4,8,16,128]{3,2,1,0:T(8,128)(2,1)S(1)}, u32[]{:S(2)}) copy-start(bf16[4,8,16,128]{3,2,1,0:T(8,128)(2,1)S(1)} %collective-permute-done.9.g1) | copy-start | bytes 393220
  41.4 3.0 %copy-start.9 = (bf16[4,8,16,128]{3,2,1,0:T(8,128)(2,1)}, bf16[4,8,16,128]{3,2,1,0:T(8,128)(2,1)S(1)}, u32[]{:S(2)}) copy-start(bf16[4,8,16,128]{3,2,1,0:T(8,128)(2,1)S(1)} %collective-permute-done.10.g2) | copy-start | bytes 393220
  44.4 0.7 copy-start.10
  48.0 53.2 %all-to-all-start.1 = ((f32[16,16,256]{2,1,0:T(8,128)}), f32[16,16,256]{2,1,0:T(8,128)S(1)}, u32[]{:S(2)}, u32[]{:S(2)}) async-start(f32[16,16,256]{2,1,0:T(8,128)} %far.1), calls=%async_computation.1 | async-start | bytes 524288 | tf_op jit(solution)/shard_map/all_to_all | solution.py:268
  66.2 22.8 %collective-permute-start.3 = (bf16[8,3,64,128]{3,2,1,0:T(8,128)(2,1)}, bf16[8,3,64,128]{3,2,1,0:T(8,128)(2,1)S(1)}, u32[]{:S(2)}, u32[]{:S(2)}) collective-permute-start(bf16[8,3,64,128]{3,2,1,0:T(8,128)(2,1)} %get-tuple-element.21), channel_id=1, source_target_pairs={{0,1},{1,0},{2,3},{3,2},{4,5},{5,4},{6,7},{7,6},{8,9},{9,8},{10,11... | collective-permute-start | bytes 1179656 | tf_op jit(solution)/shard_map/ppermute | solution.py:241
  72.1 0.8 copy-start.4
  72.1 1.0 copy-start.5
  82.2 14.0 %collective-permute-start.4 = (bf16[8,64,128]{2,1,0:T(8,128)(2,1)}, bf16[8,64,128]{2,1,0:T(8,128)(2,1)S(1)}, u32[]{:S(2)}, u32[]{:S(2)}) collective-permute-start(bf16[8,64,128]{2,1,0:T(8,128)(2,1)} %get-tuple-element.22), channel_id=1, source_target_pairs={{0,1},{1,0},{2,3},{3,2},{4,5},{5,4},{6,7},{7,6},{8,9},{9,8},{10,11... | collective-permute-start | bytes 393224 | tf_op jit(solution)/shard_map/ppermute | solution.py:254
  82.4 18.8 %collective-permute-start.5 = (f32[8,16,256]{2,1,0:T(8,128)}, f32[8,16,256]{2,1,0:T(8,128)S(1)}, u32[]{:S(2)}, u32[]{:S(2)}) collective-permute-start(f32[8,16,256]{2,1,0:T(8,128)} %get-tuple-element.23), channel_id=1, source_target_pairs={{0,1},{1,0},{2,3},{3,2},{4,5},{5,4},{6,7},{7,6},{8,9},{9,8},{10,11... | collective-permute-start | bytes 393224 | tf_op jit(solution)/shard_map/ppermute | solution.py:255
  89.0 12.2 %copy-start.6 = (bf16[8,3,64,128]{3,2,1,0:T(8,128)(2,1)}, bf16[8,3,64,128]{3,2,1,0:T(8,128)(2,1)S(1)}, u32[]{:S(2)}) copy-start(bf16[8,3,64,128]{3,2,1,0:T(8,128)(2,1)S(1)} %collective-permute-done.3.ra) | copy-start | bytes 1179652
  96.2 5.0 %copy-start.11 = (bf16[8,64,128]{2,1,0:T(8,128)(2,1)}, bf16[8,64,128]{2,1,0:T(8,128)(2,1)S(1)}, u32[]{:S(2)}) copy-start(bf16[8,64,128]{2,1,0:T(8,128)(2,1)S(1)} %collective-permute-done.4.rb) | copy-start | bytes 393220
  101.2 0.6 copy-start.12
  101.2 0.7 copy-start.1

commit v2 on v0

v2 whole, which is shorter than its diff:
```python
import math

import jax
import jax.numpy as jnp
from jax import lax
from jax.experimental import pallas as pl
from jax.experimental.pallas import tpu as pltpu
from jax.sharding import PartitionSpec as P

F32 = jnp.float32
BF16 = jnp.bfloat16
HD = 128
NEG = -1e30
SCALE = math.log2(math.e) / math.sqrt(HD)
VMEM = pltpu.VMEM
LIMIT = 24 * 2**20


def dot_t(a, b):
    return lax.dot_general(a, b, (((1,), (1,)), ((), ())), preferred_element_type=F32)


def dot(a, b):
    return lax.dot_general(a, b, (((1,), (0,)), ((), ())), preferred_element_type=F32)


def iota(shape, axis):
    return lax.broadcasted_iota(jnp.int32, shape, axis)


def attend(s, v):
    m = jnp.max(s, axis=1, keepdims=True)
    e = jnp.exp2(s - m)
    l = jnp.sum(e, axis=1, keepdims=True)
    return dot(e.astype(BF16), v) / l, m + jnp.log2(l)


def merge(o0, z0, o1, z1):
    top = jnp.maximum(z0, z1)
    w0, w1 = jnp.exp2(z0 - top), jnp.exp2(z1 - top)
    den = w0 + w1
    return (w0 * o0 + w1 * o1) / den, top + jnp.log2(den)


def split3(z):
    hi = z.astype(BF16).astype(F32)
    mid = (z - hi).astype(BF16).astype(F32)
    lo = z - hi - mid
    lane = iota((z.shape[0], HD), 1)
    out = jnp.where(lane == 0, hi, jnp.where(lane == 1, mid, jnp.where(lane == 2, lo, 0.0)))
    return out.astype(BF16)


def join3(p):
    return jnp.sum(p.astype(F32), axis=1, keepdims=True)


def head(h):
    return slice(h * HD, (h + 1) * HD)


def head_copies(hbm, vmem, sems):
    def copy(n, h):
        return pltpu.make_async_copy(
            hbm[n].at[:, head(h)], vmem.at[n, :, head(h)], sems.at[n, h])

    for h in range(8):
        for n in range(3):
            copy(n, h).start()

    def arrive(h):
        for n in range(3):
            copy(n, h).wait()

    return arrive


def select_kernel(q, k, v, q1, kv1, x2, rows_in, wide, s1, s2, sems, sems_out):
    tp = lax.axis_index("tp")
    arrive = head_copies((q, k, v), rows_in, sems)
    pending = []

    def leave(src, dst, slot, h):
        copy = pltpu.make_async_copy(src, dst, sems_out.at[slot, h])
        copy.start()
        pending.append(copy)

    for h in range(8):
        arrive(h)
        far = []
        for n in range(3):
            buf = wide.at[(3 * h + n) % 6]
            buf[...] = rows_in[n, :, head(h)].astype(F32)
            s1[n, h] = buf[pl.ds(h % 4, 128, stride=4), :].astype(BF16)
            if n > 0:
                far.append(buf[pl.ds(8 * tp + h, 8, stride=64), :])
            s2[h, 32 * n : 32 * n + 32] = buf[pl.ds(8 * tp + h, 32, stride=16), :].astype(BF16)
        s2[h, 96:112] = jnp.concatenate(far, axis=0).astype(BF16)
        leave(s2.at[h], x2.at[h], 0, h)
        leave(s1.at[0, h], q1.at[h], 1, h)
        leave(s1.at[1, h], kv1.at[0, h], 2, h)
        leave(s1.at[2, h], kv1.at[1, h], 3, h)
    for copy in pending:
        copy.wait()


def local_kernel(q, k, v, keep, send, part, rows_in, mine, theirs, outs, stats, sems, sems_out):
    tp = lax.axis_index("tp")
    arrive = head_copies((q, k, v), rows_in, sems)
    pending = []
    ok = iota((256, 256), 1) <= iota((256, 256), 0)
    for h in range(8):
        arrive(h)
        o_ref, z_ref = outs.at[h % 4], stats.at[h % 4]
        for b in range(2):
            rows = slice(256 * b, 256 * b + 256)
            upto = slice(0, 256 * b + 256)
            s = dot_t(rows_in[0, rows, head(h)], rows_in[1, upto, head(h)]) * SCALE
            last = jnp.where(ok, s[:, 256 * b :], NEG)
            s = last if b == 0 else jnp.concatenate([s[:, :256], last], axis=1)
            o, z = attend(s, rows_in[2, upto, head(h)])
            o_ref[rows, :] = o
            z_ref[rows, :] = jnp.broadcast_to(z, (256, HD))
        for n in range(3):
            r = (h + n + 1) % 4
            mine[h, n] = o_ref[pl.ds(r + 256 * tp, 64, stride=4), :].astype(BF16)
            theirs[h, n] = o_ref[pl.ds(r + 256 * (1 - tp), 64, stride=4), :].astype(BF16)
        for slot, (src, dst) in enumerate(((theirs, send), (mine, keep))):
            copy = pltpu.make_async_copy(src.at[h], dst.at[h], sems_out.at[slot, h])
            copy.start()
            pending.append(copy)
        part[h, :, :HD] = o_ref[pl.ds(h % 4, 128, stride=4), :]
        part[h, :, HD:] = z_ref[pl.ds(h % 4, 128, stride=4), :]
    for copy in pending:
        copy.wait()


def near_kernel(q1, own, mate, far_a, far_b, part, keep, send, outs, stats):
    tp = lax.axis_index("tp")
    c4 = lax.rem(lax.axis_index("ctx"), 4)
    row, col = iota((128, 512), 0), iota((128, 512), 1)
    start = jnp.where(c4 >= 2, 0, 256)
    stop = jnp.where(lax.rem(c4, 2) == 1, 384, 256)
    ok = ((col >= start) & (col < stop)) | ((col >= 384) & (col - 384 <= row))
    for h in range(8):
        o_ref, z_ref = outs.at[h % 4], stats.at[h % 4]
        keys = jnp.concatenate([far_a[0, h], far_b[0, h], mate[0, h], own[0, h]], axis=0)
        vals = jnp.concatenate([far_a[1, h], far_b[1, h], mate[1, h], own[1, h]], axis=0)
        s = dot_t(q1[h], keys) * SCALE
        o1, z1 = attend(jnp.where(ok, s, NEG), vals)
        o, z = merge(part[h, :, :HD], part[h, :, HD : HD + 1], o1, z1)
        o_ref[...] = o
        z_ref[...] = jnp.broadcast_to(z, (128, HD))
        for ref, side in ((keep, tp), (send, 1 - tp)):
            base = pl.multiple_of(64 * side, 64)
            ref[h, :64] = o_ref[pl.ds(base, 64), :].astype(BF16)
            few = z_ref[pl.ds(64 * side + 2 * tp + h // 4, 16, stride=4), :]
            ref[h, 64:80] = split3(few[:, 0:1])


def far_kernel(own, mate, line, g1, g2, g3, out, rows, sums, stats):
    c = lax.axis_index("ctx")
    x, y = lax.div(c, 32), lax.rem(lax.div(c, 8), 4)

    def part(ref, start):
        return ref[:, start : start + 32].astype(F32).reshape(256, HD)

    rows[...] = part(own, 0)
    keys = jnp.concatenate([part(mate, 0), part(own, 32)], axis=0).astype(BF16)
    vals = jnp.concatenate([part(mate, 32), part(own, 64)], axis=0).astype(BF16)
    s = dot_t(rows[...].astype(BF16), keys) * SCALE
    row, col = iota(s.shape, 0), iota(s.shape, 1)
    ok = ((col < 256) & (lax.rem(y, 2) == 1)) | ((col >= 256) & (col - 256 <= row))
    o2, z2 = attend(jnp.where(ok, s, NEG), vals)
    sums[...] = o2
    stats[...] = jnp.broadcast_to(z2, (256, HD))

    q3 = rows[pl.ds(0, 64, stride=4), :].astype(BF16)
    keys, vals = [], []
    for ref in (g1, g2, g3, line):
        for j in range(4):
            b = ref[j].astype(F32)
            keys.append(b[:, 0:8].reshape(64, HD))
            vals.append(b[:, 8:16].reshape(64, HD))
    keys = jnp.concatenate(keys, axis=0).astype(BF16)
    vals = jnp.concatenate(vals, axis=0).astype(BF16)
    s = dot_t(q3, keys) * SCALE
    row, col = iota(s.shape, 0), iota(s.shape, 1)
    slot = lax.shift_right_logical(col, 6)
    earlier_x = (slot < 12) & (jnp.bitwise_xor(lax.shift_right_logical(slot, 2) + 1, x) < x)
    earlier_y = (slot > 12) & (jnp.bitwise_xor(slot - 12, y) < y)
    mine = (slot == 12) & (col - 768 <= row)
    o3, z3 = attend(jnp.where(earlier_x | earlier_y | mine, s, NEG), vals)
    pick = pl.ds(0, 64, stride=4)
    o, z = merge(sums[pick, :], stats[pick, :][:, 0:1], o3, z3)
    sums[pick, :] = o
    stats[pick, :] = jnp.broadcast_to(z, (64, HD))
    for j in range(16):
        out[j, :, :HD] = sums[16 * j : 16 * j + 16, :].astype(BF16)
        out[j, :, HD:] = split3(stats[16 * j : 16 * j + 16, :][:, 0:1])


def join_kernel(ka, kb, ra, rb, back, out, wide):
    tp = lax.axis_index("tp")
    for h in range(8):
        for side, (first, second) in enumerate(((ka, kb), (ra, rb))):
            src = tp if side == 0 else 1 - tp
            buf = wide.at[(2 * h + side) % 4]
            for n in range(3):
                buf[pl.ds((h + n + 1) % 4, 64, stride=4), :] = first[h, n].astype(F32)
            buf[pl.ds(h % 4, 64, stride=4), :] = second[h, :64].astype(F32)
            pick = pl.ds(8 * src + h, 16, stride=16)
            more = back[2 * h + src]
            o, _ = merge(
                buf[pick, :], join3(second[h, 64:80]), more[:, :HD].astype(F32), join3(more[:, HD:]))
            buf[pick, :] = o
            cols = pl.ds(pl.multiple_of(src * 1024 + h * HD, HD), HD)
            out[:, cols] = buf[...].astype(BF16)


def call(kernel, name, ins, outs, scratch):
    vm, hbm = pl.BlockSpec(memory_space=VMEM), pl.BlockSpec(memory_space=pltpu.HBM)
    spaces = {"V": VMEM, "H": pltpu.HBM}
    args = [pltpu.with_memory_space_constraint(a, spaces[m]) if m else a for a, m in ins]
    return pl.pallas_call(
        kernel,
        out_shape=[spaces[m](*o) if m else jax.ShapeDtypeStruct(*o) for o, m in outs],
        in_specs=[hbm if m == "H" else vm for _, m in ins],
        out_specs=[hbm if m == "H" else vm for _, m in outs],
        scratch_shapes=scratch,
        compiler_params=pltpu.CompilerParams(vmem_limit_bytes=LIMIT),
        name=name,
    )(*args)


def local(queries, key_rows, value_rows):
    n = 128

    def exchange(value, axes, size, total):
        groups = [[size * b + i for i in range(size)] for b in range(total // size)]
        return lax.all_to_all(
            value, axes, split_axis=0, concat_axis=0, tiled=True, axis_index_groups=groups)

    def flip(value, bits):
        return lax.ppermute(value, "ctx", [(i, i ^ bits) for i in range(n)])

    barrier = lax.optimization_barrier
    dma = pltpu.SemaphoreType.DMA
    args = [(queries, "H"), (key_rows, "H"), (value_rows, "H")]
    q1, kv1, x2 = call(
        select_kernel, "select", args,
        ((((8, 128, HD), BF16), "H"), (((2, 8, 128, HD), BF16), "H"), (((8, 112, HD), BF16), "H")),
        [VMEM((3, 512, 1024), BF16), VMEM((6, 512, HD), F32), VMEM((3, 8, 128, HD), BF16),
         VMEM((8, 112, HD), BF16), dma((3, 8)), dma((4, 8))])
    y2 = exchange(x2, "ctx", 8, n)
    mate = flip(kv1, 1)
    far_a = flip(kv1, 2)

    y2, queries, key_rows, value_rows = barrier((y2, queries, key_rows, value_rows))
    kv2 = y2[:, 32:112]
    kv3 = y2[:, 96:112]
    flips = [flip(kv2 if j == 1 else kv3, 8 * j) for j in (1, 2, 3)]

    keep, send, part = call(
        local_kernel, "local", [(queries, "H"), (key_rows, "H"), (value_rows, "H")],
        ((((8, 3, 64, HD), BF16), "H"), (((8, 3, 64, HD), BF16), "H"), (((8, 128, 256), F32), "V")),
        [VMEM((3, 512, 1024), BF16), VMEM((8, 3, 64, HD), BF16), VMEM((8, 3, 64, HD), BF16),
         VMEM((4, 512, HD), F32), VMEM((4, 512, HD), F32), dma((3, 8)), dma((2, 8))])
    swap = [(0, 1), (1, 0)]
    got = lax.ppermute(send, "tp", swap)

    line = jnp.stack([kv3, flips[0][:, 64:80], flips[1], flips[2]])
    line, far_a, part = barrier((line, far_a, part))
    ahead = [flip(line, 32 * j) for j in (1, 2, 3)]
    far_b = flip(far_a, 1)

    keep1, send1 = call(
        near_kernel, "near", [(a, "V") for a in (q1, kv1, mate, far_a, far_b, part)],
        ((((8, 80, HD), BF16), None), (((8, 80, HD), BF16), None)),
        [VMEM((4, 128, HD), F32), VMEM((4, 128, HD), F32)])
    got1 = lax.ppermute(send1, "tp", swap)

    y2, keep1 = barrier((y2, keep1))
    (back,) = call(
        far_kernel, "far", [(a, "V") for a in (y2, flips[0], line, *ahead)],
        ((((16, 16, 256), BF16), None),), [VMEM((256, HD), F32)] * 3)
    back = exchange(back, ("ctx", "tp"), 16, 2 * n)

    (out,) = call(
        join_kernel, "join", [(a, "V") for a in (keep, keep1, got, got1, back)],
        ((((256, 2048), BF16), None),), [VMEM((4, 256, HD), F32)])
    return out


def solution(mesh):
    return jax.shard_map(
        local,
        mesh=mesh,
        in_specs=(P("ctx", "tp"), P("ctx", "tp"), P("ctx", "tp")),
        out_specs=P(("ctx", "tp"), None),
        check_vma=False,
    )
```

time: 310 us -> 71.7 us (0.23)
  waiting for transfers between devices: 125 us -> 20.7 us
  between operations: 58.8 us -> 0.13 us
  local copies, waits for them, and re-layouts: 43.8 us -> 0.04 us
  blocking collectives: 31.4 us -> 0 us
  starting transfers between devices: 7.63 us -> 31.6 us
  other arithmetic: 23 us -> 0.02 us
  Pallas kernels: 0 us -> 18.2 us
  matrix products: 16.5 us -> 0 us
    all_gather x1 -> x0, waiting for transfers between devices: 82.3 us -> none  [local(): lax.all_gather(gather_rows(key_value_couple, DILATION_FOURTH, shift_level...]
    all_to_all x1 -> x0, blocking collectives: 31.4 us -> none  [local(): lax.all_to_all(combined, 'tp', split_axis=0, concat_axis=1, tiled=True)]
    ppermute x6 -> x11, waiting for transfers between devices: 42.9 us -> 14 us  [the longest x1 11 us: local(): got1 = lax.ppermute(send1, 'tp', swap)]
    unnamed x85 -> x6, local copies, waits for them, and re-layouts: 23.5 us -> 0.01 us
    pallas_call x0 -> x5, Pallas kernels: none -> 18.2 us  [call(): pl.pallas_call(kernel, out_shape=[spaces[m](*o) if m else jax.ShapeDtypeS...]
    dot_general x8 -> x0, matrix products: 16.5 us -> none  [the longest x4 10.1 us: attend(): jnp.einsum('hqk,hkd->hqd', exponent.astype(jnp.bfloat16), value_part, pre...]
    ppermute x6 -> x11, starting transfers between devices: 7.62 us -> 22.2 us  [the longest x9 11.7 us: flip(): return lax.ppermute(value, 'ctx', [(i, i ^ bits) for i in range(n)])]
    all_to_all x0 -> x2, starting transfers between devices: none -> 9.43 us  [exchange(): lax.all_to_all(value, axes, split_axis=0, concat_axis=0, tiled=True, axis...]
  transfers between devices with their start and end apart: 7 -> 13, of which waited for: 4 -> 3; matrix products, arithmetic and copies ran while one was open for 19% -> 0% of each run, Pallas kernels for 0% -> 18%
where the time goes in v2:
time: 71.7 us; the launch traced here: 70.7 us
  starting transfers between devices  31.6 us (44%)
  waiting for transfers between devices  20.7 us (29%)
  Pallas kernels  18.2 us (25%)
    pallas_call x5, Pallas kernels, call(): pl.pallas_call(kernel, out_shape=[spaces[m](*o) if m else jax.ShapeDtypeS...  18.2 us
    ppermute x9, starting transfers between devices, flip(): return lax.ppermute(value, 'ctx', [(i, i ^ bits) for i in range(n)])  11.7 us
    ppermute x1, waiting for transfers between devices, local(): got1 = lax.ppermute(send1, 'tp', swap)  11 us
    all_to_all x2, starting transfers between devices, exchange(): lax.all_to_all(value, axes, split_axis=0, concat_axis=0, tiled=True, axis...  9.43 us
    all_to_all x2, waiting for transfers between devices, exchange(): lax.all_to_all(value, axes, split_axis=0, concat_axis=0, tiled=True, axis...  6.73 us
    ppermute x1, starting transfers between devices, local(): got1 = lax.ppermute(send1, 'tp', swap)  5.71 us
    ppermute x1, starting transfers between devices, local(): got = lax.ppermute(send, 'tp', swap)  4.75 us
    ppermute x9, waiting for transfers between devices, flip(): return lax.ppermute(value, 'ctx', [(i, i ^ bits) for i in range(n)])  2.96 us
  transfers between devices with their start and end apart: 13, of which 3 were waited for; matrix products, arithmetic and copies ran while one was open for 0% of the time, Pallas kernels for 18%

profile of v2, /device:TPU:6, one launch (start us, length us, event | category | flops | bytes accessed | tf_op | source)
XLA Modules:
  0.0 70.7 jit_solution(4916359889315501817)
XLA Ops:
  0.0 3.5 %select.1 = (bf16[8,128,128]{2,1,0:T(8,128)(2,1)}, bf16[2,8,128,128]{3,2,1,0:T(8,128)(2,1)}, bf16[8,112,128]{2,1,0:T(8,128)(2,1)}) custom-call(bf16[512,1024]{1,0:T(8,128)(2,1)} %q.2, bf16[512,1024]{1,0:T(8,128)(2,1)} %k.2, bf16[512,1024]{1,0:T(8,128)(2,1)} %v.2), custom_call_target="tpu_custom_call" | custom-call | tf_op jit(solution)/shard_map/select/pallas_call | solution.py:225
  3.5 5.9 %all-to-all-start = ((bf16[8,112,128]{2,1,0:T(8,128)(2,1)}), bf16[8,112,128]{2,1,0:T(8,128)(2,1)S(1)}, u32[]{:S(2)}, u32[]{:S(2)}) async-start(bf16[8,112,128]{2,1,0:T(8,128)(2,1)} %get-tuple-element.22), calls=%async_computation | async-start | bytes 458752 | tf_op jit(solution)/shard_map/all_to_all | solution.py:241
  9.5 2.0 %collective-permute-start.4 = (bf16[2,8,128,128]{3,2,1,0:T(8,128)(2,1)}, bf16[2,8,128,128]{3,2,1,0:T(8,128)(2,1)S(1)}, u32[]{:S(2)}, u32[]{:S(2)}) collective-permute-start(bf16[2,8,128,128]{3,2,1,0:T(8,128)(2,1)} %get-tuple-element.29.own), channel_id=1, source_target_pairs={{0,4},{2,6},{4,0},{6,2},{8,12},{10,14},{12,8},{14,10},{16,20},{18,... | collective-permute-start | bytes 1572872 | tf_op jit(solution)/shard_map/ppermute | solution.py:245
  11.5 0.0 collective-permute-start
  11.5 6.7 %all-to-all-done.own = bf16[8,112,128]{2,1,0:T(8,128)(2,1)S(1)} async-done(((bf16[8,112,128]{2,1,0:T(8,128)(2,1)}), bf16[8,112,128]{2,1,0:T(8,128)(2,1)S(1)}, u32[]{:S(2)}, u32[]{:S(2)}) %all-to-all-start) | async-done | bytes 229408 | tf_op jit(solution)/shard_map/all_to_all | solution.py:241
  18.2 1.7 %collective-permute-start.1 = (bf16[8,80,128]{2,1,0:T(8,128)(2,1)S(1)}, bf16[8,80,128]{2,1,0:T(8,128)(2,1)S(1)}, u32[]{:S(2)}, u32[]{:S(2)}) collective-permute-start(bf16[8,80,128]{2,1,0:T(8,128)(2,1)S(1)} %slice.10), channel_id=1, source_target_pairs={{0,16},{2,18},{4,20},{6,22},{8,24},{10,26},{12,28},{14,30},{16,0},... | collective-permute-start | bytes 491528 | tf_op jit(solution)/shard_map/ppermute | solution.py:245
  19.9 3.0 %collective-permute-start.2 = (bf16[8,16,128]{2,1,0:T(8,128)(2,1)S(1)}, bf16[8,16,128]{2,1,0:T(8,128)(2,1)S(1)}, u32[]{:S(2)}, u32[]{:S(2)}) collective-permute-start(bf16[8,16,128]{2,1,0:T(8,128)(2,1)S(1)} %get-tuple-element.40), channel_id=1, source_target_pairs={{0,32},{2,34},{4,36},{6,38},{8,40},{10,42},{12,44},{14,46},{16,48}... | collective-permute-start | bytes 98312 | tf_op jit(solution)/shard_map/ppermute | solution.py:245
  22.9 0.2 collective-permute-start.3
  23.1 0.0 copy-start
  23.1 8.4 %local.1 = (bf16[8,3,64,128]{3,2,1,0:T(8,128)(2,1)}, bf16[8,3,64,128]{3,2,1,0:T(8,128)(2,1)}, f32[8,128,256]{2,1,0:T(8,128)S(1)}) custom-call(bf16[512,1024]{1,0:T(8,128)(2,1)} %q.2, bf16[512,1024]{1,0:T(8,128)(2,1)} %k.2, bf16[512,1024]{1,0:T(8,128)(2,1)} %v.2), custom_call_target="tpu_custom_call" | custom-call | tf_op jit(solution)/shard_map/local/pallas_call | solution.py:225
  31.5 0.0 copy-start.2
  31.5 0.0 collective-permute-done.1.mate
  31.5 0.0 collective-permute-done.2
  31.6 0.0 collective-permute-done.3
  31.6 0.0 collective-permute-done.4.far_a
  31.6 0.1 collective-permute-start.5
  31.7 4.8 %collective-permute-start.6 = (bf16[8,3,64,128]{3,2,1,0:T(8,128)(2,1)}, bf16[8,3,64,128]{3,2,1,0:T(8,128)(2,1)S(1)}, u32[]{:S(2)}, u32[]{:S(2)}) collective-permute-start(bf16[8,3,64,128]{3,2,1,0:T(8,128)(2,1)} %get-tuple-element.35), channel_id=1, source_target_pairs={{0,1},{1,0},{2,3},{3,2},{4,5},{5,4},{6,7},{7,6},{8,9},{9,8},{10,11... | collective-permute-start | bytes 1179656 | tf_op jit(solution)/shard_map/ppermute | solution.py:270
  36.5 0.5 collective-permute-start.10
  36.9 0.9 %collective-permute-start.8 = (bf16[4,8,16,128]{3,2,1,0:T(8,128)(2,1)S(1)}, bf16[4,8,16,128]{3,2,1,0:T(8,128)(2,1)S(1)}, u32[]{:S(2)}, u32[]{:S(2)}) collective-permute-start(bf16[4,8,16,128]{3,2,1,0:T(8,128)(2,1)S(1)} %pad_maximum_fusion.line), channel_id=1, source_target_pairs={{0,64},{2,66},{4,68},{6,70},{8,72},{10,74},{12,76},{14,78},{16,80}... | collective-permute-start | bytes 393224 | tf_op jit(solution)/shard_map/ppermute | solution.py:245
  37.8 0.0 collective-permute-done.mate
  37.8 3.3 %collective-permute-start.9 = (bf16[4,8,16,128]{3,2,1,0:T(8,128)(2,1)S(1)}, bf16[4,8,16,128]{3,2,1,0:T(8,128)(2,1)S(1)}, u32[]{:S(2)}, u32[]{:S(2)}) collective-permute-start(bf16[4,8,16,128]{3,2,1,0:T(8,128)(2,1)S(1)} %pad_maximum_fusion.line), channel_id=1, source_target_pairs={{0,128},{2,130},{4,132},{6,134},{8,136},{10,138},{12,140},{14,142}... | collective-permute-start | bytes 393224 | tf_op jit(solution)/shard_map/ppermute | solution.py:245
  41.2 0.0 collective-permute-done.5.far_b
  41.2 0.0 copy-done
  41.2 0.0 copy-done.2
  41.2 3.1 %near.1 = (bf16[8,80,128]{2,1,0:T(8,128)(2,1)S(1)}, bf16[8,80,128]{2,1,0:T(8,128)(2,1)S(1)}) custom-call(bf16[8,128,128]{2,1,0:T(8,128)(2,1)S(1)} %copy-done.2, bf16[2,8,128,128]{3,2,1,0:T(8,128)(2,1)S(1)} %copy-done, bf16[2,8,128,128]{3,2,1,0:T(8,128)(2,1)S(1)} %collective-permute-done.mate, bf16[2,8,128,128]{3,2,1,0:T(8,128)(2,1)S(1)} %collective-permute-done.4.far_a, ...), custom_call_target="tpu_custom_call" | custom-call | tf_op jit(solution)/shard_map/near/pallas_call | solution.py:225
  44.2 0.0 collective-permute-done.10.g3
  44.2 0.0 collective-permute-done.8.g1
  44.3 2.9 %collective-permute-done.9.g2 = bf16[4,8,16,128]{3,2,1,0:T(8,128)(2,1)S(1)} collective-permute-done((bf16[4,8,16,128]{3,2,1,0:T(8,128)(2,1)S(1)}, bf16[4,8,16,128]{3,2,1,0:T(8,128)(2,1)S(1)}, u32[]{:S(2)}, u32[]{:S(2)}) %collective-permute-start.9) | collective-permute-done | bytes 131104 | tf_op jit(solution)/shard_map/ppermute | solution.py:245
  47.2 0.0 copy-start.1
  47.2 1.6 %far.1 = bf16[16,16,256]{2,1,0:T(8,128)(2,1)} custom-call(bf16[8,112,128]{2,1,0:T(8,128)(2,1)S(1)} %all-to-all-done.own, bf16[8,80,128]{2,1,0:T(8,128)(2,1)S(1)} %collective-permute-done.1.mate, bf16[4,8,16,128]{3,2,1,0:T(8,128)(2,1)S(1)} %pad_maximum_fusion.line, bf16[4,8,16,128]{3,2,1,0:T(8,128)(2,1)S(1)} %collective-permute-done.8.g1, ...), custom_call_target="tpu_custom_call" | custom-call | tf_op jit(solution)/shard_map/far/pallas_call | solution.py:225
  48.8 3.5 %all-to-all-start.1 = ((bf16[16,16,256]{2,1,0:T(8,128)(2,1)}), bf16[16,16,256]{2,1,0:T(8,128)(2,1)S(1)}, u32[]{:S(2)}, u32[]{:S(2)}) async-start(bf16[16,16,256]{2,1,0:T(8,128)(2,1)} %far.1), calls=%async_computation.1 | async-start | bytes 262144 | tf_op jit(solution)/shard_map/all_to_all | solution.py:241
  52.3 5.7 %collective-permute-start.7 = (bf16[8,80,128]{2,1,0:T(8,128)(2,1)S(1)}, bf16[8,80,128]{2,1,0:T(8,128)(2,1)S(1)}, u32[]{:S(2)}, u32[]{:S(2)}) collective-permute-start(bf16[8,80,128]{2,1,0:T(8,128)(2,1)S(1)} %get-tuple-element.36), channel_id=1, source_target_pairs={{0,1},{1,0},{2,3},{3,2},{4,5},{5,4},{6,7},{7,6},{8,9},{9,8},{10,11... | collective-permute-start | bytes 491528 | tf_op jit(solution)/shard_map/ppermute | solution.py:281
  58.0 0.0 collective-permute-done.6.ra
  58.0 11.0 %collective-permute-done.7.rb = bf16[8,80,128]{2,1,0:T(8,128)(2,1)S(1)} collective-permute-done((bf16[8,80,128]{2,1,0:T(8,128)(2,1)S(1)}, bf16[8,80,128]{2,1,0:T(8,128)(2,1)S(1)}, u32[]{:S(2)}, u32[]{:S(2)}) %collective-permute-start.7) | collective-permute-done | bytes 163872 | tf_op jit(solution)/shard_map/ppermute | solution.py:281
  69.0 0.0 all-to-all-done.1.back
  69.0 0.0 copy-done.1
  69.0 1.6 %join.1 = bf16[256,2048]{1,0:T(8,128)(2,1)} custom-call(bf16[8,3,64,128]{3,2,1,0:T(8,128)(2,1)S(1)} %copy-done.1, bf16[8,80,128]{2,1,0:T(8,128)(2,1)S(1)} %get-tuple-element.34.kb, bf16[8,3,64,128]{3,2,1,0:T(8,128)(2,1)S(1)} %collective-permute-done.6.ra, bf16[8,80,128]{2,1,0:T(8,128)(2,1)S(1)} %collective-permute-done.7.rb, ...), custom_call_target="tpu_custom_call" | custom-call | tf_op jit(solution)/shard_map/join/pallas_call | solution.py:225
  (4 shorter events, 0.0 us)
Async XLA Ops:
  3.5 14.7 %all-to-all-start = ((bf16[8,112,128]{2,1,0:T(8,128)(2,1)}), bf16[8,112,128]{2,1,0:T(8,128)(2,1)S(1)}, u32[]{:S(2)}, u32[]{:S(2)}) async-start(bf16[8,112,128]{2,1,0:T(8,128)(2,1)} %get-tuple-element.22), calls=%async_computation | async-start | bytes 458752 | tf_op jit(solution)/shard_map/all_to_all | solution.py:241
  9.5 22.1 %collective-permute-start.4 = (bf16[2,8,128,128]{3,2,1,0:T(8,128)(2,1)}, bf16[2,8,128,128]{3,2,1,0:T(8,128)(2,1)S(1)}, u32[]{:S(2)}, u32[]{:S(2)}) collective-permute-start(bf16[2,8,128,128]{3,2,1,0:T(8,128)(2,1)} %get-tuple-element.29.own), channel_id=1, source_target_pairs={{0,4},{2,6},{4,0},{6,2},{8,12},{10,14},{12,8},{14,10},{16,20},{18,... | collective-permute-start | bytes 1572872 | tf_op jit(solution)/shard_map/ppermute | solution.py:245
  11.5 26.3 %collective-permute-start = (bf16[2,8,128,128]{3,2,1,0:T(8,128)(2,1)}, bf16[2,8,128,128]{3,2,1,0:T(8,128)(2,1)S(1)}, u32[]{:S(2)}, u32[]{:S(2)}) collective-permute-start(bf16[2,8,128,128]{3,2,1,0:T(8,128)(2,1)} %get-tuple-element.29.own), channel_id=1, source_target_pairs={{0,2},{2,0},{4,6},{6,4},{8,10},{10,8},{12,14},{14,12},{16,18},{18,... | collective-permute-start | bytes 1572872 | tf_op jit(solution)/shard_map/ppermute | solution.py:245
  18.2 13.3 %collective-permute-start.1 = (bf16[8,80,128]{2,1,0:T(8,128)(2,1)S(1)}, bf16[8,80,128]{2,1,0:T(8,128)(2,1)S(1)}, u32[]{:S(2)}, u32[]{:S(2)}) collective-permute-start(bf16[8,80,128]{2,1,0:T(8,128)(2,1)S(1)} %slice.10), channel_id=1, source_target_pairs={{0,16},{2,18},{4,20},{6,22},{8,24},{10,26},{12,28},{14,30},{16,0},... | collective-permute-start | bytes 491528 | tf_op jit(solution)/shard_map/ppermute | solution.py:245
  19.9 11.6 %collective-permute-start.2 = (bf16[8,16,128]{2,1,0:T(8,128)(2,1)S(1)}, bf16[8,16,128]{2,1,0:T(8,128)(2,1)S(1)}, u32[]{:S(2)}, u32[]{:S(2)}) collective-permute-start(bf16[8,16,128]{2,1,0:T(8,128)(2,1)S(1)} %get-tuple-element.40), channel_id=1, source_target_pairs={{0,32},{2,34},{4,36},{6,38},{8,40},{10,42},{12,44},{14,46},{16,48}... | collective-permute-start | bytes 98312 | tf_op jit(solution)/shard_map/ppermute | solution.py:245
  22.9 8.7 %collective-permute-start.3 = (bf16[8,16,128]{2,1,0:T(8,128)(2,1)S(1)}, bf16[8,16,128]{2,1,0:T(8,128)(2,1)S(1)}, u32[]{:S(2)}, u32[]{:S(2)}) collective-permute-start(bf16[8,16,128]{2,1,0:T(8,128)(2,1)S(1)} %get-tuple-element.40), channel_id=1, source_target_pairs={{0,48},{2,50},{4,52},{6,54},{8,56},{10,58},{12,60},{14,62},{16,32}... | collective-permute-start | bytes 98312 | tf_op jit(solution)/shard_map/ppermute | solution.py:245
  23.1 18.1 %copy-start = (bf16[2,8,128,128]{3,2,1,0:T(8,128)(2,1)S(1)}, bf16[2,8,128,128]{3,2,1,0:T(8,128)(2,1)}, u32[]{:S(2)}) copy-start(bf16[2,8,128,128]{3,2,1,0:T(8,128)(2,1)} %get-tuple-element.29.own) | copy-start | bytes 1572868
  31.5 9.7 %copy-start.2 = (bf16[8,128,128]{2,1,0:T(8,128)(2,1)S(1)}, bf16[8,128,128]{2,1,0:T(8,128)(2,1)}, u32[]{:S(2)}) copy-start(bf16[8,128,128]{2,1,0:T(8,128)(2,1)} %get-tuple-element.28.q1) | copy-start | bytes 786436
  31.6 9.6 %collective-permute-start.5 = (bf16[2,8,128,128]{3,2,1,0:T(8,128)(2,1)S(1)}, bf16[2,8,128,128]{3,2,1,0:T(8,128)(2,1)S(1)}, u32[]{:S(2)}, u32[]{:S(2)}) collective-permute-start(bf16[2,8,128,128]{3,2,1,0:T(8,128)(2,1)S(1)} %collective-permute-done.4.far_a), channel_id=1, source_target_pairs={{0,2},{2,0},{4,6},{6,4},{8,10},{10,8},{12,14},{14,12},{16,18},{18,... | collective-permute-start | bytes 1572872 | tf_op jit(solution)/shard_map/ppermute | solution.py:245
  31.7 26.3 %collective-permute-start.6 = (bf16[8,3,64,128]{3,2,1,0:T(8,128)(2,1)}, bf16[8,3,64,128]{3,2,1,0:T(8,128)(2,1)S(1)}, u32[]{:S(2)}, u32[]{:S(2)}) collective-permute-start(bf16[8,3,64,128]{3,2,1,0:T(8,128)(2,1)} %get-tuple-element.35), channel_id=1, source_target_pairs={{0,1},{1,0},{2,3},{3,2},{4,5},{5,4},{6,7},{7,6},{8,9},{9,8},{10,11... | collective-permute-start | bytes 1179656 | tf_op jit(solution)/shard_map/ppermute | solution.py:270
  36.5 7.8 %collective-permute-start.10 = (bf16[4,8,16,128]{3,2,1,0:T(8,128)(2,1)S(1)}, bf16[4,8,16,128]{3,2,1,0:T(8,128)(2,1)S(1)}, u32[]{:S(2)}, u32[]{:S(2)}) collective-permute-start(bf16[4,8,16,128]{3,2,1,0:T(8,128)(2,1)S(1)} %pad_maximum_fusion.line), channel_id=1, source_target_pairs={{0,192},{2,194},{4,196},{6,198},{8,200},{10,202},{12,204},{14,206}... | collective-permute-start | bytes 393224 | tf_op jit(solution)/shard_map/ppermute | solution.py:245
  36.9 7.3 %collective-permute-start.8 = (bf16[4,8,16,128]{3,2,1,0:T(8,128)(2,1)S(1)}, bf16[4,8,16,128]{3,2,1,0:T(8,128)(2,1)S(1)}, u32[]{:S(2)}, u32[]{:S(2)}) collective-permute-start(bf16[4,8,16,128]{3,2,1,0:T(8,128)(2,1)S(1)} %pad_maximum_fusion.line), channel_id=1, source_target_pairs={{0,64},{2,66},{4,68},{6,70},{8,72},{10,74},{12,76},{14,78},{16,80}... | collective-permute-start | bytes 393224 | tf_op jit(solution)/shard_map/ppermute | solution.py:245
  37.8 9.4 %collective-permute-start.9 = (bf16[4,8,16,128]{3,2,1,0:T(8,128)(2,1)S(1)}, bf16[4,8,16,128]{3,2,1,0:T(8,128)(2,1)S(1)}, u32[]{:S(2)}, u32[]{:S(2)}) collective-permute-start(bf16[4,8,16,128]{3,2,1,0:T(8,128)(2,1)S(1)} %pad_maximum_fusion.line), channel_id=1, source_target_pairs={{0,128},{2,130},{4,132},{6,134},{8,136},{10,138},{12,140},{14,142}... | collective-permute-start | bytes 393224 | tf_op jit(solution)/shard_map/ppermute | solution.py:245
  47.2 21.8 %copy-start.1 = (bf16[8,3,64,128]{3,2,1,0:T(8,128)(2,1)S(1)}, bf16[8,3,64,128]{3,2,1,0:T(8,128)(2,1)}, u32[]{:S(2)}) copy-start(bf16[8,3,64,128]{3,2,1,0:T(8,128)(2,1)} %get-tuple-element.26.ka) | copy-start | bytes 1179652
  48.8 20.2 %all-to-all-start.1 = ((bf16[16,16,256]{2,1,0:T(8,128)(2,1)}), bf16[16,16,256]{2,1,0:T(8,128)(2,1)S(1)}, u32[]{:S(2)}, u32[]{:S(2)}) async-start(bf16[16,16,256]{2,1,0:T(8,128)(2,1)} %far.1), calls=%async_computation.1 | async-start | bytes 262144 | tf_op jit(solution)/shard_map/all_to_all | solution.py:241
  52.3 16.7 %collective-permute-start.7 = (bf16[8,80,128]{2,1,0:T(8,128)(2,1)S(1)}, bf16[8,80,128]{2,1,0:T(8,128)(2,1)S(1)}, u32[]{:S(2)}, u32[]{:S(2)}) collective-permute-start(bf16[8,80,128]{2,1,0:T(8,128)(2,1)S(1)} %get-tuple-element.36), channel_id=1, source_target_pairs={{0,1},{1,0},{2,3},{3,2},{4,5},{5,4},{6,7},{7,6},{8,9},{9,8},{10,11... | collective-permute-start | bytes 491528 | tf_op jit(solution)/shard_map/ppermute | solution.py:281

commit v3 on v2

--- a/solution.py
+++ b/solution.py
@@ -6,6 +6,7 @@
 from jax.experimental import pallas as pl
 from jax.experimental.pallas import tpu as pltpu
 from jax.sharding import PartitionSpec as P
+
 
 F32 = jnp.float32
 BF16 = jnp.bfloat16
@@ -104,58 +105,69 @@
         copy.wait()
 
 
-def local_kernel(q, k, v, keep, send, part, rows_in, mine, theirs, outs, stats, sems, sems_out):
+def local_kernel(q, k, v, keep, send, part, mine, theirs, rest, outs, stats, sems_out):
     tp = lax.axis_index("tp")
-    arrive = head_copies((q, k, v), rows_in, sems)
     pending = []
     ok = iota((256, 256), 1) <= iota((256, 256), 0)
     for h in range(8):
-        arrive(h)
         o_ref, z_ref = outs.at[h % 4], stats.at[h % 4]
         for b in range(2):
             rows = slice(256 * b, 256 * b + 256)
             upto = slice(0, 256 * b + 256)
-            s = dot_t(rows_in[0, rows, head(h)], rows_in[1, upto, head(h)]) * SCALE
+            s = dot_t(q[rows, head(h)], k[upto, head(h)]) * SCALE
             last = jnp.where(ok, s[:, 256 * b :], NEG)
             s = last if b == 0 else jnp.concatenate([s[:, :256], last], axis=1)
-            o, z = attend(s, rows_in[2, upto, head(h)])
+            o, z = attend(s, v[upto, head(h)])
             o_ref[rows, :] = o
             z_ref[rows, :] = jnp.broadcast_to(z, (256, HD))
         for n in range(3):
             r = (h + n + 1) % 4
             mine[h, n] = o_ref[pl.ds(r + 256 * tp, 64, stride=4), :].astype(BF16)
             theirs[h, n] = o_ref[pl.ds(r + 256 * (1 - tp), 64, stride=4), :].astype(BF16)
-        for slot, (src, dst) in enumerate(((theirs, send), (mine, keep))):
+        rest[h, :, :HD] = o_ref[pl.ds(h % 4, 128, stride=4), :]
+        rest[h, :, HD:] = z_ref[pl.ds(h % 4, 128, stride=4), :]
+        for slot, (src, dst) in enumerate(((theirs, send), (mine, keep), (rest, part))):
             copy = pltpu.make_async_copy(src.at[h], dst.at[h], sems_out.at[slot, h])
             copy.start()
             pending.append(copy)
-        part[h, :, :HD] = o_ref[pl.ds(h % 4, 128, stride=4), :]
-        part[h, :, HD:] = z_ref[pl.ds(h % 4, 128, stride=4), :]
     for copy in pending:
         copy.wait()
 
 
-def near_kernel(q1, own, mate, far_a, far_b, part, keep, send, outs, stats):
+def near_kernel(
+    q1_in, own_in, part_in, mate, far_a, far_b, keep, send, q1, own, part, outs, stats, sems):
+    copies = [
+        pltpu.make_async_copy(*pair, sems.at[n])
+        for n, pair in enumerate(((q1_in, q1), (own_in, own), (part_in, part)))
+    ]
+    for copy in copies:
+        copy.start()
     tp = lax.axis_index("tp")
     c4 = lax.rem(lax.axis_index("ctx"), 4)
     row, col = iota((128, 512), 0), iota((128, 512), 1)
     start = jnp.where(c4 >= 2, 0, 256)
     stop = jnp.where(lax.rem(c4, 2) == 1, 384, 256)
     ok = ((col >= start) & (col < stop)) | ((col >= 384) & (col - 384 <= row))
-    for h in range(8):
-        o_ref, z_ref = outs.at[h % 4], stats.at[h % 4]
+    copies[0].wait()
+    copies[1].wait()
+    for h in range(8):
         keys = jnp.concatenate([far_a[0, h], far_b[0, h], mate[0, h], own[0, h]], axis=0)
         vals = jnp.concatenate([far_a[1, h], far_b[1, h], mate[1, h], own[1, h]], axis=0)
         s = dot_t(q1[h], keys) * SCALE
-        o1, z1 = attend(jnp.where(ok, s, NEG), vals)
-        o, z = merge(part[h, :, :HD], part[h, :, HD : HD + 1], o1, z1)
+        o, z = attend(jnp.where(ok, s, NEG), vals)
+        outs[h] = o
+        stats[h] = jnp.broadcast_to(z, (128, HD))
+    copies[2].wait()
+    for h in range(8):
+        o_ref, z_ref = outs.at[h], stats.at[h]
+        o, z = merge(part[h, :, :HD], part[h, :, HD:], o_ref[...], z_ref[...])
         o_ref[...] = o
-        z_ref[...] = jnp.broadcast_to(z, (128, HD))
+        z_ref[...] = z
         for ref, side in ((keep, tp), (send, 1 - tp)):
             base = pl.multiple_of(64 * side, 64)
             ref[h, :64] = o_ref[pl.ds(base, 64), :].astype(BF16)
             few = z_ref[pl.ds(64 * side + 2 * tp + h // 4, 16, stride=4), :]
-            ref[h, 64:80] = split3(few[:, 0:1])
+            ref[h, 64:80] = split3(few)
 
 
 def far_kernel(own, mate, line, g1, g2, g3, out, rows, sums, stats):
@@ -218,7 +230,7 @@
             out[:, cols] = buf[...].astype(BF16)
 
 
-def call(kernel, name, ins, outs, scratch):
+def call(kernel, ins, outs, scratch):
     vm, hbm = pl.BlockSpec(memory_space=VMEM), pl.BlockSpec(memory_space=pltpu.HBM)
     spaces = {"V": VMEM, "H": pltpu.HBM}
     args = [pltpu.with_memory_space_constraint(a, spaces[m]) if m else a for a, m in ins]
@@ -229,7 +241,6 @@
         out_specs=[hbm if m == "H" else vm for _, m in outs],
         scratch_shapes=scratch,
         compiler_params=pltpu.CompilerParams(vmem_limit_bytes=LIMIT),
-        name=name,
     )(*args)
 
 
@@ -248,46 +259,46 @@
     dma = pltpu.SemaphoreType.DMA
     args = [(queries, "H"), (key_rows, "H"), (value_rows, "H")]
     q1, kv1, x2 = call(
-        select_kernel, "select", args,
+        select_kernel, args,
         ((((8, 128, HD), BF16), "H"), (((2, 8, 128, HD), BF16), "H"), (((8, 112, HD), BF16), "H")),
         [VMEM((3, 512, 1024), BF16), VMEM((6, 512, HD), F32), VMEM((3, 8, 128, HD), BF16),
          VMEM((8, 112, HD), BF16), dma((3, 8)), dma((4, 8))])
     y2 = exchange(x2, "ctx", 8, n)
+    far_a = lax.ppermute(kv1, "ctx", [(i, i + 2) for i in range(n) if i % 4 < 2])
     mate = flip(kv1, 1)
-    far_a = flip(kv1, 2)
-
-    y2, queries, key_rows, value_rows = barrier((y2, queries, key_rows, value_rows))
+
+    keep, send, part = call(
+        local_kernel, [(a, "V") for a in (queries, key_rows, value_rows)],
+        ((((8, 3, 64, HD), BF16), "H"), (((8, 3, 64, HD), BF16), "H"), (((8, 128, 256), F32), "H")),
+        [VMEM((8, 3, 64, HD), BF16), VMEM((8, 3, 64, HD), BF16), VMEM((8, 128, 256), F32),
+         VMEM((4, 512, HD), F32), VMEM((4, 512, HD), F32), dma((3, 8))])
+    swap = [(0, 1), (1, 0)]
+    y2, part = barrier((y2, part))
     kv2 = y2[:, 32:112]
     kv3 = y2[:, 96:112]
     flips = [flip(kv2 if j == 1 else kv3, 8 * j) for j in (1, 2, 3)]
-
-    keep, send, part = call(
-        local_kernel, "local", [(queries, "H"), (key_rows, "H"), (value_rows, "H")],
-        ((((8, 3, 64, HD), BF16), "H"), (((8, 3, 64, HD), BF16), "H"), (((8, 128, 256), F32), "V")),
-        [VMEM((3, 512, 1024), BF16), VMEM((8, 3, 64, HD), BF16), VMEM((8, 3, 64, HD), BF16),
-         VMEM((4, 512, HD), F32), VMEM((4, 512, HD), F32), dma((3, 8)), dma((2, 8))])
-    swap = [(0, 1), (1, 0)]
     got = lax.ppermute(send, "tp", swap)
 
     line = jnp.stack([kv3, flips[0][:, 64:80], flips[1], flips[2]])
-    line, far_a, part = barrier((line, far_a, part))
     ahead = [flip(line, 32 * j) for j in (1, 2, 3)]
     far_b = flip(far_a, 1)
 
     keep1, send1 = call(
-        near_kernel, "near", [(a, "V") for a in (q1, kv1, mate, far_a, far_b, part)],
+        near_kernel,
+        [(a, "H") for a in (q1, kv1, part)] + [(a, "V") for a in (mate, far_a, far_b)],
         ((((8, 80, HD), BF16), None), (((8, 80, HD), BF16), None)),
-        [VMEM((4, 128, HD), F32), VMEM((4, 128, HD), F32)])
+        [VMEM((8, 128, HD), BF16), VMEM((2, 8, 128, HD), BF16), VMEM((8, 128, 256), F32),
+         VMEM((8, 128, HD), F32), VMEM((8, 128, HD), F32), dma((3,))])
     got1 = lax.ppermute(send1, "tp", swap)
 
     y2, keep1 = barrier((y2, keep1))
     (back,) = call(
-        far_kernel, "far", [(a, "V") for a in (y2, flips[0], line, *ahead)],
+        far_kernel, [(a, "V") for a in (y2, flips[0], line, *ahead)],
         ((((16, 16, 256), BF16), None),), [VMEM((256, HD), F32)] * 3)
     back = exchange(back, ("ctx", "tp"), 16, 2 * n)
 
     (out,) = call(
-        join_kernel, "join", [(a, "V") for a in (keep, keep1, got, got1, back)],
+        join_kernel, [(a, "V") for a in (keep, keep1, got, got1, back)],
         ((((256, 2048), BF16), None),), [VMEM((4, 256, HD), F32)])
     return out
 

time: 71.7 us -> 73.8 us (1.029)
  starting transfers between devices: 31.6 us -> 39.5 us
  waiting for transfers between devices: 20.7 us -> 14.7 us
    all_to_all x2, waiting for transfers between devices: 6.73 us -> 0.01 us  [exchange(): lax.all_to_all(value, axes, split_axis=0, concat_axis=0, tiled=True, axis...]
    ppermute x0 -> x1, starting transfers between devices: none -> 4.62 us  [local(): lax.ppermute(kv1, 'ctx', [(i, i + 2) for i in range(n) if i % 4 < 2])]
    all_to_all x2, starting transfers between devices: 9.43 us -> 11.4 us  [exchange(): lax.all_to_all(value, axes, split_axis=0, concat_axis=0, tiled=True, axis...]
    ppermute x9 -> x8, starting transfers between devices: 11.7 us -> 12.5 us  [flip(): return lax.ppermute(value, 'ctx', [(i, i ^ bits) for i in range(n)])]
    ppermute x9 -> x8, waiting for transfers between devices: 2.96 us -> 3.66 us  [flip(): return lax.ppermute(value, 'ctx', [(i, i ^ bits) for i in range(n)])]
where the time goes in v3:
time: 73.8 us; the launch traced here: 72.4 us
  starting transfers between devices  39.5 us (54%)
  Pallas kernels  18.1 us (25%)
  waiting for transfers between devices  14.7 us (20%)
    pallas_call x5, Pallas kernels, call(): pl.pallas_call(kernel, out_shape=[spaces[m](*o) if m else jax.ShapeDtypeS...  18.1 us
    ppermute x8, starting transfers between devices, flip(): return lax.ppermute(value, 'ctx', [(i, i ^ bits) for i in range(n)])  12.5 us
    all_to_all x2, starting transfers between devices, exchange(): lax.all_to_all(value, axes, split_axis=0, concat_axis=0, tiled=True, axis...  11.4 us
    ppermute x1, waiting for transfers between devices, local(): got1 = lax.ppermute(send1, 'tp', swap)  11 us
    ppermute x1, starting transfers between devices, local(): got1 = lax.ppermute(send1, 'tp', swap)  5.83 us
    ppermute x1, starting transfers between devices, local(): got = lax.ppermute(send, 'tp', swap)  5.18 us
    ppermute x1, starting transfers between devices, local(): lax.ppermute(kv1, 'ctx', [(i, i + 2) for i in range(n) if i % 4 < 2])  4.62 us
    ppermute x8, waiting for transfers between devices, flip(): return lax.ppermute(value, 'ctx', [(i, i ^ bits) for i in range(n)])  3.66 us
  transfers between devices with their start and end apart: 13, of which 3 were waited for; matrix products, arithmetic and copies ran while one was open for 0% of the time, Pallas kernels for 18%

profile of v3, /device:TPU:6, one launch (start us, length us, event | category | flops | bytes accessed | tf_op | source)
XLA Modules:
  0.0 72.4 jit_solution(4181283260066206353)
XLA Ops:
  0.0 0.0 copy-start.2
  0.0 0.0 copy-start.1
  0.0 0.0 copy-start
  0.0 3.7 %shard_map.38 = (bf16[8,128,128]{2,1,0:T(8,128)(2,1)}, bf16[2,8,128,128]{3,2,1,0:T(8,128)(2,1)}, bf16[8,112,128]{2,1,0:T(8,128)(2,1)}) custom-call(bf16[512,1024]{1,0:T(8,128)(2,1)} %q.3, bf16[512,1024]{1,0:T(8,128)(2,1)} %k.3, bf16[512,1024]{1,0:T(8,128)(2,1)} %v.3), custom_call_target="tpu_custom_call" | custom-call | tf_op jit(solution)/shard_map/pallas_call | solution.py:237
  3.7 4.6 %collective-permute-start.1 = (bf16[2,8,128,128]{3,2,1,0:T(8,128)(2,1)}, bf16[2,8,128,128]{3,2,1,0:T(8,128)(2,1)}, u32[]{:S(2)}, u32[]{:S(2)}) collective-permute-start(bf16[2,8,128,128]{3,2,1,0:T(8,128)(2,1)} %get-tuple-element.22.own_in), channel_id=1, source_target_pairs={{0,4},{2,6},{8,12},{10,14},{16,20},{18,22},{24,28},{26,30},{32,36}... | collective-permute-start | bytes 1572872 | tf_op jit(solution)/shard_map/ppermute | solution.py:267
  8.3 4.5 %all-to-all-start = ((bf16[8,112,128]{2,1,0:T(8,128)(2,1)}), bf16[8,112,128]{2,1,0:T(8,128)(2,1)S(1)}, u32[]{:S(2)}, u32[]{:S(2)}) async-start(bf16[8,112,128]{2,1,0:T(8,128)(2,1)} %get-tuple-element.18), calls=%async_computation | async-start | bytes 458752 | tf_op jit(solution)/shard_map/all_to_all | solution.py:252
  12.9 0.5 collective-permute-start
  13.4 0.0 copy-done.2
  13.4 0.0 copy-done.1
  13.4 0.0 copy-done
  13.4 6.2 %shard_map.37 = (bf16[8,3,64,128]{3,2,1,0:T(8,128)(2,1)}, bf16[8,3,64,128]{3,2,1,0:T(8,128)(2,1)}, f32[8,128,256]{2,1,0:T(8,128)}) custom-call(bf16[512,1024]{1,0:T(8,128)(2,1)S(1)} %copy-done, bf16[512,1024]{1,0:T(8,128)(2,1)S(1)} %copy-done.1, bf16[512,1024]{1,0:T(8,128)(2,1)S(1)} %copy-done.2), custom_call_target="tpu_custom_call" | custom-call | tf_op jit(solution)/shard_map/pallas_call | solution.py:237
  19.6 5.2 %collective-permute-start.3 = (bf16[8,3,64,128]{3,2,1,0:T(8,128)(2,1)}, bf16[8,3,64,128]{3,2,1,0:T(8,128)(2,1)S(1)}, u32[]{:S(2)}, u32[]{:S(2)}) collective-permute-start(bf16[8,3,64,128]{3,2,1,0:T(8,128)(2,1)} %get-tuple-element.26), channel_id=1, source_target_pairs={{0,1},{1,0},{2,3},{3,2},{4,5},{5,4},{6,7},{7,6},{8,9},{9,8},{10,11... | collective-permute-start | bytes 1179656 | tf_op jit(solution)/shard_map/ppermute | solution.py:280
  24.8 0.0 all-to-all-done.own
  24.8 1.7 %collective-permute-start.5 = (bf16[8,80,128]{2,1,0:T(8,128)(2,1)S(1)}, bf16[8,80,128]{2,1,0:T(8,128)(2,1)S(1)}, u32[]{:S(2)}, u32[]{:S(2)}) collective-permute-start(bf16[8,80,128]{2,1,0:T(8,128)(2,1)S(1)} %slice.9), channel_id=1, source_target_pairs={{0,16},{2,18},{4,20},{6,22},{8,24},{10,26},{12,28},{14,30},{16,0},... | collective-permute-start | bytes 491528 | tf_op jit(solution)/shard_map/ppermute | solution.py:256
  26.5 0.0 collective-permute-done.1.far_a
  26.5 0.0 collective-permute-start.2
  26.5 3.0 %collective-permute-start.6 = (bf16[8,16,128]{2,1,0:T(8,128)(2,1)S(1)}, bf16[8,16,128]{2,1,0:T(8,128)(2,1)S(1)}, u32[]{:S(2)}, u32[]{:S(2)}) collective-permute-start(bf16[8,16,128]{2,1,0:T(8,128)(2,1)S(1)} %get-tuple-element.30), channel_id=1, source_target_pairs={{0,32},{2,34},{4,36},{6,38},{8,40},{10,42},{12,44},{14,46},{16,48}... | collective-permute-start | bytes 98312 | tf_op jit(solution)/shard_map/ppermute | solution.py:256
  29.5 1.7 %collective-permute-done.5.mate = bf16[8,80,128]{2,1,0:T(8,128)(2,1)S(1)} collective-permute-done((bf16[8,80,128]{2,1,0:T(8,128)(2,1)S(1)}, bf16[8,80,128]{2,1,0:T(8,128)(2,1)S(1)}, u32[]{:S(2)}, u32[]{:S(2)}) %collective-permute-start.5) | collective-permute-done | bytes 163872 | tf_op jit(solution)/shard_map/ppermute | solution.py:256
  31.1 3.1 %collective-permute-start.7 = (bf16[8,16,128]{2,1,0:T(8,128)(2,1)S(1)}, bf16[8,16,128]{2,1,0:T(8,128)(2,1)S(1)}, u32[]{:S(2)}, u32[]{:S(2)}) collective-permute-start(bf16[8,16,128]{2,1,0:T(8,128)(2,1)S(1)} %get-tuple-element.30), channel_id=1, source_target_pairs={{0,48},{2,50},{4,52},{6,54},{8,56},{10,58},{12,60},{14,62},{16,32}... | collective-permute-start | bytes 98312 | tf_op jit(solution)/shard_map/ppermute | solution.py:256
  34.3 0.0 collective-permute-done.6
  34.3 2.0 %collective-permute-done.7 = bf16[8,16,128]{2,1,0:T(8,128)(2,1)S(1)} collective-permute-done((bf16[8,16,128]{2,1,0:T(8,128)(2,1)S(1)}, bf16[8,16,128]{2,1,0:T(8,128)(2,1)S(1)}, u32[]{:S(2)}, u32[]{:S(2)}) %collective-permute-start.7) | collective-permute-done | bytes 32800 | tf_op jit(solution)/shard_map/ppermute | solution.py:256
  36.3 0.6 collective-permute-start.10
  36.8 2.4 %collective-permute-start.9 = (bf16[4,8,16,128]{3,2,1,0:T(8,128)(2,1)S(1)}, bf16[4,8,16,128]{3,2,1,0:T(8,128)(2,1)S(1)}, u32[]{:S(2)}, u32[]{:S(2)}) collective-permute-start(bf16[4,8,16,128]{3,2,1,0:T(8,128)(2,1)S(1)} %pad_maximum_fusion.line), channel_id=1, source_target_pairs={{0,128},{2,130},{4,132},{6,134},{8,136},{10,138},{12,140},{14,142}... | collective-permute-start | bytes 393224 | tf_op jit(solution)/shard_map/ppermute | solution.py:256
  39.3 0.0 collective-permute-done.mate
  39.3 1.2 %collective-permute-start.8 = (bf16[4,8,16,128]{3,2,1,0:T(8,128)(2,1)S(1)}, bf16[4,8,16,128]{3,2,1,0:T(8,128)(2,1)S(1)}, u32[]{:S(2)}, u32[]{:S(2)}) collective-permute-start(bf16[4,8,16,128]{3,2,1,0:T(8,128)(2,1)S(1)} %pad_maximum_fusion.line), channel_id=1, source_target_pairs={{0,64},{2,66},{4,68},{6,70},{8,72},{10,74},{12,76},{14,78},{16,80}... | collective-permute-start | bytes 393224 | tf_op jit(solution)/shard_map/ppermute | solution.py:256
  40.5 0.0 collective-permute-done.2.far_b
  40.5 4.9 %shard_map.39 = (bf16[8,80,128]{2,1,0:T(8,128)(2,1)S(1)}, bf16[8,80,128]{2,1,0:T(8,128)(2,1)S(1)}) custom-call(bf16[8,128,128]{2,1,0:T(8,128)(2,1)} %get-tuple-element.21.q1_in, bf16[2,8,128,128]{3,2,1,0:T(8,128)(2,1)} %get-tuple-element.22.own_in, f32[8,128,256]{2,1,0:T(8,128)} %get-tuple-element.23.part_in, ...), custom_call_target="tpu_custom_call" | custom-call | tf_op jit(solution)/shard_map/pallas_call | solution.py:237
  45.4 0.0 collective-permute-done.10.g3
  45.4 0.0 collective-permute-done.9.g2
  45.4 0.0 collective-permute-done.8.g1
  45.5 0.0 copy-start.3
  45.5 1.6 %shard_map.40 = bf16[16,16,256]{2,1,0:T(8,128)(2,1)} custom-call(bf16[8,112,128]{2,1,0:T(8,128)(2,1)S(1)} %all-to-all-done.own, bf16[8,80,128]{2,1,0:T(8,128)(2,1)S(1)} %collective-permute-done.5.mate, bf16[4,8,16,128]{3,2,1,0:T(8,128)(2,1)S(1)} %pad_maximum_fusion.line, bf16[4,8,16,128]{3,2,1,0:T(8,128)(2,1)S(1)} %collective-permute-done.8.g1, ...), custom_call_target="tpu_custom_call" | custom-call | tf_op jit(solution)/shard_map/pallas_call | solution.py:237
  47.1 6.9 %all-to-all-start.1 = ((bf16[16,16,256]{2,1,0:T(8,128)(2,1)}), bf16[16,16,256]{2,1,0:T(8,128)(2,1)S(1)}, u32[]{:S(2)}, u32[]{:S(2)}) async-start(bf16[16,16,256]{2,1,0:T(8,128)(2,1)} %shard_map.40), calls=%async_computation.1 | async-start | bytes 262144 | tf_op jit(solution)/shard_map/all_to_all | solution.py:252
  54.0 5.8 %collective-permute-start.4 = (bf16[8,80,128]{2,1,0:T(8,128)(2,1)S(1)}, bf16[8,80,128]{2,1,0:T(8,128)(2,1)S(1)}, u32[]{:S(2)}, u32[]{:S(2)}) collective-permute-start(bf16[8,80,128]{2,1,0:T(8,128)(2,1)S(1)} %get-tuple-element.27), channel_id=1, source_target_pairs={{0,1},{1,0},{2,3},{3,2},{4,5},{5,4},{6,7},{7,6},{8,9},{9,8},{10,11... | collective-permute-start | bytes 491528 | tf_op jit(solution)/shard_map/ppermute | solution.py:292
  59.8 0.0 collective-permute-done.3.ra
  59.8 11.0 %collective-permute-done.4.rb = bf16[8,80,128]{2,1,0:T(8,128)(2,1)S(1)} collective-permute-done((bf16[8,80,128]{2,1,0:T(8,128)(2,1)S(1)}, bf16[8,80,128]{2,1,0:T(8,128)(2,1)S(1)}, u32[]{:S(2)}, u32[]{:S(2)}) %collective-permute-start.4) | collective-permute-done | bytes 163872 | tf_op jit(solution)/shard_map/ppermute | solution.py:292
  70.8 0.0 all-to-all-done.1.back
  70.8 0.0 copy-done.3
  70.8 1.6 %shard_map.41 = bf16[256,2048]{1,0:T(8,128)(2,1)} custom-call(bf16[8,3,64,128]{3,2,1,0:T(8,128)(2,1)S(1)} %copy-done.3, bf16[8,80,128]{2,1,0:T(8,128)(2,1)S(1)} %get-tuple-element.25.kb, bf16[8,3,64,128]{3,2,1,0:T(8,128)(2,1)S(1)} %collective-permute-done.3.ra, bf16[8,80,128]{2,1,0:T(8,128)(2,1)S(1)} %collective-permute-done.4.rb, ...), custom_call_target="tpu_custom_call" | custom-call | tf_op jit(solution)/shard_map/pallas_call | solution.py:237
  (4 shorter events, 0.0 us)
Async XLA Ops:
  0.0 13.4 %copy-start.2 = (bf16[512,1024]{1,0:T(8,128)(2,1)S(1)}, bf16[512,1024]{1,0:T(8,128)(2,1)}, u32[]{:S(2)}) copy-start(bf16[512,1024]{1,0:T(8,128)(2,1)} %v.3) | copy-start | bytes 3145732
  0.0 13.4 %copy-start.1 = (bf16[512,1024]{1,0:T(8,128)(2,1)S(1)}, bf16[512,1024]{1,0:T(8,128)(2,1)}, u32[]{:S(2)}) copy-start(bf16[512,1024]{1,0:T(8,128)(2,1)} %k.3) | copy-start | bytes 3145732
  0.0 13.4 %copy-start = (bf16[512,1024]{1,0:T(8,128)(2,1)S(1)}, bf16[512,1024]{1,0:T(8,128)(2,1)}, u32[]{:S(2)}) copy-start(bf16[512,1024]{1,0:T(8,128)(2,1)} %q.3) | copy-start | bytes 3145732
  3.7 22.8 %collective-permute-start.1 = (bf16[2,8,128,128]{3,2,1,0:T(8,128)(2,1)}, bf16[2,8,128,128]{3,2,1,0:T(8,128)(2,1)}, u32[]{:S(2)}, u32[]{:S(2)}) collective-permute-start(bf16[2,8,128,128]{3,2,1,0:T(8,128)(2,1)} %get-tuple-element.22.own_in), channel_id=1, source_target_pairs={{0,4},{2,6},{8,12},{10,14},{16,20},{18,22},{24,28},{26,30},{32,36}... | collective-permute-start | bytes 1572872 | tf_op jit(solution)/shard_map/ppermute | solution.py:267
  8.3 16.4 %all-to-all-start = ((bf16[8,112,128]{2,1,0:T(8,128)(2,1)}), bf16[8,112,128]{2,1,0:T(8,128)(2,1)S(1)}, u32[]{:S(2)}, u32[]{:S(2)}) async-start(bf16[8,112,128]{2,1,0:T(8,128)(2,1)} %get-tuple-element.18), calls=%async_computation | async-start | bytes 458752 | tf_op jit(solution)/shard_map/all_to_all | solution.py:252
  12.9 26.4 %collective-permute-start = (bf16[2,8,128,128]{3,2,1,0:T(8,128)(2,1)}, bf16[2,8,128,128]{3,2,1,0:T(8,128)(2,1)}, u32[]{:S(2)}, u32[]{:S(2)}) collective-permute-start(bf16[2,8,128,128]{3,2,1,0:T(8,128)(2,1)} %get-tuple-element.22.own_in), channel_id=1, source_target_pairs={{0,2},{2,0},{4,6},{6,4},{8,10},{10,8},{12,14},{14,12},{16,18},{18,... | collective-permute-start | bytes 1572872 | tf_op jit(solution)/shard_map/ppermute | solution.py:256
  19.6 40.2 %collective-permute-start.3 = (bf16[8,3,64,128]{3,2,1,0:T(8,128)(2,1)}, bf16[8,3,64,128]{3,2,1,0:T(8,128)(2,1)S(1)}, u32[]{:S(2)}, u32[]{:S(2)}) collective-permute-start(bf16[8,3,64,128]{3,2,1,0:T(8,128)(2,1)} %get-tuple-element.26), channel_id=1, source_target_pairs={{0,1},{1,0},{2,3},{3,2},{4,5},{5,4},{6,7},{7,6},{8,9},{9,8},{10,11... | collective-permute-start | bytes 1179656 | tf_op jit(solution)/shard_map/ppermute | solution.py:280
  24.8 6.3 %collective-permute-start.5 = (bf16[8,80,128]{2,1,0:T(8,128)(2,1)S(1)}, bf16[8,80,128]{2,1,0:T(8,128)(2,1)S(1)}, u32[]{:S(2)}, u32[]{:S(2)}) collective-permute-start(bf16[8,80,128]{2,1,0:T(8,128)(2,1)S(1)} %slice.9), channel_id=1, source_target_pairs={{0,16},{2,18},{4,20},{6,22},{8,24},{10,26},{12,28},{14,30},{16,0},... | collective-permute-start | bytes 491528 | tf_op jit(solution)/shard_map/ppermute | solution.py:256
  26.5 14.0 %collective-permute-start.2 = (bf16[2,8,128,128]{3,2,1,0:T(8,128)(2,1)}, bf16[2,8,128,128]{3,2,1,0:T(8,128)(2,1)S(1)}, u32[]{:S(2)}, u32[]{:S(2)}) collective-permute-start(bf16[2,8,128,128]{3,2,1,0:T(8,128)(2,1)} %collective-permute-done.1.far_a), channel_id=1, source_target_pairs={{0,2},{2,0},{4,6},{6,4},{8,10},{10,8},{12,14},{14,12},{16,18},{18,... | collective-permute-start | bytes 1572872 | tf_op jit(solution)/shard_map/ppermute | solution.py:256
  26.5 7.8 %collective-permute-start.6 = (bf16[8,16,128]{2,1,0:T(8,128)(2,1)S(1)}, bf16[8,16,128]{2,1,0:T(8,128)(2,1)S(1)}, u32[]{:S(2)}, u32[]{:S(2)}) collective-permute-start(bf16[8,16,128]{2,1,0:T(8,128)(2,1)S(1)} %get-tuple-element.30), channel_id=1, source_target_pairs={{0,32},{2,34},{4,36},{6,38},{8,40},{10,42},{12,44},{14,46},{16,48}... | collective-permute-start | bytes 98312 | tf_op jit(solution)/shard_map/ppermute | solution.py:256
  31.1 5.1 %collective-permute-start.7 = (bf16[8,16,128]{2,1,0:T(8,128)(2,1)S(1)}, bf16[8,16,128]{2,1,0:T(8,128)(2,1)S(1)}, u32[]{:S(2)}, u32[]{:S(2)}) collective-permute-start(bf16[8,16,128]{2,1,0:T(8,128)(2,1)S(1)} %get-tuple-element.30), channel_id=1, source_target_pairs={{0,48},{2,50},{4,52},{6,54},{8,56},{10,58},{12,60},{14,62},{16,32}... | collective-permute-start | bytes 98312 | tf_op jit(solution)/shard_map/ppermute | solution.py:256
  36.3 9.1 %collective-permute-start.10 = (bf16[4,8,16,128]{3,2,1,0:T(8,128)(2,1)S(1)}, bf16[4,8,16,128]{3,2,1,0:T(8,128)(2,1)S(1)}, u32[]{:S(2)}, u32[]{:S(2)}) collective-permute-start(bf16[4,8,16,128]{3,2,1,0:T(8,128)(2,1)S(1)} %pad_maximum_fusion.line), channel_id=1, source_target_pairs={{0,192},{2,194},{4,196},{6,198},{8,200},{10,202},{12,204},{14,206}... | collective-permute-start | bytes 393224 | tf_op jit(solution)/shard_map/ppermute | solution.py:256
  36.8 8.6 %collective-permute-start.9 = (bf16[4,8,16,128]{3,2,1,0:T(8,128)(2,1)S(1)}, bf16[4,8,16,128]{3,2,1,0:T(8,128)(2,1)S(1)}, u32[]{:S(2)}, u32[]{:S(2)}) collective-permute-start(bf16[4,8,16,128]{3,2,1,0:T(8,128)(2,1)S(1)} %pad_maximum_fusion.line), channel_id=1, source_target_pairs={{0,128},{2,130},{4,132},{6,134},{8,136},{10,138},{12,140},{14,142}... | collective-permute-start | bytes 393224 | tf_op jit(solution)/shard_map/ppermute | solution.py:256
  39.3 6.2 %collective-permute-start.8 = (bf16[4,8,16,128]{3,2,1,0:T(8,128)(2,1)S(1)}, bf16[4,8,16,128]{3,2,1,0:T(8,128)(2,1)S(1)}, u32[]{:S(2)}, u32[]{:S(2)}) collective-permute-start(bf16[4,8,16,128]{3,2,1,0:T(8,128)(2,1)S(1)} %pad_maximum_fusion.line), channel_id=1, source_target_pairs={{0,64},{2,66},{4,68},{6,70},{8,72},{10,74},{12,76},{14,78},{16,80}... | collective-permute-start | bytes 393224 | tf_op jit(solution)/shard_map/ppermute | solution.py:256
  45.5 25.3 %copy-start.3 = (bf16[8,3,64,128]{3,2,1,0:T(8,128)(2,1)S(1)}, bf16[8,3,64,128]{3,2,1,0:T(8,128)(2,1)}, u32[]{:S(2)}) copy-start(bf16[8,3,64,128]{3,2,1,0:T(8,128)(2,1)} %get-tuple-element.17.ka) | copy-start | bytes 1179652
  47.1 23.7 %all-to-all-start.1 = ((bf16[16,16,256]{2,1,0:T(8,128)(2,1)}), bf16[16,16,256]{2,1,0:T(8,128)(2,1)S(1)}, u32[]{:S(2)}, u32[]{:S(2)}) async-start(bf16[16,16,256]{2,1,0:T(8,128)(2,1)} %shard_map.40), calls=%async_computation.1 | async-start | bytes 262144 | tf_op jit(solution)/shard_map/all_to_all | solution.py:252
  54.0 16.8 %collective-permute-start.4 = (bf16[8,80,128]{2,1,0:T(8,128)(2,1)S(1)}, bf16[8,80,128]{2,1,0:T(8,128)(2,1)S(1)}, u32[]{:S(2)}, u32[]{:S(2)}) collective-permute-start(bf16[8,80,128]{2,1,0:T(8,128)(2,1)S(1)} %get-tuple-element.27), channel_id=1, source_target_pairs={{0,1},{1,0},{2,3},{3,2},{4,5},{5,4},{6,7},{7,6},{8,9},{9,8},{10,11... | collective-permute-start | bytes 491528 | tf_op jit(solution)/shard_map/ppermute | solution.py:292

commit v4 on v3

--- a/solution.py
+++ b/solution.py
@@ -32,28 +32,36 @@
 def attend(s, v):
     m = jnp.max(s, axis=1, keepdims=True)
     e = jnp.exp2(s - m)
-    l = jnp.sum(e, axis=1, keepdims=True)
-    return dot(e.astype(BF16), v) / l, m + jnp.log2(l)
-
-
-def merge(o0, z0, o1, z1):
-    top = jnp.maximum(z0, z1)
-    w0, w1 = jnp.exp2(z0 - top), jnp.exp2(z1 - top)
-    den = w0 + w1
-    return (w0 * o0 + w1 * o1) / den, top + jnp.log2(den)
-
-
-def split3(z):
+    return m, jnp.sum(e, axis=1, keepdims=True), dot(e.astype(BF16), v)
+
+
+def merge(m0, l0, a0, m1, l1, a1):
+    top = jnp.maximum(m0, m1)
+    w0, w1 = jnp.exp2(m0 - top), jnp.exp2(m1 - top)
+    return top, w0 * l0 + w1 * l1, w0 * a0 + w1 * a1
+
+
+def attend_whole(s, v):
+    m, l, a = attend(s, v)
+    return a / l, m + jnp.log2(l)
+
+
+def merge_whole(o0, z0, o1, z1):
+    top, den, num = merge(z0, 1.0, o0, z1, 1.0, o1)
+    return num / den, top + jnp.log2(den)
+
+
+def split3(z, start=0, rest=0.0):
     hi = z.astype(BF16).astype(F32)
     mid = (z - hi).astype(BF16).astype(F32)
-    lo = z - hi - mid
-    lane = iota((z.shape[0], HD), 1)
-    out = jnp.where(lane == 0, hi, jnp.where(lane == 1, mid, jnp.where(lane == 2, lo, 0.0)))
-    return out.astype(BF16)
-
-
-def join3(p):
-    return jnp.sum(p.astype(F32), axis=1, keepdims=True)
+    lane = iota((z.shape[0], HD), 1) - start
+    return jnp.where(
+        lane == 0, hi, jnp.where(lane == 1, mid, jnp.where(lane == 2, z - hi - mid, rest)))
+
+
+def join3(p, start=0):
+    lane = iota(p.shape, 1) - start
+    return jnp.sum(jnp.where((lane >= 0) & (lane < 3), p.astype(F32), 0.0), axis=1, keepdims=True)
 
 
 def head(h):
@@ -105,27 +113,29 @@
         copy.wait()
 
 
-def local_kernel(q, k, v, keep, send, part, mine, theirs, rest, outs, stats, sems_out):
+def local_kernel(qkv, keep, send, part, mine, theirs, rest, outs, tops, dens, sems_out):
     tp = lax.axis_index("tp")
     pending = []
     ok = iota((256, 256), 1) <= iota((256, 256), 0)
     for h in range(8):
-        o_ref, z_ref = outs.at[h % 4], stats.at[h % 4]
+        o_ref, m_ref, l_ref = outs.at[h % 4], tops.at[h % 4], dens.at[h % 4]
         for b in range(2):
             rows = slice(256 * b, 256 * b + 256)
             upto = slice(0, 256 * b + 256)
-            s = dot_t(q[rows, head(h)], k[upto, head(h)]) * SCALE
+            s = dot_t(qkv[0, rows, head(h)], qkv[1, upto, head(h)]) * SCALE
             last = jnp.where(ok, s[:, 256 * b :], NEG)
             s = last if b == 0 else jnp.concatenate([s[:, :256], last], axis=1)
-            o, z = attend(s, v[upto, head(h)])
-            o_ref[rows, :] = o
-            z_ref[rows, :] = jnp.broadcast_to(z, (256, HD))
+            m, l, a = attend(s, qkv[2, upto, head(h)])
+            o_ref[rows, :] = a / l
+            m_ref[rows, :] = jnp.broadcast_to(m, (256, HD))
+            l_ref[rows, :] = jnp.broadcast_to(l, (256, HD))
         for n in range(3):
             r = (h + n + 1) % 4
             mine[h, n] = o_ref[pl.ds(r + 256 * tp, 64, stride=4), :].astype(BF16)
             theirs[h, n] = o_ref[pl.ds(r + 256 * (1 - tp), 64, stride=4), :].astype(BF16)
-        rest[h, :, :HD] = o_ref[pl.ds(h % 4, 128, stride=4), :]
-        rest[h, :, HD:] = z_ref[pl.ds(h % 4, 128, stride=4), :]
+        pick = pl.ds(h % 4, 128, stride=4)
+        rest[h, :, :HD] = o_ref[pick, :]
+        rest[h, :, HD:] = m_ref[pick, :] + jnp.log2(l_ref[pick, :])
         for slot, (src, dst) in enumerate(((theirs, send), (mine, keep), (rest, part))):
             copy = pltpu.make_async_copy(src.at[h], dst.at[h], sems_out.at[slot, h])
             copy.start()
@@ -134,40 +144,49 @@
         copy.wait()
 
 
-def near_kernel(
-    q1_in, own_in, part_in, mate, far_a, far_b, keep, send, q1, own, part, outs, stats, sems):
-    copies = [
-        pltpu.make_async_copy(*pair, sems.at[n])
-        for n, pair in enumerate(((q1_in, q1), (own_in, own), (part_in, part)))
-    ]
+def fetch_kernel(*refs):
+    half = (len(refs) - 1) // 2
+    sems = refs[-1]
+    copies = []
+    for n in range(half):
+        for h in range(2):
+            part = pl.ds(h * (refs[n].shape[0] // 2), refs[n].shape[0] // 2)
+            copies.append(
+                pltpu.make_async_copy(refs[n].at[part], refs[half + n].at[part], sems.at[n, h]))
     for copy in copies:
         copy.start()
+    for copy in copies:
+        copy.wait()
+
+
+def near_kernel(q1, own, part, mate, far_a, far_b, keep, send, outs, tops, dens):
     tp = lax.axis_index("tp")
     c4 = lax.rem(lax.axis_index("ctx"), 4)
     row, col = iota((128, 512), 0), iota((128, 512), 1)
     start = jnp.where(c4 >= 2, 0, 256)
     stop = jnp.where(lax.rem(c4, 2) == 1, 384, 256)
     ok = ((col >= start) & (col < stop)) | ((col >= 384) & (col - 384 <= row))
-    copies[0].wait()
-    copies[1].wait()
     for h in range(8):
         keys = jnp.concatenate([far_a[0, h], far_b[0, h], mate[0, h], own[0, h]], axis=0)
         vals = jnp.concatenate([far_a[1, h], far_b[1, h], mate[1, h], own[1, h]], axis=0)
-        s = dot_t(q1[h], keys) * SCALE
-        o, z = attend(jnp.where(ok, s, NEG), vals)
-        outs[h] = o
-        stats[h] = jnp.broadcast_to(z, (128, HD))
-    copies[2].wait()
-    for h in range(8):
-        o_ref, z_ref = outs.at[h], stats.at[h]
-        o, z = merge(part[h, :, :HD], part[h, :, HD:], o_ref[...], z_ref[...])
-        o_ref[...] = o
-        z_ref[...] = z
-        for ref, side in ((keep, tp), (send, 1 - tp)):
+        m, l, a = attend(jnp.where(ok, dot_t(q1[h], keys) * SCALE, NEG), vals)
+        outs[h] = a
+        tops[h] = jnp.broadcast_to(m, (128, HD))
+        dens[h] = jnp.broadcast_to(l, (128, HD))
+    terms = [jnp.zeros((16, HD), F32)] * 2
+    for h in range(8):
+        top, den, num = merge(part[h, :, HD:], 1.0, part[h, :, :HD], tops[h], dens[h], outs[h])
+        outs[h] = num / den
+        tops[h] = top
+        dens[h] = den
+        for n, (ref, side) in enumerate(((keep, tp), (send, 1 - tp))):
             base = pl.multiple_of(64 * side, 64)
-            ref[h, :64] = o_ref[pl.ds(base, 64), :].astype(BF16)
-            few = z_ref[pl.ds(64 * side + 2 * tp + h // 4, 16, stride=4), :]
-            ref[h, 64:80] = split3(few)
+            ref[64 * h : 64 * h + 64] = outs[h, pl.ds(base, 64), :].astype(BF16)
+            pick = pl.ds(64 * side + 2 * tp + h // 4, 16, stride=4)
+            few = tops[h, pick, :] + jnp.log2(dens[h, pick, :])
+            terms[n] = split3(few, 3 * h, terms[n])
+    for ref, value in zip((keep, send), terms):
+        ref[512:528] = value.astype(BF16)
 
 
 def far_kernel(own, mate, line, g1, g2, g3, out, rows, sums, stats):
@@ -183,7 +202,7 @@
     s = dot_t(rows[...].astype(BF16), keys) * SCALE
     row, col = iota(s.shape, 0), iota(s.shape, 1)
     ok = ((col < 256) & (lax.rem(y, 2) == 1)) | ((col >= 256) & (col - 256 <= row))
-    o2, z2 = attend(jnp.where(ok, s, NEG), vals)
+    o2, z2 = attend_whole(jnp.where(ok, s, NEG), vals)
     sums[...] = o2
     stats[...] = jnp.broadcast_to(z2, (256, HD))
 
@@ -202,14 +221,14 @@
     earlier_x = (slot < 12) & (jnp.bitwise_xor(lax.shift_right_logical(slot, 2) + 1, x) < x)
     earlier_y = (slot > 12) & (jnp.bitwise_xor(slot - 12, y) < y)
     mine = (slot == 12) & (col - 768 <= row)
-    o3, z3 = attend(jnp.where(earlier_x | earlier_y | mine, s, NEG), vals)
+    o3, z3 = attend_whole(jnp.where(earlier_x | earlier_y | mine, s, NEG), vals)
     pick = pl.ds(0, 64, stride=4)
-    o, z = merge(sums[pick, :], stats[pick, :][:, 0:1], o3, z3)
+    o, z = merge_whole(sums[pick, :], stats[pick, :][:, 0:1], o3, z3)
     sums[pick, :] = o
     stats[pick, :] = jnp.broadcast_to(z, (64, HD))
     for j in range(16):
         out[j, :, :HD] = sums[16 * j : 16 * j + 16, :].astype(BF16)
-        out[j, :, HD:] = split3(stats[16 * j : 16 * j + 16, :][:, 0:1])
+        out[j, :, HD:] = split3(stats[16 * j : 16 * j + 16, :]).astype(BF16)
 
 
 def join_kernel(ka, kb, ra, rb, back, out, wide):
@@ -220,12 +239,13 @@
             buf = wide.at[(2 * h + side) % 4]
             for n in range(3):
                 buf[pl.ds((h + n + 1) % 4, 64, stride=4), :] = first[h, n].astype(F32)
-            buf[pl.ds(h % 4, 64, stride=4), :] = second[h, :64].astype(F32)
+            buf[pl.ds(h % 4, 64, stride=4), :] = second[64 * h : 64 * h + 64].astype(F32)
             pick = pl.ds(8 * src + h, 16, stride=16)
             more = back[2 * h + src]
-            o, _ = merge(
-                buf[pick, :], join3(second[h, 64:80]), more[:, :HD].astype(F32), join3(more[:, HD:]))
-            buf[pick, :] = o
+            _, den, num = merge(
+                join3(second[512:528], 3 * h), 1.0, buf[pick, :],
+                join3(more[:, HD:]), 1.0, more[:, :HD].astype(F32))
+            buf[pick, :] = num / den
             cols = pl.ds(pl.multiple_of(src * 1024 + h * HD, HD), HD)
             out[:, cols] = buf[...].astype(BF16)
 
@@ -258,20 +278,21 @@
     barrier = lax.optimization_barrier
     dma = pltpu.SemaphoreType.DMA
     args = [(queries, "H"), (key_rows, "H"), (value_rows, "H")]
-    q1, kv1, x2 = call(
+    q1, kv1, x2, rows = call(
         select_kernel, args,
-        ((((8, 128, HD), BF16), "H"), (((2, 8, 128, HD), BF16), "H"), (((8, 112, HD), BF16), "H")),
-        [VMEM((3, 512, 1024), BF16), VMEM((6, 512, HD), F32), VMEM((3, 8, 128, HD), BF16),
+        ((((8, 128, HD), BF16), "H"), (((2, 8, 128, HD), BF16), "H"), (((8, 112, HD), BF16), "H"),
+         (((3, 512, 1024), BF16), "V")),
+        [VMEM((6, 512, HD), F32), VMEM((3, 8, 128, HD), BF16),
          VMEM((8, 112, HD), BF16), dma((3, 8)), dma((4, 8))])
     y2 = exchange(x2, "ctx", 8, n)
     far_a = lax.ppermute(kv1, "ctx", [(i, i + 2) for i in range(n) if i % 4 < 2])
     mate = flip(kv1, 1)
 
     keep, send, part = call(
-        local_kernel, [(a, "V") for a in (queries, key_rows, value_rows)],
+        local_kernel, [(rows, "V")],
         ((((8, 3, 64, HD), BF16), "H"), (((8, 3, 64, HD), BF16), "H"), (((8, 128, 256), F32), "H")),
-        [VMEM((8, 3, 64, HD), BF16), VMEM((8, 3, 64, HD), BF16), VMEM((8, 128, 256), F32),
-         VMEM((4, 512, HD), F32), VMEM((4, 512, HD), F32), dma((3, 8))])
+        [VMEM((8, 3, 64, HD), BF16), VMEM((8, 3, 64, HD), BF16), VMEM((8, 128, 256), F32)]
+        + [VMEM((4, 512, HD), F32)] * 3 + [dma((3, 8))])
     swap = [(0, 1), (1, 0)]
     y2, part = barrier((y2, part))
     kv2 = y2[:, 32:112]
@@ -283,12 +304,13 @@
     ahead = [flip(line, 32 * j) for j in (1, 2, 3)]
     far_b = flip(far_a, 1)
 
+    held = call(
+        fetch_kernel, [(a, "H") for a in (q1, kv1, part)],
+        [((a.shape, a.dtype), "V") for a in (q1, kv1, part)], [dma((3, 2))])
     keep1, send1 = call(
-        near_kernel,
-        [(a, "H") for a in (q1, kv1, part)] + [(a, "V") for a in (mate, far_a, far_b)],
-        ((((8, 80, HD), BF16), None), (((8, 80, HD), BF16), None)),
-        [VMEM((8, 128, HD), BF16), VMEM((2, 8, 128, HD), BF16), VMEM((8, 128, 256), F32),
-         VMEM((8, 128, HD), F32), VMEM((8, 128, HD), F32), dma((3,))])
+        near_kernel, [(a, "V") for a in (*held, mate, far_a, far_b)],
+        ((((528, HD), BF16), None), (((528, HD), BF16), None)),
+        [VMEM((8, 128, HD), F32)] * 3)
     got1 = lax.ppermute(send1, "tp", swap)
 
     y2, keep1 = barrier((y2, keep1))

time: 73.8 us -> 72.4 us (0.981)
  waiting for transfers between devices: 14.7 us -> 13.4 us
    ppermute x1, waiting for transfers between devices: 11 us -> 9.76 us  [local(): got1 = lax.ppermute(send1, 'tp', swap)]
    pallas_call x5 -> x6, Pallas kernels: 18.1 us -> 18.1 us  [call(): pl.pallas_call(kernel, out_shape=[spaces[m](*o) if m else jax.ShapeDtypeS...]
where the time goes in v4:
time: 72.4 us; the launch traced here: 71.3 us
  starting transfers between devices  39.7 us (55%)
  Pallas kernels  18.1 us (25%)
  waiting for transfers between devices  13.4 us (19%)
    pallas_call x6, Pallas kernels, call(): pl.pallas_call(kernel, out_shape=[spaces[m](*o) if m else jax.ShapeDtypeS...  18.1 us
    ppermute x8, starting transfers between devices, flip(): return lax.ppermute(value, 'ctx', [(i, i ^ bits) for i in range(n)])  12.5 us
    all_to_all x2, starting transfers between devices, exchange(): lax.all_to_all(value, axes, split_axis=0, concat_axis=0, tiled=True, axis...  11.5 us
    ppermute x1, waiting for transfers between devices, local(): got1 = lax.ppermute(send1, 'tp', swap)  9.76 us
    ppermute x1, starting transfers between devices, local(): got1 = lax.ppermute(send1, 'tp', swap)  5.83 us
    ppermute x1, starting transfers between devices, local(): got = lax.ppermute(send, 'tp', swap)  5.15 us
    ppermute x1, starting transfers between devices, local(): lax.ppermute(kv1, 'ctx', [(i, i + 2) for i in range(n) if i % 4 < 2])  4.64 us
    ppermute x8, waiting for transfers between devices, flip(): return lax.ppermute(value, 'ctx', [(i, i ^ bits) for i in range(n)])  3.58 us
  transfers between devices with their start and end apart: 13, of which 3 were waited for; matrix products, arithmetic and copies ran while one was open for 0% of the time, Pallas kernels for 18%

profile of v4, /device:TPU:6, one launch (start us, length us, event | category | flops | bytes accessed | tf_op | source)
XLA Modules:
  0.0 71.3 jit_solution(3999240679626389461)
XLA Ops:
  0.0 3.5 %shard_map.37 = (bf16[8,128,128]{2,1,0:T(8,128)(2,1)}, bf16[2,8,128,128]{3,2,1,0:T(8,128)(2,1)}, bf16[8,112,128]{2,1,0:T(8,128)(2,1)}, bf16[3,512,1024]{2,1,0:T(8,128)(2,1)S(1)}) custom-call(bf16[512,1024]{1,0:T(8,128)(2,1)} %q.1, bf16[512,1024]{1,0:T(8,128)(2,1)} %k.1, bf16[512,1024]{1,0:T(8,128)(2,1)} %v.1), custom_call_target="tpu_custom_call" | custom-call | tf_op jit(solution)/shard_map/pallas_call | solution.py:257
  3.6 4.6 %collective-permute-start.1 = (bf16[2,8,128,128]{3,2,1,0:T(8,128)(2,1)}, bf16[2,8,128,128]{3,2,1,0:T(8,128)(2,1)}, u32[]{:S(2)}, u32[]{:S(2)}) collective-permute-start(bf16[2,8,128,128]{3,2,1,0:T(8,128)(2,1)} %get-tuple-element.27.refs_1_), channel_id=1, source_target_pairs={{0,4},{2,6},{8,12},{10,14},{16,20},{18,22},{24,28},{26,30},{32,36}... | collective-permute-start | bytes 1572872 | tf_op jit(solution)/shard_map/ppermute | solution.py:288
  8.2 4.5 %all-to-all-start = ((bf16[8,112,128]{2,1,0:T(8,128)(2,1)}), bf16[8,112,128]{2,1,0:T(8,128)(2,1)S(1)}, u32[]{:S(2)}, u32[]{:S(2)}) async-start(bf16[8,112,128]{2,1,0:T(8,128)(2,1)} %get-tuple-element.23), calls=%async_computation | async-start | bytes 458752 | tf_op jit(solution)/shard_map/all_to_all | solution.py:272
  12.8 0.5 collective-permute-start
  13.3 6.1 %shard_map.38 = (bf16[8,3,64,128]{3,2,1,0:T(8,128)(2,1)}, bf16[8,3,64,128]{3,2,1,0:T(8,128)(2,1)}, f32[8,128,256]{2,1,0:T(8,128)}) custom-call(bf16[3,512,1024]{2,1,0:T(8,128)(2,1)S(1)} %get-tuple-element.21.qkv), custom_call_target="tpu_custom_call" | custom-call | tf_op jit(solution)/shard_map/pallas_call | solution.py:257
  19.4 5.2 %collective-permute-start.3 = (bf16[8,3,64,128]{3,2,1,0:T(8,128)(2,1)}, bf16[8,3,64,128]{3,2,1,0:T(8,128)(2,1)S(1)}, u32[]{:S(2)}, u32[]{:S(2)}) collective-permute-start(bf16[8,3,64,128]{3,2,1,0:T(8,128)(2,1)} %get-tuple-element.34), channel_id=1, source_target_pairs={{0,1},{1,0},{2,3},{3,2},{4,5},{5,4},{6,7},{7,6},{8,9},{9,8},{10,11... | collective-permute-start | bytes 1179656 | tf_op jit(solution)/shard_map/ppermute | solution.py:301
  24.6 0.0 all-to-all-done.own
  24.6 1.7 %collective-permute-start.5 = (bf16[8,80,128]{2,1,0:T(8,128)(2,1)S(1)}, bf16[8,80,128]{2,1,0:T(8,128)(2,1)S(1)}, u32[]{:S(2)}, u32[]{:S(2)}) collective-permute-start(bf16[8,80,128]{2,1,0:T(8,128)(2,1)S(1)} %slice.9), channel_id=1, source_target_pairs={{0,16},{2,18},{4,20},{6,22},{8,24},{10,26},{12,28},{14,30},{16,0},... | collective-permute-start | bytes 491528 | tf_op jit(solution)/shard_map/ppermute | solution.py:276
  26.2 0.0 collective-permute-done.1.far_a
  26.2 0.0 collective-permute-start.2
  26.3 3.0 %collective-permute-start.6 = (bf16[8,16,128]{2,1,0:T(8,128)(2,1)S(1)}, bf16[8,16,128]{2,1,0:T(8,128)(2,1)S(1)}, u32[]{:S(2)}, u32[]{:S(2)}) collective-permute-start(bf16[8,16,128]{2,1,0:T(8,128)(2,1)S(1)} %get-tuple-element.38), channel_id=1, source_target_pairs={{0,32},{2,34},{4,36},{6,38},{8,40},{10,42},{12,44},{14,46},{16,48}... | collective-permute-start | bytes 98312 | tf_op jit(solution)/shard_map/ppermute | solution.py:276
  29.3 1.6 %collective-permute-done.5.mate = bf16[8,80,128]{2,1,0:T(8,128)(2,1)S(1)} collective-permute-done((bf16[8,80,128]{2,1,0:T(8,128)(2,1)S(1)}, bf16[8,80,128]{2,1,0:T(8,128)(2,1)S(1)}, u32[]{:S(2)}, u32[]{:S(2)}) %collective-permute-start.5) | collective-permute-done | bytes 163872 | tf_op jit(solution)/shard_map/ppermute | solution.py:276
  30.9 3.2 %collective-permute-start.7 = (bf16[8,16,128]{2,1,0:T(8,128)(2,1)S(1)}, bf16[8,16,128]{2,1,0:T(8,128)(2,1)S(1)}, u32[]{:S(2)}, u32[]{:S(2)}) collective-permute-start(bf16[8,16,128]{2,1,0:T(8,128)(2,1)S(1)} %get-tuple-element.38), channel_id=1, source_target_pairs={{0,48},{2,50},{4,52},{6,54},{8,56},{10,58},{12,60},{14,62},{16,32}... | collective-permute-start | bytes 98312 | tf_op jit(solution)/shard_map/ppermute | solution.py:276
  34.1 0.0 collective-permute-done.6
  34.1 1.9 %collective-permute-done.7 = bf16[8,16,128]{2,1,0:T(8,128)(2,1)S(1)} collective-permute-done((bf16[8,16,128]{2,1,0:T(8,128)(2,1)S(1)}, bf16[8,16,128]{2,1,0:T(8,128)(2,1)S(1)}, u32[]{:S(2)}, u32[]{:S(2)}) %collective-permute-start.7) | collective-permute-done | bytes 32800 | tf_op jit(solution)/shard_map/ppermute | solution.py:276
  36.0 0.6 collective-permute-start.10
  36.6 2.4 %collective-permute-start.9 = (bf16[4,8,16,128]{3,2,1,0:T(8,128)(2,1)S(1)}, bf16[4,8,16,128]{3,2,1,0:T(8,128)(2,1)S(1)}, u32[]{:S(2)}, u32[]{:S(2)}) collective-permute-start(bf16[4,8,16,128]{3,2,1,0:T(8,128)(2,1)S(1)} %pad_maximum_fusion.line), channel_id=1, source_target_pairs={{0,128},{2,130},{4,132},{6,134},{8,136},{10,138},{12,140},{14,142}... | collective-permute-start | bytes 393224 | tf_op jit(solution)/shard_map/ppermute | solution.py:276
  39.0 0.0 collective-permute-done.mate
  39.0 1.2 %collective-permute-start.8 = (bf16[4,8,16,128]{3,2,1,0:T(8,128)(2,1)S(1)}, bf16[4,8,16,128]{3,2,1,0:T(8,128)(2,1)S(1)}, u32[]{:S(2)}, u32[]{:S(2)}) collective-permute-start(bf16[4,8,16,128]{3,2,1,0:T(8,128)(2,1)S(1)} %pad_maximum_fusion.line), channel_id=1, source_target_pairs={{0,64},{2,66},{4,68},{6,70},{8,72},{10,74},{12,76},{14,78},{16,80}... | collective-permute-start | bytes 393224 | tf_op jit(solution)/shard_map/ppermute | solution.py:276
  40.2 0.0 copy-start
  40.2 1.6 %shard_map.39 = (bf16[8,128,128]{2,1,0:T(8,128)(2,1)S(1)}, bf16[2,8,128,128]{3,2,1,0:T(8,128)(2,1)S(1)}, f32[8,128,256]{2,1,0:T(8,128)S(1)}) custom-call(bf16[8,128,128]{2,1,0:T(8,128)(2,1)} %get-tuple-element.26.refs_0_, bf16[2,8,128,128]{3,2,1,0:T(8,128)(2,1)} %get-tuple-element.27.refs_1_, f32[8,128,256]{2,1,0:T(8,128)} %get-tuple-element.28.refs_2_), custom_call_target="tpu_custom_call" | custom-call | tf_op jit(solution)/shard_map/pallas_call | solution.py:257
  41.8 0.0 collective-permute-done.2.far_b
  41.8 3.7 %shard_map.40 = (bf16[528,128]{1,0:T(8,128)(2,1)S(1)}, bf16[528,128]{1,0:T(8,128)(2,1)S(1)}) custom-call(bf16[8,128,128]{2,1,0:T(8,128)(2,1)S(1)} %get-tuple-element.29.q1, bf16[2,8,128,128]{3,2,1,0:T(8,128)(2,1)S(1)} %get-tuple-element.30.own, f32[8,128,256]{2,1,0:T(8,128)S(1)} %get-tuple-element.31.part, ...), custom_call_target="tpu_custom_call" | custom-call | tf_op jit(solution)/shard_map/pallas_call | solution.py:257
  45.5 0.0 collective-permute-done.10.g3
  45.5 0.0 collective-permute-done.9.g2
  45.5 0.0 collective-permute-done.8.g1
  45.5 1.5 %shard_map.41 = bf16[16,16,256]{2,1,0:T(8,128)(2,1)} custom-call(bf16[8,112,128]{2,1,0:T(8,128)(2,1)S(1)} %all-to-all-done.own, bf16[8,80,128]{2,1,0:T(8,128)(2,1)S(1)} %collective-permute-done.5.mate, bf16[4,8,16,128]{3,2,1,0:T(8,128)(2,1)S(1)} %pad_maximum_fusion.line, bf16[4,8,16,128]{3,2,1,0:T(8,128)(2,1)S(1)} %collective-permute-done.8.g1, ...), custom_call_target="tpu_custom_call" | custom-call | tf_op jit(solution)/shard_map/pallas_call | solution.py:257
  47.0 7.0 %all-to-all-start.1 = ((bf16[16,16,256]{2,1,0:T(8,128)(2,1)}), bf16[16,16,256]{2,1,0:T(8,128)(2,1)S(1)}, u32[]{:S(2)}, u32[]{:S(2)}) async-start(bf16[16,16,256]{2,1,0:T(8,128)(2,1)} %shard_map.41), calls=%async_computation.1 | async-start | bytes 262144 | tf_op jit(solution)/shard_map/all_to_all | solution.py:272
  54.0 5.8 %collective-permute-start.4 = (bf16[528,128]{1,0:T(8,128)(2,1)S(1)}, bf16[528,128]{1,0:T(8,128)(2,1)S(1)}, u32[]{:S(2)}, u32[]{:S(2)}) collective-permute-start(bf16[528,128]{1,0:T(8,128)(2,1)S(1)} %get-tuple-element.35), channel_id=1, source_target_pairs={{0,1},{1,0},{2,3},{3,2},{4,5},{5,4},{6,7},{7,6},{8,9},{9,8},{10,11... | collective-permute-start | bytes 405512 | tf_op jit(solution)/shard_map/ppermute | solution.py:314
  59.9 0.0 collective-permute-done.3.ra
  59.9 9.8 %collective-permute-done.4.rb = bf16[528,128]{1,0:T(8,128)(2,1)S(1)} collective-permute-done((bf16[528,128]{1,0:T(8,128)(2,1)S(1)}, bf16[528,128]{1,0:T(8,128)(2,1)S(1)}, u32[]{:S(2)}, u32[]{:S(2)}) %collective-permute-start.4) | collective-permute-done | bytes 135200 | tf_op jit(solution)/shard_map/ppermute | solution.py:314
  69.6 0.0 all-to-all-done.1.back
  69.6 0.0 copy-done
  69.6 1.6 %shard_map.42 = bf16[256,2048]{1,0:T(8,128)(2,1)} custom-call(bf16[8,3,64,128]{3,2,1,0:T(8,128)(2,1)S(1)} %copy-done, bf16[528,128]{1,0:T(8,128)(2,1)S(1)} %get-tuple-element.33.kb, bf16[8,3,64,128]{3,2,1,0:T(8,128)(2,1)S(1)} %collective-permute-done.3.ra, bf16[528,128]{1,0:T(8,128)(2,1)S(1)} %collective-permute-done.4.rb, ...), custom_call_target="tpu_custom_call" | custom-call | tf_op jit(solution)/shard_map/pallas_call | solution.py:257
  (4 shorter events, 0.0 us)
Async XLA Ops:
  3.6 22.7 %collective-permute-start.1 = (bf16[2,8,128,128]{3,2,1,0:T(8,128)(2,1)}, bf16[2,8,128,128]{3,2,1,0:T(8,128)(2,1)}, u32[]{:S(2)}, u32[]{:S(2)}) collective-permute-start(bf16[2,8,128,128]{3,2,1,0:T(8,128)(2,1)} %get-tuple-element.27.refs_1_), channel_id=1, source_target_pairs={{0,4},{2,6},{8,12},{10,14},{16,20},{18,22},{24,28},{26,30},{32,36}... | collective-permute-start | bytes 1572872 | tf_op jit(solution)/shard_map/ppermute | solution.py:288
  8.2 16.4 %all-to-all-start = ((bf16[8,112,128]{2,1,0:T(8,128)(2,1)}), bf16[8,112,128]{2,1,0:T(8,128)(2,1)S(1)}, u32[]{:S(2)}, u32[]{:S(2)}) async-start(bf16[8,112,128]{2,1,0:T(8,128)(2,1)} %get-tuple-element.23), calls=%async_computation | async-start | bytes 458752 | tf_op jit(solution)/shard_map/all_to_all | solution.py:272
  12.8 26.3 %collective-permute-start = (bf16[2,8,128,128]{3,2,1,0:T(8,128)(2,1)}, bf16[2,8,128,128]{3,2,1,0:T(8,128)(2,1)}, u32[]{:S(2)}, u32[]{:S(2)}) collective-permute-start(bf16[2,8,128,128]{3,2,1,0:T(8,128)(2,1)} %get-tuple-element.27.refs_1_), channel_id=1, source_target_pairs={{0,2},{2,0},{4,6},{6,4},{8,10},{10,8},{12,14},{14,12},{16,18},{18,... | collective-permute-start | bytes 1572872 | tf_op jit(solution)/shard_map/ppermute | solution.py:276
  19.4 40.5 %collective-permute-start.3 = (bf16[8,3,64,128]{3,2,1,0:T(8,128)(2,1)}, bf16[8,3,64,128]{3,2,1,0:T(8,128)(2,1)S(1)}, u32[]{:S(2)}, u32[]{:S(2)}) collective-permute-start(bf16[8,3,64,128]{3,2,1,0:T(8,128)(2,1)} %get-tuple-element.34), channel_id=1, source_target_pairs={{0,1},{1,0},{2,3},{3,2},{4,5},{5,4},{6,7},{7,6},{8,9},{9,8},{10,11... | collective-permute-start | bytes 1179656 | tf_op jit(solution)/shard_map/ppermute | solution.py:301
  24.6 6.3 %collective-permute-start.5 = (bf16[8,80,128]{2,1,0:T(8,128)(2,1)S(1)}, bf16[8,80,128]{2,1,0:T(8,128)(2,1)S(1)}, u32[]{:S(2)}, u32[]{:S(2)}) collective-permute-start(bf16[8,80,128]{2,1,0:T(8,128)(2,1)S(1)} %slice.9), channel_id=1, source_target_pairs={{0,16},{2,18},{4,20},{6,22},{8,24},{10,26},{12,28},{14,30},{16,0},... | collective-permute-start | bytes 491528 | tf_op jit(solution)/shard_map/ppermute | solution.py:276
  26.2 15.6 %collective-permute-start.2 = (bf16[2,8,128,128]{3,2,1,0:T(8,128)(2,1)}, bf16[2,8,128,128]{3,2,1,0:T(8,128)(2,1)S(1)}, u32[]{:S(2)}, u32[]{:S(2)}) collective-permute-start(bf16[2,8,128,128]{3,2,1,0:T(8,128)(2,1)} %collective-permute-done.1.far_a), channel_id=1, source_target_pairs={{0,2},{2,0},{4,6},{6,4},{8,10},{10,8},{12,14},{14,12},{16,18},{18,... | collective-permute-start | bytes 1572872 | tf_op jit(solution)/shard_map/ppermute | solution.py:276
  26.3 7.8 %collective-permute-start.6 = (bf16[8,16,128]{2,1,0:T(8,128)(2,1)S(1)}, bf16[8,16,128]{2,1,0:T(8,128)(2,1)S(1)}, u32[]{:S(2)}, u32[]{:S(2)}) collective-permute-start(bf16[8,16,128]{2,1,0:T(8,128)(2,1)S(1)} %get-tuple-element.38), channel_id=1, source_target_pairs={{0,32},{2,34},{4,36},{6,38},{8,40},{10,42},{12,44},{14,46},{16,48}... | collective-permute-start | bytes 98312 | tf_op jit(solution)/shard_map/ppermute | solution.py:276
  30.9 5.1 %collective-permute-start.7 = (bf16[8,16,128]{2,1,0:T(8,128)(2,1)S(1)}, bf16[8,16,128]{2,1,0:T(8,128)(2,1)S(1)}, u32[]{:S(2)}, u32[]{:S(2)}) collective-permute-start(bf16[8,16,128]{2,1,0:T(8,128)(2,1)S(1)} %get-tuple-element.38), channel_id=1, source_target_pairs={{0,48},{2,50},{4,52},{6,54},{8,56},{10,58},{12,60},{14,62},{16,32}... | collective-permute-start | bytes 98312 | tf_op jit(solution)/shard_map/ppermute | solution.py:276
  36.0 9.5 %collective-permute-start.10 = (bf16[4,8,16,128]{3,2,1,0:T(8,128)(2,1)S(1)}, bf16[4,8,16,128]{3,2,1,0:T(8,128)(2,1)S(1)}, u32[]{:S(2)}, u32[]{:S(2)}) collective-permute-start(bf16[4,8,16,128]{3,2,1,0:T(8,128)(2,1)S(1)} %pad_maximum_fusion.line), channel_id=1, source_target_pairs={{0,192},{2,194},{4,196},{6,198},{8,200},{10,202},{12,204},{14,206}... | collective-permute-start | bytes 393224 | tf_op jit(solution)/shard_map/ppermute | solution.py:276
  36.6 8.9 %collective-permute-start.9 = (bf16[4,8,16,128]{3,2,1,0:T(8,128)(2,1)S(1)}, bf16[4,8,16,128]{3,2,1,0:T(8,128)(2,1)S(1)}, u32[]{:S(2)}, u32[]{:S(2)}) collective-permute-start(bf16[4,8,16,128]{3,2,1,0:T(8,128)(2,1)S(1)} %pad_maximum_fusion.line), channel_id=1, source_target_pairs={{0,128},{2,130},{4,132},{6,134},{8,136},{10,138},{12,140},{14,142}... | collective-permute-start | bytes 393224 | tf_op jit(solution)/shard_map/ppermute | solution.py:276
  39.0 6.5 %collective-permute-start.8 = (bf16[4,8,16,128]{3,2,1,0:T(8,128)(2,1)S(1)}, bf16[4,8,16,128]{3,2,1,0:T(8,128)(2,1)S(1)}, u32[]{:S(2)}, u32[]{:S(2)}) collective-permute-start(bf16[4,8,16,128]{3,2,1,0:T(8,128)(2,1)S(1)} %pad_maximum_fusion.line), channel_id=1, source_target_pairs={{0,64},{2,66},{4,68},{6,70},{8,72},{10,74},{12,76},{14,78},{16,80}... | collective-permute-start | bytes 393224 | tf_op jit(solution)/shard_map/ppermute | solution.py:276
  40.2 29.4 %copy-start = (bf16[8,3,64,128]{3,2,1,0:T(8,128)(2,1)S(1)}, bf16[8,3,64,128]{3,2,1,0:T(8,128)(2,1)}, u32[]{:S(2)}) copy-start(bf16[8,3,64,128]{3,2,1,0:T(8,128)(2,1)} %get-tuple-element.22.ka) | copy-start | bytes 1179652
  47.0 22.6 %all-to-all-start.1 = ((bf16[16,16,256]{2,1,0:T(8,128)(2,1)}), bf16[16,16,256]{2,1,0:T(8,128)(2,1)S(1)}, u32[]{:S(2)}, u32[]{:S(2)}) async-start(bf16[16,16,256]{2,1,0:T(8,128)(2,1)} %shard_map.41), calls=%async_computation.1 | async-start | bytes 262144 | tf_op jit(solution)/shard_map/all_to_all | solution.py:272
  54.0 15.6 %collective-permute-start.4 = (bf16[528,128]{1,0:T(8,128)(2,1)S(1)}, bf16[528,128]{1,0:T(8,128)(2,1)S(1)}, u32[]{:S(2)}, u32[]{:S(2)}) collective-permute-start(bf16[528,128]{1,0:T(8,128)(2,1)S(1)} %get-tuple-element.35), channel_id=1, source_target_pairs={{0,1},{1,0},{2,3},{3,2},{4,5},{5,4},{6,7},{7,6},{8,9},{9,8},{10,11... | collective-permute-start | bytes 405512 | tf_op jit(solution)/shard_map/ppermute | solution.py:314

commit v5 on v4

--- a/solution.py
+++ b/solution.py
@@ -1,3 +1,4 @@
+import functools
 import math
 
 import jax
@@ -113,11 +114,12 @@
         copy.wait()
 
 
-def local_kernel(qkv, keep, send, part, mine, theirs, rest, outs, tops, dens, sems_out):
+def local_kernel(heads, qkv, *refs):
+    keep, send, part, mine, theirs, rest, outs, tops, dens, sems_out = refs[-10:]
     tp = lax.axis_index("tp")
     pending = []
     ok = iota((256, 256), 1) <= iota((256, 256), 0)
-    for h in range(8):
+    for h in heads:
         o_ref, m_ref, l_ref = outs.at[h % 4], tops.at[h % 4], dens.at[h % 4]
         for b in range(2):
             rows = slice(256 * b, 256 * b + 256)
@@ -250,7 +252,7 @@
             out[:, cols] = buf[...].astype(BF16)
 
 
-def call(kernel, ins, outs, scratch):
+def call(kernel, ins, outs, scratch, aliases={}):
     vm, hbm = pl.BlockSpec(memory_space=VMEM), pl.BlockSpec(memory_space=pltpu.HBM)
     spaces = {"V": VMEM, "H": pltpu.HBM}
     args = [pltpu.with_memory_space_constraint(a, spaces[m]) if m else a for a, m in ins]
@@ -260,7 +262,9 @@
         in_specs=[hbm if m == "H" else vm for _, m in ins],
         out_specs=[hbm if m == "H" else vm for _, m in outs],
         scratch_shapes=scratch,
-        compiler_params=pltpu.CompilerParams(vmem_limit_bytes=LIMIT),
+        compiler_params=pltpu.CompilerParams(
+            vmem_limit_bytes=LIMIT),
+        input_output_aliases=aliases,
     )(*args)
 
 
@@ -288,16 +292,22 @@
     far_a = lax.ppermute(kv1, "ctx", [(i, i + 2) for i in range(n) if i % 4 < 2])
     mate = flip(kv1, 1)
 
-    keep, send, part = call(
-        local_kernel, [(rows, "V")],
-        ((((8, 3, 64, HD), BF16), "H"), (((8, 3, 64, HD), BF16), "H"), (((8, 128, 256), F32), "H")),
-        [VMEM((8, 3, 64, HD), BF16), VMEM((8, 3, 64, HD), BF16), VMEM((8, 128, 256), F32)]
-        + [VMEM((4, 512, HD), F32)] * 3 + [dma((3, 8))])
+    def attend_local(heads, before=()):
+        return call(
+            functools.partial(local_kernel, heads), [(rows, "V")] + [(a, "H") for a in before],
+            ((((8, 3, 64, HD), BF16), "H"), (((8, 3, 64, HD), BF16), "H"),
+             (((8, 128, 256), F32), "H")),
+            [VMEM((8, 3, 64, HD), BF16), VMEM((8, 3, 64, HD), BF16), VMEM((8, 128, 256), F32)]
+            + [VMEM((4, 512, HD), F32)] * 3 + [dma((3, 8))],
+            {1: 0, 2: 1, 3: 2} if before else {})
+
+    keep, send, part = attend_local(range(6))
     swap = [(0, 1), (1, 0)]
     y2, part = barrier((y2, part))
     kv2 = y2[:, 32:112]
     kv3 = y2[:, 96:112]
     flips = [flip(kv2 if j == 1 else kv3, 8 * j) for j in (1, 2, 3)]
+    keep, send, part = attend_local(range(6, 8), (keep, send, part))
     got = lax.ppermute(send, "tp", swap)
 
     line = jnp.stack([kv3, flips[0][:, 64:80], flips[1], flips[2]])

time: 72.4 us -> 71.3 us (0.985)
  starting transfers between devices: 39.7 us -> 36.4 us
  waiting for transfers between devices: 13.4 us -> 14.5 us
  Pallas kernels: 18.1 us -> 19.1 us
    all_to_all x2, waiting for transfers between devices: 0.01 us -> 4.34 us  [exchange(): lax.all_to_all(value, axes, split_axis=0, concat_axis=0, tiled=True, axis...]
    ppermute x8, waiting for transfers between devices: 3.58 us -> 0.34 us  [flip(): return lax.ppermute(value, 'ctx', [(i, i ^ bits) for i in range(n)])]
    ppermute x8, starting transfers between devices: 12.5 us -> 10.2 us  [flip(): return lax.ppermute(value, 'ctx', [(i, i ^ bits) for i in range(n)])]
    all_to_all x2, starting transfers between devices: 11.5 us -> 9.32 us  [exchange(): lax.all_to_all(value, axes, split_axis=0, concat_axis=0, tiled=True, axis...]
    ppermute x1, starting transfers between devices: 5.15 us -> 6.41 us  [local(): got = lax.ppermute(send, 'tp', swap)]
    pallas_call x6 -> x7, Pallas kernels: 18.1 us -> 19.1 us  [call(): pl.pallas_call(kernel, out_shape=[spaces[m](*o) if m else jax.ShapeDtypeS...]
  transfers between devices with their start and end apart: 13 -> 13, of which waited for: 3 -> 3; matrix products, arithmetic and copies ran while one was open for 0% -> 0% of each run, Pallas kernels for 18% -> 20%
where the time goes in v5:
time: 71.3 us; the launch traced here: 70.1 us
  starting transfers between devices  36.4 us (51%)
  Pallas kernels  19.1 us (27%)
  waiting for transfers between devices  14.5 us (20%)
    pallas_call x7, Pallas kernels, call(): pl.pallas_call(kernel, out_shape=[spaces[m](*o) if m else jax.ShapeDtypeS...  19.1 us
    ppermute x8, starting transfers between devices, flip(): return lax.ppermute(value, 'ctx', [(i, i ^ bits) for i in range(n)])  10.2 us
    ppermute x1, waiting for transfers between devices, local(): got1 = lax.ppermute(send1, 'tp', swap)  9.76 us
    all_to_all x2, starting transfers between devices, exchange(): lax.all_to_all(value, axes, split_axis=0, concat_axis=0, tiled=True, axis...  9.32 us
    ppermute x1, starting transfers between devices, local(): got = lax.ppermute(send, 'tp', swap)  6.41 us
    ppermute x1, starting transfers between devices, local(): got1 = lax.ppermute(send1, 'tp', swap)  5.83 us
    ppermute x1, starting transfers between devices, local(): lax.ppermute(kv1, 'ctx', [(i, i + 2) for i in range(n) if i % 4 < 2])  4.63 us
    all_to_all x2, waiting for transfers between devices, exchange(): lax.all_to_all(value, axes, split_axis=0, concat_axis=0, tiled=True, axis...  4.34 us
  transfers between devices with their start and end apart: 13, of which 3 were waited for; matrix products, arithmetic and copies ran while one was open for 0% of the time, Pallas kernels for 20%

profile of v5, /device:TPU:6, one launch (start us, length us, event | category | flops | bytes accessed | tf_op | source)
XLA Modules:
  0.0 70.1 jit_solution(5917850782876385046)
XLA Ops:
  0.0 3.5 %shard_map.37 = (bf16[8,128,128]{2,1,0:T(8,128)(2,1)}, bf16[2,8,128,128]{3,2,1,0:T(8,128)(2,1)}, bf16[8,112,128]{2,1,0:T(8,128)(2,1)}, bf16[3,512,1024]{2,1,0:T(8,128)(2,1)S(1)}) custom-call(bf16[512,1024]{1,0:T(8,128)(2,1)} %q.1, bf16[512,1024]{1,0:T(8,128)(2,1)} %k.1, bf16[512,1024]{1,0:T(8,128)(2,1)} %v.1), custom_call_target="tpu_custom_call" | custom-call | tf_op jit(solution)/shard_map/pallas_call | solution.py:259
  3.5 4.6 %collective-permute-start.1 = (bf16[2,8,128,128]{3,2,1,0:T(8,128)(2,1)}, bf16[2,8,128,128]{3,2,1,0:T(8,128)(2,1)}, u32[]{:S(2)}, u32[]{:S(2)}) collective-permute-start(bf16[2,8,128,128]{3,2,1,0:T(8,128)(2,1)} %get-tuple-element.33.refs_1_), channel_id=1, source_target_pairs={{0,4},{2,6},{8,12},{10,14},{16,20},{18,22},{24,28},{26,30},{32,36}... | collective-permute-start | bytes 1572872 | tf_op jit(solution)/shard_map/ppermute | solution.py:292
  8.2 4.5 %all-to-all-start = ((bf16[8,112,128]{2,1,0:T(8,128)(2,1)}), bf16[8,112,128]{2,1,0:T(8,128)(2,1)S(1)}, u32[]{:S(2)}, u32[]{:S(2)}) async-start(bf16[8,112,128]{2,1,0:T(8,128)(2,1)} %get-tuple-element.27), calls=%async_computation | async-start | bytes 458752 | tf_op jit(solution)/shard_map/all_to_all | solution.py:276
  12.7 0.5 collective-permute-start
  13.2 4.9 %shard_map.38 = (bf16[8,3,64,128]{3,2,1,0:T(8,128)(2,1)}, bf16[8,3,64,128]{3,2,1,0:T(8,128)(2,1)}, f32[8,128,256]{2,1,0:T(8,128)}) custom-call(bf16[3,512,1024]{2,1,0:T(8,128)(2,1)S(1)} %get-tuple-element.24.qkv), custom_call_target="tpu_custom_call" | custom-call | tf_op jit(solution)/shard_map/pallas_call | solution.py:259
  18.1 4.3 %all-to-all-done.own = bf16[8,112,128]{2,1,0:T(8,128)(2,1)S(1)} async-done(((bf16[8,112,128]{2,1,0:T(8,128)(2,1)}), bf16[8,112,128]{2,1,0:T(8,128)(2,1)S(1)}, u32[]{:S(2)}, u32[]{:S(2)}) %all-to-all-start) | async-done | bytes 229408 | tf_op jit(solution)/shard_map/all_to_all | solution.py:276
  22.5 1.7 %collective-permute-start.5 = (bf16[8,80,128]{2,1,0:T(8,128)(2,1)S(1)}, bf16[8,80,128]{2,1,0:T(8,128)(2,1)S(1)}, u32[]{:S(2)}, u32[]{:S(2)}) collective-permute-start(bf16[8,80,128]{2,1,0:T(8,128)(2,1)S(1)} %slice.9), channel_id=1, source_target_pairs={{0,16},{2,18},{4,20},{6,22},{8,24},{10,26},{12,28},{14,30},{16,0},... | collective-permute-start | bytes 491528 | tf_op jit(solution)/shard_map/ppermute | solution.py:280
  24.1 0.0 collective-permute-done.1.far_a
  24.1 0.0 collective-permute-start.2
  24.1 3.0 %collective-permute-start.6 = (bf16[8,16,128]{2,1,0:T(8,128)(2,1)S(1)}, bf16[8,16,128]{2,1,0:T(8,128)(2,1)S(1)}, u32[]{:S(2)}, u32[]{:S(2)}) collective-permute-start(bf16[8,16,128]{2,1,0:T(8,128)(2,1)S(1)} %get-tuple-element.44), channel_id=1, source_target_pairs={{0,32},{2,34},{4,36},{6,38},{8,40},{10,42},{12,44},{14,46},{16,48}... | collective-permute-start | bytes 98312 | tf_op jit(solution)/shard_map/ppermute | solution.py:280
  27.1 0.2 collective-permute-start.7
  27.4 2.3 %shard_map.39 = (bf16[8,3,64,128]{3,2,1,0:T(8,128)(2,1)}, bf16[8,3,64,128]{3,2,1,0:T(8,128)(2,1)}, f32[8,128,256]{2,1,0:T(8,128)}) custom-call(bf16[3,512,1024]{2,1,0:T(8,128)(2,1)S(1)} %get-tuple-element.24.qkv, bf16[8,3,64,128]{3,2,1,0:T(8,128)(2,1)} %get-tuple-element.25.refs_0_, ...), custom_call_target="tpu_custom_call", output_to_operand_aliasing={{0}: (1, {}), {1}: (2, {}), {2}: (3, {})} | custom-call | tf_op jit(solution)/shard_map/pallas_call | solution.py:259
  29.7 0.0 collective-permute-done.5.mate
  29.7 6.4 %collective-permute-start.3 = (bf16[8,3,64,128]{3,2,1,0:T(8,128)(2,1)}, bf16[8,3,64,128]{3,2,1,0:T(8,128)(2,1)S(1)}, u32[]{:S(2)}, u32[]{:S(2)}) collective-permute-start(bf16[8,3,64,128]{3,2,1,0:T(8,128)(2,1)} %get-tuple-element.40), channel_id=1, source_target_pairs={{0,1},{1,0},{2,3},{3,2},{4,5},{5,4},{6,7},{7,6},{8,9},{9,8},{10,11... | collective-permute-start | bytes 1179656 | tf_op jit(solution)/shard_map/ppermute | solution.py:311
  36.1 0.0 collective-permute-done.6
  36.1 0.0 collective-permute-done.7
  36.2 0.6 collective-permute-start.10
  36.7 0.9 %collective-permute-start.8 = (bf16[4,8,16,128]{3,2,1,0:T(8,128)(2,1)S(1)}, bf16[4,8,16,128]{3,2,1,0:T(8,128)(2,1)S(1)}, u32[]{:S(2)}, u32[]{:S(2)}) collective-permute-start(bf16[4,8,16,128]{3,2,1,0:T(8,128)(2,1)S(1)} %pad_maximum_fusion.line), channel_id=1, source_target_pairs={{0,64},{2,66},{4,68},{6,70},{8,72},{10,74},{12,76},{14,78},{16,80}... | collective-permute-start | bytes 393224 | tf_op jit(solution)/shard_map/ppermute | solution.py:280
  37.6 0.0 collective-permute-done.mate
  37.6 3.3 %collective-permute-start.9 = (bf16[4,8,16,128]{3,2,1,0:T(8,128)(2,1)S(1)}, bf16[4,8,16,128]{3,2,1,0:T(8,128)(2,1)S(1)}, u32[]{:S(2)}, u32[]{:S(2)}) collective-permute-start(bf16[4,8,16,128]{3,2,1,0:T(8,128)(2,1)S(1)} %pad_maximum_fusion.line), channel_id=1, source_target_pairs={{0,128},{2,130},{4,132},{6,134},{8,136},{10,138},{12,140},{14,142}... | collective-permute-start | bytes 393224 | tf_op jit(solution)/shard_map/ppermute | solution.py:280
  41.0 0.0 copy-start
  41.0 1.6 %shard_map.40 = (bf16[8,128,128]{2,1,0:T(8,128)(2,1)S(1)}, bf16[2,8,128,128]{3,2,1,0:T(8,128)(2,1)S(1)}, f32[8,128,256]{2,1,0:T(8,128)S(1)}) custom-call(bf16[8,128,128]{2,1,0:T(8,128)(2,1)} %get-tuple-element.32.refs_0_, bf16[2,8,128,128]{3,2,1,0:T(8,128)(2,1)} %get-tuple-element.33.refs_1_, f32[8,128,256]{2,1,0:T(8,128)} %get-tuple-element.34.refs_2_), custom_call_target="tpu_custom_call" | custom-call | tf_op jit(solution)/shard_map/pallas_call | solution.py:259
  42.5 0.0 collective-permute-done.2.far_b
  42.6 3.7 %shard_map.41 = (bf16[528,128]{1,0:T(8,128)(2,1)S(1)}, bf16[528,128]{1,0:T(8,128)(2,1)S(1)}) custom-call(bf16[8,128,128]{2,1,0:T(8,128)(2,1)S(1)} %get-tuple-element.35.q1, bf16[2,8,128,128]{3,2,1,0:T(8,128)(2,1)S(1)} %get-tuple-element.36.own, f32[8,128,256]{2,1,0:T(8,128)S(1)} %get-tuple-element.37.part, ...), custom_call_target="tpu_custom_call" | custom-call | tf_op jit(solution)/shard_map/pallas_call | solution.py:259
  46.2 0.0 collective-permute-done.10.g3
  46.2 0.0 collective-permute-done.8.g1
  46.3 0.3 collective-permute-done.9.g2
  46.6 1.5 %shard_map.42 = bf16[16,16,256]{2,1,0:T(8,128)(2,1)} custom-call(bf16[8,112,128]{2,1,0:T(8,128)(2,1)S(1)} %all-to-all-done.own, bf16[8,80,128]{2,1,0:T(8,128)(2,1)S(1)} %collective-permute-done.5.mate, bf16[4,8,16,128]{3,2,1,0:T(8,128)(2,1)S(1)} %pad_maximum_fusion.line, bf16[4,8,16,128]{3,2,1,0:T(8,128)(2,1)S(1)} %collective-permute-done.8.g1, ...), custom_call_target="tpu_custom_call" | custom-call | tf_op jit(solution)/shard_map/pallas_call | solution.py:259
  48.1 4.8 %all-to-all-start.1 = ((bf16[16,16,256]{2,1,0:T(8,128)(2,1)}), bf16[16,16,256]{2,1,0:T(8,128)(2,1)S(1)}, u32[]{:S(2)}, u32[]{:S(2)}) async-start(bf16[16,16,256]{2,1,0:T(8,128)(2,1)} %shard_map.42), calls=%async_computation.1 | async-start | bytes 262144 | tf_op jit(solution)/shard_map/all_to_all | solution.py:276
  52.9 5.8 %collective-permute-start.4 = (bf16[528,128]{1,0:T(8,128)(2,1)S(1)}, bf16[528,128]{1,0:T(8,128)(2,1)S(1)}, u32[]{:S(2)}, u32[]{:S(2)}) collective-permute-start(bf16[528,128]{1,0:T(8,128)(2,1)S(1)} %get-tuple-element.41), channel_id=1, source_target_pairs={{0,1},{1,0},{2,3},{3,2},{4,5},{5,4},{6,7},{7,6},{8,9},{9,8},{10,11... | collective-permute-start | bytes 405512 | tf_op jit(solution)/shard_map/ppermute | solution.py:324
  58.7 0.0 collective-permute-done.3.ra
  58.7 9.8 %collective-permute-done.4.rb = bf16[528,128]{1,0:T(8,128)(2,1)S(1)} collective-permute-done((bf16[528,128]{1,0:T(8,128)(2,1)S(1)}, bf16[528,128]{1,0:T(8,128)(2,1)S(1)}, u32[]{:S(2)}, u32[]{:S(2)}) %collective-permute-start.4) | collective-permute-done | bytes 135200 | tf_op jit(solution)/shard_map/ppermute | solution.py:324
  68.5 0.0 all-to-all-done.1.back
  68.5 0.0 copy-done
  68.5 1.6 %shard_map.43 = bf16[256,2048]{1,0:T(8,128)(2,1)} custom-call(bf16[8,3,64,128]{3,2,1,0:T(8,128)(2,1)S(1)} %copy-done, bf16[528,128]{1,0:T(8,128)(2,1)S(1)} %get-tuple-element.39.kb, bf16[8,3,64,128]{3,2,1,0:T(8,128)(2,1)S(1)} %collective-permute-done.3.ra, bf16[528,128]{1,0:T(8,128)(2,1)S(1)} %collective-permute-done.4.rb, ...), custom_call_target="tpu_custom_call" | custom-call | tf_op jit(solution)/shard_map/pallas_call | solution.py:259
  (4 shorter events, 0.0 us)
Async XLA Ops:
  3.5 20.6 %collective-permute-start.1 = (bf16[2,8,128,128]{3,2,1,0:T(8,128)(2,1)}, bf16[2,8,128,128]{3,2,1,0:T(8,128)(2,1)}, u32[]{:S(2)}, u32[]{:S(2)}) collective-permute-start(bf16[2,8,128,128]{3,2,1,0:T(8,128)(2,1)} %get-tuple-element.33.refs_1_), channel_id=1, source_target_pairs={{0,4},{2,6},{8,12},{10,14},{16,20},{18,22},{24,28},{26,30},{32,36}... | collective-permute-start | bytes 1572872 | tf_op jit(solution)/shard_map/ppermute | solution.py:292
  8.2 14.3 %all-to-all-start = ((bf16[8,112,128]{2,1,0:T(8,128)(2,1)}), bf16[8,112,128]{2,1,0:T(8,128)(2,1)S(1)}, u32[]{:S(2)}, u32[]{:S(2)}) async-start(bf16[8,112,128]{2,1,0:T(8,128)(2,1)} %get-tuple-element.27), calls=%async_computation | async-start | bytes 458752 | tf_op jit(solution)/shard_map/all_to_all | solution.py:276
  12.7 24.9 %collective-permute-start = (bf16[2,8,128,128]{3,2,1,0:T(8,128)(2,1)}, bf16[2,8,128,128]{3,2,1,0:T(8,128)(2,1)}, u32[]{:S(2)}, u32[]{:S(2)}) collective-permute-start(bf16[2,8,128,128]{3,2,1,0:T(8,128)(2,1)} %get-tuple-element.33.refs_1_), channel_id=1, source_target_pairs={{0,2},{2,0},{4,6},{6,4},{8,10},{10,8},{12,14},{14,12},{16,18},{18,... | collective-permute-start | bytes 1572872 | tf_op jit(solution)/shard_map/ppermute | solution.py:280
  22.5 7.2 %collective-permute-start.5 = (bf16[8,80,128]{2,1,0:T(8,128)(2,1)S(1)}, bf16[8,80,128]{2,1,0:T(8,128)(2,1)S(1)}, u32[]{:S(2)}, u32[]{:S(2)}) collective-permute-start(bf16[8,80,128]{2,1,0:T(8,128)(2,1)S(1)} %slice.9), channel_id=1, source_target_pairs={{0,16},{2,18},{4,20},{6,22},{8,24},{10,26},{12,28},{14,30},{16,0},... | collective-permute-start | bytes 491528 | tf_op jit(solution)/shard_map/ppermute | solution.py:280
  24.1 18.4 %collective-permute-start.2 = (bf16[2,8,128,128]{3,2,1,0:T(8,128)(2,1)}, bf16[2,8,128,128]{3,2,1,0:T(8,128)(2,1)S(1)}, u32[]{:S(2)}, u32[]{:S(2)}) collective-permute-start(bf16[2,8,128,128]{3,2,1,0:T(8,128)(2,1)} %collective-permute-done.1.far_a), channel_id=1, source_target_pairs={{0,2},{2,0},{4,6},{6,4},{8,10},{10,8},{12,14},{14,12},{16,18},{18,... | collective-permute-start | bytes 1572872 | tf_op jit(solution)/shard_map/ppermute | solution.py:280
  24.1 12.0 %collective-permute-start.6 = (bf16[8,16,128]{2,1,0:T(8,128)(2,1)S(1)}, bf16[8,16,128]{2,1,0:T(8,128)(2,1)S(1)}, u32[]{:S(2)}, u32[]{:S(2)}) collective-permute-start(bf16[8,16,128]{2,1,0:T(8,128)(2,1)S(1)} %get-tuple-element.44), channel_id=1, source_target_pairs={{0,32},{2,34},{4,36},{6,38},{8,40},{10,42},{12,44},{14,46},{16,48}... | collective-permute-start | bytes 98312 | tf_op jit(solution)/shard_map/ppermute | solution.py:280
  27.1 9.0 %collective-permute-start.7 = (bf16[8,16,128]{2,1,0:T(8,128)(2,1)S(1)}, bf16[8,16,128]{2,1,0:T(8,128)(2,1)S(1)}, u32[]{:S(2)}, u32[]{:S(2)}) collective-permute-start(bf16[8,16,128]{2,1,0:T(8,128)(2,1)S(1)} %get-tuple-element.44), channel_id=1, source_target_pairs={{0,48},{2,50},{4,52},{6,54},{8,56},{10,58},{12,60},{14,62},{16,32}... | collective-permute-start | bytes 98312 | tf_op jit(solution)/shard_map/ppermute | solution.py:280
  29.7 29.0 %collective-permute-start.3 = (bf16[8,3,64,128]{3,2,1,0:T(8,128)(2,1)}, bf16[8,3,64,128]{3,2,1,0:T(8,128)(2,1)S(1)}, u32[]{:S(2)}, u32[]{:S(2)}) collective-permute-start(bf16[8,3,64,128]{3,2,1,0:T(8,128)(2,1)} %get-tuple-element.40), channel_id=1, source_target_pairs={{0,1},{1,0},{2,3},{3,2},{4,5},{5,4},{6,7},{7,6},{8,9},{9,8},{10,11... | collective-permute-start | bytes 1179656 | tf_op jit(solution)/shard_map/ppermute | solution.py:311
  36.2 10.1 %collective-permute-start.10 = (bf16[4,8,16,128]{3,2,1,0:T(8,128)(2,1)S(1)}, bf16[4,8,16,128]{3,2,1,0:T(8,128)(2,1)S(1)}, u32[]{:S(2)}, u32[]{:S(2)}) collective-permute-start(bf16[4,8,16,128]{3,2,1,0:T(8,128)(2,1)S(1)} %pad_maximum_fusion.line), channel_id=1, source_target_pairs={{0,192},{2,194},{4,196},{6,198},{8,200},{10,202},{12,204},{14,206}... | collective-permute-start | bytes 393224 | tf_op jit(solution)/shard_map/ppermute | solution.py:280
  36.7 9.5 %collective-permute-start.8 = (bf16[4,8,16,128]{3,2,1,0:T(8,128)(2,1)S(1)}, bf16[4,8,16,128]{3,2,1,0:T(8,128)(2,1)S(1)}, u32[]{:S(2)}, u32[]{:S(2)}) collective-permute-start(bf16[4,8,16,128]{3,2,1,0:T(8,128)(2,1)S(1)} %pad_maximum_fusion.line), channel_id=1, source_target_pairs={{0,64},{2,66},{4,68},{6,70},{8,72},{10,74},{12,76},{14,78},{16,80}... | collective-permute-start | bytes 393224 | tf_op jit(solution)/shard_map/ppermute | solution.py:280
  37.6 9.0 %collective-permute-start.9 = (bf16[4,8,16,128]{3,2,1,0:T(8,128)(2,1)S(1)}, bf16[4,8,16,128]{3,2,1,0:T(8,128)(2,1)S(1)}, u32[]{:S(2)}, u32[]{:S(2)}) collective-permute-start(bf16[4,8,16,128]{3,2,1,0:T(8,128)(2,1)S(1)} %pad_maximum_fusion.line), channel_id=1, source_target_pairs={{0,128},{2,130},{4,132},{6,134},{8,136},{10,138},{12,140},{14,142}... | collective-permute-start | bytes 393224 | tf_op jit(solution)/shard_map/ppermute | solution.py:280
  41.0 27.5 %copy-start = (bf16[8,3,64,128]{3,2,1,0:T(8,128)(2,1)S(1)}, bf16[8,3,64,128]{3,2,1,0:T(8,128)(2,1)}, u32[]{:S(2)}) copy-start(bf16[8,3,64,128]{3,2,1,0:T(8,128)(2,1)} %get-tuple-element.30.ka) | copy-start | bytes 1179652
  48.1 20.4 %all-to-all-start.1 = ((bf16[16,16,256]{2,1,0:T(8,128)(2,1)}), bf16[16,16,256]{2,1,0:T(8,128)(2,1)S(1)}, u32[]{:S(2)}, u32[]{:S(2)}) async-start(bf16[16,16,256]{2,1,0:T(8,128)(2,1)} %shard_map.42), calls=%async_computation.1 | async-start | bytes 262144 | tf_op jit(solution)/shard_map/all_to_all | solution.py:276
  52.9 15.6 %collective-permute-start.4 = (bf16[528,128]{1,0:T(8,128)(2,1)S(1)}, bf16[528,128]{1,0:T(8,128)(2,1)S(1)}, u32[]{:S(2)}, u32[]{:S(2)}) collective-permute-start(bf16[528,128]{1,0:T(8,128)(2,1)S(1)} %get-tuple-element.41), channel_id=1, source_target_pairs={{0,1},{1,0},{2,3},{3,2},{4,5},{5,4},{6,7},{7,6},{8,9},{9,8},{10,11... | collective-permute-start | bytes 405512 | tf_op jit(solution)/shard_map/ppermute | solution.py:324
